TPU v7x, 32 devices: a whole 2x2x4 slice. The times are simulated.
32 devices in a mesh: dp: 8 (over z, y), fsdp: 4 (over x, core).
Axes of the slice: x: 2, y: 2, z: 4, core: 2. Of those that a mesh axis runs over, the one named last changes fastest.
Arguments:
- tokens: bfloat16 [64, 1024, 768], P(('dp', 'fsdp')), may hold values from -6 to 6
- lengths: int32 [64], replicated, may hold values from 128 to 1024, as said below
- deal_order: int32 [64], replicated, may hold values from 0 to 63, as said below
- qkv_weight: bfloat16 [768, 2304], P(('dp', 'fsdp')), may hold values from -0.21875 to 0.21875
- query_bias: bfloat16 [768], P(('dp', 'fsdp')), may hold values from -3 to 3
- value_bias: bfloat16 [768], P(('dp', 'fsdp')), may hold values from -3 to 3
- out_weight: bfloat16 [768, 768], P(('dp', 'fsdp')), may hold values from -0.875 to 0.875
- out_bias: bfloat16 [768], P(('dp', 'fsdp')), may hold values from -3 to 3
- attn_gain: bfloat16 [768], P(('dp', 'fsdp')), may hold values from 0.5 to 1.5
- attn_shift: bfloat16 [768], P(('dp', 'fsdp')), may hold values from -2 to 2
- up_weight: bfloat16 [768, 3072], P(('dp', 'fsdp')), may hold values from -0.21875 to 0.21875
- up_bias: bfloat16 [3072], P(('dp', 'fsdp')), may hold values from -3 to 3
- down_weight: bfloat16 [3072, 768], P(('dp', 'fsdp')), may hold values from -0.109375 to 0.109375
- down_bias: bfloat16 [768], P(('dp', 'fsdp')), may hold values from -3 to 3
- ffn_gain: bfloat16 [768], P(('dp', 'fsdp')), may hold values from 0.5 to 1.5
- ffn_shift: bfloat16 [768], P(('dp', 'fsdp')), may hold values from -2 to 2
- cotangent: bfloat16 [64, 1024, 768], P(('dp', 'fsdp')), may hold values from -6 to 6
Outputs:
- layer_out: bfloat16 [64, 1024, 768], P(('dp', 'fsdp'))
- input_grad: bfloat16 [64, 1024, 768], P(('dp', 'fsdp'))
- qkvw_grad: float32 [768, 2304], P(('dp', 'fsdp'))
- qbias_grad: float32 [768], P(('dp', 'fsdp'))
- vbias_grad: float32 [768], P(('dp', 'fsdp'))
- outw_grad: float32 [768, 768], P(('dp', 'fsdp'))
- outb_grad: float32 [768], P(('dp', 'fsdp'))
- gaina_grad: float32 [768], P(('dp', 'fsdp'))
- shifta_grad: float32 [768], P(('dp', 'fsdp'))
- upw_grad: float32 [768, 3072], P(('dp', 'fsdp'))
- upb_grad: float32 [3072], P(('dp', 'fsdp'))
- downw_grad: float32 [3072, 768], P(('dp', 'fsdp'))
- downb_grad: float32 [768], P(('dp', 'fsdp'))
- gainf_grad: float32 [768], P(('dp', 'fsdp'))
- shiftf_grad: float32 [768], P(('dp', 'fsdp'))
- branch_rms: float32 [64, 3], P(('dp', 'fsdp'))
Inputs may be any that keep to these rules, and one draw needn't show every extreme that they name: `lengths`: some sequence has exactly 1024 valid tokens and some exactly 128. `deal_order`: A permutation of the sequences that maps each aligned block of 8 sequences onto itself; the 2 sequences of an aligned block of 2 go to 2 different aligned blocks of 2.
All inputs are finite; a program needn't handle non-finite values.
Results may differ from a plain program's by a relative error of at most 0.014.
The roundings to bfloat16 on the way count: a program that leaves them out, or rounds other values in their place, can miss the bound.
Values may be sent and summed in bfloat16 or wider, within the bound.
A program may use at most 448 MiB of HBM per device.

v0:
```python
import math

import jax
import jax.numpy as jnp
from jax import lax
from jax.sharding import PartitionSpec as P

HEADS = 12
HEAD_DIM = 64
LEN = 1024
BLOCK = 512


norm_eps = 1e-05
masked_fill = -1e30


def layer_norm(values, norm_gain, norm_shift):
    center = values - jnp.mean(values, axis=-1, keepdims=True)
    spread = jnp.mean(center * center, axis=-1, keepdims=True)
    return center * lax.rsqrt(spread + norm_eps) * norm_gain + norm_shift


def exact_gelu(values):
    return jax.nn.gelu(values, approximate=False)


def lower_dot(left, right):
    return jnp.dot(left, right, preferred_element_type=jnp.float32)


def rows_dot(left, right):
    return lax.dot_general(
        left, right, (((0,), (0,)), ((), ())), preferred_element_type=jnp.float32
    )


def back_dot(left, right):
    return lax.dot_general(
        left, right, (((1,), (1,)), ((), ())), preferred_element_type=jnp.float32
    )


def score_block(queries, key_heads, length):
    places = jnp.arange(key_heads.shape[0])
    scores = jnp.einsum("qhd,khd->hqk", queries, key_heads, preferred_element_type=jnp.float32) * (
        1.0 / math.sqrt(HEAD_DIM)
    )
    return jnp.where((places < length)[None, None, :], scores, masked_fill)


def forward_block(queries, key_heads, value_heads, length):
    scores = score_block(queries, key_heads, length)
    row_max = jnp.max(scores, axis=-1, keepdims=True)
    exp_scores = jnp.exp(scores - row_max)
    row_total = jnp.sum(exp_scores, axis=-1, keepdims=True)
    weights_low = (exp_scores / row_total).astype(jnp.bfloat16)
    context = jnp.einsum(
        "hqk,khd->qhd", weights_low, value_heads, preferred_element_type=jnp.float32
    )
    return (context, (row_max + jnp.log(row_total))[:, :, 0])


def backward_block(queries, key_heads, value_heads, grad_rows, logsum, length):
    scores = score_block(queries, key_heads, length)
    weights = jnp.exp(scores - logsum[:, :, None])
    grad_weights = jnp.einsum(
        "qhd,khd->hqk", grad_rows, value_heads, preferred_element_type=jnp.float32
    )
    grad_scores = (
        weights * (grad_weights - jnp.sum(weights * grad_weights, axis=-1, keepdims=True))
    ).astype(jnp.bfloat16)
    factor = 1.0 / math.sqrt(HEAD_DIM)
    grad_query = (
        jnp.einsum("hqk,khd->qhd", grad_scores, key_heads, preferred_element_type=jnp.float32)
        * factor
    )
    grad_key = (
        jnp.einsum("hqk,qhd->khd", grad_scores, queries, preferred_element_type=jnp.float32)
        * factor
    )
    grad_value = jnp.einsum(
        "hqk,qhd->khd", weights.astype(jnp.bfloat16), grad_rows, preferred_element_type=jnp.float32
    )
    return (grad_query, grad_key, grad_value)


def attention_forward(query_rows, key_rows, value_rows, length):
    heads_query = query_rows.reshape(LEN, HEADS, HEAD_DIM)
    key_heads = key_rows.reshape(LEN, HEADS, HEAD_DIM)
    value_heads = value_rows.reshape(LEN, HEADS, HEAD_DIM)
    contexts = []
    logsums = []
    for block_index in range(LEN // BLOCK):
        queries = heads_query[block_index * BLOCK : (block_index + 1) * BLOCK]
        context, logsum = forward_block(queries, key_heads, value_heads, length)
        contexts.append(context)
        logsums.append(logsum)
    return (jnp.concatenate(contexts, axis=0).reshape(LEN, HEADS * HEAD_DIM), logsums)


def attention_backward(query_rows, key_rows, value_rows, grad_context, logsums, length):
    heads_query = query_rows.reshape(LEN, HEADS, HEAD_DIM)
    key_heads = key_rows.reshape(LEN, HEADS, HEAD_DIM)
    value_heads = value_rows.reshape(LEN, HEADS, HEAD_DIM)
    heads_grad = grad_context.reshape(LEN, HEADS, HEAD_DIM)
    grad_queries = []
    grad_keys = jnp.zeros((LEN, HEADS, HEAD_DIM), jnp.float32)
    grad_values = jnp.zeros((LEN, HEADS, HEAD_DIM), jnp.float32)
    for block_index in range(LEN // BLOCK):
        queries = heads_query[block_index * BLOCK : (block_index + 1) * BLOCK]
        grad_rows = heads_grad[block_index * BLOCK : (block_index + 1) * BLOCK]
        grad_query, grad_key, grad_value = backward_block(
            queries, key_heads, value_heads, grad_rows, logsums[block_index], length
        )
        grad_queries.append(grad_query)
        grad_keys = grad_keys + grad_key
        grad_values = grad_values + grad_value
    model_width = HEADS * HEAD_DIM
    return (
        jnp.concatenate(grad_queries, axis=0).reshape(LEN, model_width),
        grad_keys.reshape(LEN, model_width),
        grad_values.reshape(LEN, model_width),
    )


def forward_pass(inputs_row, length, params):
    (
        w_qkv,
        bias_query,
        bias_value,
        w_out,
        bias_out,
        gain_attn,
        shift_attn,
        w_up,
        bias_up,
        w_down,
        bias_down,
        gain_ffn,
        shift_ffn,
    ) = params
    model_width = inputs_row.shape[1]
    usable = (jnp.arange(LEN) < length).astype(jnp.float32)[:, None]
    inputs_wide = inputs_row.astype(jnp.float32)
    projected = lower_dot(inputs_row, w_qkv)
    query_rows = (projected[:, :model_width] + bias_query.astype(jnp.float32)).astype(jnp.bfloat16)
    key_rows = projected[:, model_width : 2 * model_width].astype(jnp.bfloat16)
    value_rows = (projected[:, 2 * model_width :] + bias_value.astype(jnp.float32)).astype(
        jnp.bfloat16
    )
    context, logsums = attention_forward(query_rows, key_rows, value_rows, length)
    context_low = context.astype(jnp.bfloat16)
    branch_attn = lower_dot(context_low, w_out) + bias_out.astype(jnp.float32)
    hidden, attn_norm_back = jax.vjp(
        layer_norm,
        inputs_wide + branch_attn,
        gain_attn.astype(jnp.float32),
        shift_attn.astype(jnp.float32),
    )
    hidden_low = hidden.astype(jnp.bfloat16)
    gate_in = lower_dot(hidden_low, w_up) + bias_up.astype(jnp.float32)
    activated, gelu_back = jax.vjp(exact_gelu, gate_in)
    active_low = activated.astype(jnp.bfloat16)
    branch_ffn = lower_dot(active_low, w_down) + bias_down.astype(jnp.float32)
    result, ffn_norm_back = jax.vjp(
        layer_norm, hidden + branch_ffn, gain_ffn.astype(jnp.float32), shift_ffn.astype(jnp.float32)
    )
    result = (result * usable).astype(jnp.bfloat16)
    valid_count = jnp.sum(usable) * model_width
    summary = jnp.stack(
        [
            jnp.sqrt(jnp.sum(usable * inputs_wide * inputs_wide) / valid_count),
            jnp.sqrt(jnp.sum(usable * branch_attn * branch_attn) / valid_count),
            jnp.sqrt(jnp.sum(usable * branch_ffn * branch_ffn) / valid_count),
        ]
    )
    kept_state = (
        inputs_row,
        query_rows,
        key_rows,
        value_rows,
        context_low,
        logsums,
        hidden_low,
        active_low,
        attn_norm_back,
        gelu_back,
        ffn_norm_back,
        usable,
    )
    return (result, summary, kept_state)


def backward_pass(kept_state, cot_row, length, params):
    (
        inputs_row,
        query_rows,
        key_rows,
        value_rows,
        context_low,
        logsums,
        hidden_low,
        active_low,
        attn_norm_back,
        gelu_back,
        ffn_norm_back,
        usable,
    ) = kept_state
    w_qkv = params[0]
    w_out = params[3]
    w_up = params[7]
    w_down = params[9]
    model_width = inputs_row.shape[1]
    grad_sum_two, grad_gain_ffn, grad_shift_ffn = ffn_norm_back(
        cot_row.astype(jnp.float32) * usable
    )
    grad_ffn = grad_sum_two.astype(jnp.bfloat16)
    grad_w_down = rows_dot(active_low, grad_ffn)
    grad_bias_down = jnp.sum(grad_ffn.astype(jnp.float32), axis=0)
    (grad_gate,) = gelu_back(back_dot(grad_ffn, w_down))
    grad_gate_low = grad_gate.astype(jnp.bfloat16)
    grad_w_up = rows_dot(hidden_low, grad_gate_low)
    grad_bias_up = jnp.sum(grad_gate_low.astype(jnp.float32), axis=0)
    grad_hidden = grad_sum_two + back_dot(grad_gate_low, w_up)
    grad_sum_one, grad_gain_attn, grad_shift_attn = attn_norm_back(grad_hidden)
    grad_attn = grad_sum_one.astype(jnp.bfloat16)
    grad_w_out = rows_dot(context_low, grad_attn)
    grad_bias_out = jnp.sum(grad_attn.astype(jnp.float32), axis=0)
    grad_context = back_dot(grad_attn, w_out).astype(jnp.bfloat16)
    grad_query, grad_key, grad_value = attention_backward(
        query_rows, key_rows, value_rows, grad_context, logsums, length
    )
    grad_mixed = jnp.concatenate([grad_query, grad_key, grad_value], axis=1).astype(jnp.bfloat16)
    grad_w_qkv = rows_dot(inputs_row, grad_mixed)
    grad_bias_query = jnp.sum(grad_mixed[:, :model_width].astype(jnp.float32), axis=0)
    grad_bias_value = jnp.sum(grad_mixed[:, 2 * model_width :].astype(jnp.float32), axis=0)
    grad_input = (grad_sum_one + back_dot(grad_mixed, w_qkv)).astype(jnp.bfloat16)
    grads = (
        grad_w_qkv,
        grad_bias_query,
        grad_bias_value,
        grad_w_out,
        grad_bias_out,
        grad_gain_attn,
        grad_shift_attn,
        grad_w_up,
        grad_bias_up,
        grad_w_down,
        grad_bias_down,
        grad_gain_ffn,
        grad_shift_ffn,
    )
    return (grad_input, grads)


def fetch_forward(
    qkv_weight,
    query_bias,
    value_bias,
    out_weight,
    out_bias,
    attn_gain,
    attn_shift,
    up_weight,
    up_bias,
    down_weight,
    down_bias,
    ffn_gain,
    ffn_shift,
):
    return (
        lax.all_gather(qkv_weight, ("dp", "fsdp"), axis=0, tiled=True),
        lax.all_gather(query_bias, ("dp", "fsdp"), axis=0, tiled=True),
        lax.all_gather(value_bias, ("dp", "fsdp"), axis=0, tiled=True),
        lax.all_gather(out_weight, ("dp", "fsdp"), axis=0, tiled=True),
        lax.all_gather(out_bias, ("dp", "fsdp"), axis=0, tiled=True),
        lax.all_gather(attn_gain, ("dp", "fsdp"), axis=0, tiled=True),
        lax.all_gather(attn_shift, ("dp", "fsdp"), axis=0, tiled=True),
        lax.all_gather(up_weight, ("dp", "fsdp"), axis=0, tiled=True),
        lax.all_gather(up_bias, ("dp", "fsdp"), axis=0, tiled=True),
        lax.all_gather(down_weight, ("dp", "fsdp"), axis=0, tiled=True),
        lax.all_gather(down_bias, ("dp", "fsdp"), axis=0, tiled=True),
        lax.all_gather(ffn_gain, ("dp", "fsdp"), axis=0, tiled=True),
        lax.all_gather(ffn_shift, ("dp", "fsdp"), axis=0, tiled=True),
    )


def fetch_backward(
    qkv_weight,
    query_bias,
    value_bias,
    out_weight,
    out_bias,
    attn_gain,
    attn_shift,
    up_weight,
    up_bias,
    down_weight,
    down_bias,
    ffn_gain,
    ffn_shift,
):
    return (
        lax.all_gather(qkv_weight, ("dp", "fsdp"), axis=0, tiled=True),
        lax.all_gather(query_bias, ("dp", "fsdp"), axis=0, tiled=True),
        lax.all_gather(value_bias, ("dp", "fsdp"), axis=0, tiled=True),
        lax.all_gather(out_weight, ("dp", "fsdp"), axis=0, tiled=True),
        lax.all_gather(out_bias, ("dp", "fsdp"), axis=0, tiled=True),
        lax.all_gather(attn_gain, ("dp", "fsdp"), axis=0, tiled=True),
        lax.all_gather(attn_shift, ("dp", "fsdp"), axis=0, tiled=True),
        lax.all_gather(up_weight, ("dp", "fsdp"), axis=0, tiled=True),
        lax.all_gather(up_bias, ("dp", "fsdp"), axis=0, tiled=True),
        lax.all_gather(down_weight, ("dp", "fsdp"), axis=0, tiled=True),
        lax.all_gather(down_bias, ("dp", "fsdp"), axis=0, tiled=True),
        lax.all_gather(ffn_gain, ("dp", "fsdp"), axis=0, tiled=True),
        lax.all_gather(ffn_shift, ("dp", "fsdp"), axis=0, tiled=True),
    )


def body(
    tokens,
    lengths,
    deal_order,
    qkv_weight,
    query_bias,
    value_bias,
    out_weight,
    out_bias,
    attn_gain,
    attn_shift,
    up_weight,
    up_bias,
    down_weight,
    down_bias,
    ffn_gain,
    ffn_shift,
    cotangent,
):
    shards = lax.axis_size("fsdp")
    per_device = tokens.shape[0]
    column = shards * per_device
    group_base = lax.axis_index("dp") * column
    member = lax.axis_index("fsdp")
    group_order = lax.dynamic_slice_in_dim(deal_order, group_base, column) - group_base
    group_lengths = lax.dynamic_slice_in_dim(lengths, group_base, column)
    column_index = jnp.arange(column, dtype=jnp.int32)
    peer_index = jnp.arange(shards, dtype=jnp.int32)
    own_target = (
        lax.dynamic_slice_in_dim(group_order, member * per_device, per_device) // per_device
    )
    dealt_here = member * per_device + jnp.arange(per_device, dtype=jnp.int32)
    matches = group_order[None, :] == dealt_here[:, None]
    source = jnp.sum(jnp.where(matches, column_index[None, :], 0), axis=1)
    seq_lengths = jnp.sum(jnp.where(matches, group_lengths[None, :], 0), axis=1)
    to_peer = (own_target[None, :] == peer_index[:, None]).astype(jnp.bfloat16)
    from_peer = ((source // per_device)[:, None] == peer_index[None, :]).astype(jnp.bfloat16)
    outgoing = jnp.einsum(
        "gk,kld->gld", to_peer, tokens, preferred_element_type=jnp.float32
    ).astype(jnp.bfloat16)
    arrived = lax.all_to_all(outgoing, "fsdp", split_axis=0, concat_axis=0, tiled=True)
    inputs = jnp.einsum(
        "tg,gld->tld", from_peer, arrived, preferred_element_type=jnp.float32
    ).astype(jnp.bfloat16)
    model_width = tokens.shape[2]
    hidden_width = up_weight.shape[1]
    totals = (
        jnp.zeros((model_width, 3 * model_width), jnp.float32),
        jnp.zeros((model_width,), jnp.float32),
        jnp.zeros((model_width,), jnp.float32),
        jnp.zeros((model_width, model_width), jnp.float32),
        jnp.zeros((model_width,), jnp.float32),
        jnp.zeros((model_width,), jnp.float32),
        jnp.zeros((model_width,), jnp.float32),
        jnp.zeros((model_width, hidden_width), jnp.float32),
        jnp.zeros((hidden_width,), jnp.float32),
        jnp.zeros((hidden_width, model_width), jnp.float32),
        jnp.zeros((model_width,), jnp.float32),
        jnp.zeros((model_width,), jnp.float32),
        jnp.zeros((model_width,), jnp.float32),
    )
    results = []
    summaries = []
    grad_inputs = []
    for micro_index in range(per_device):
        forward_params = fetch_forward(
            qkv_weight,
            query_bias,
            value_bias,
            out_weight,
            out_bias,
            attn_gain,
            attn_shift,
            up_weight,
            up_bias,
            down_weight,
            down_bias,
            ffn_gain,
            ffn_shift,
        )
        result, summary, kept_state = forward_pass(
            inputs[micro_index], seq_lengths[micro_index], forward_params
        )
        backward_params = fetch_backward(
            qkv_weight,
            query_bias,
            value_bias,
            out_weight,
            out_bias,
            attn_gain,
            attn_shift,
            up_weight,
            up_bias,
            down_weight,
            down_bias,
            ffn_gain,
            ffn_shift,
        )
        grad_input, grads = backward_pass(
            kept_state, cotangent[micro_index], seq_lengths[micro_index], backward_params
        )
        totals = tuple((earlier + latest for earlier, latest in zip(totals, grads)))
        results.append(result)
        summaries.append(summary)
        grad_inputs.append(grad_input)
    layer_out = jnp.stack(results)
    branch_rms = jnp.stack(summaries)
    dealt_grads = jnp.stack(grad_inputs)
    returning = jnp.einsum(
        "tg,tld->gld", from_peer, dealt_grads, preferred_element_type=jnp.float32
    ).astype(jnp.bfloat16)
    came_back = lax.all_to_all(returning, "fsdp", split_axis=0, concat_axis=0, tiled=True)
    input_grad = jnp.einsum(
        "gk,gld->kld", to_peer, came_back, preferred_element_type=jnp.float32
    ).astype(jnp.bfloat16)
    (
        total_qkvw,
        total_qbias,
        total_vbias,
        total_outw,
        total_outb,
        total_gaina,
        total_shifta,
        total_upw,
        total_upb,
        total_downw,
        total_downb,
        total_gainf,
        total_shiftf,
    ) = totals
    summed = (
        lax.psum_scatter(total_qkvw, ("dp", "fsdp"), scatter_dimension=0, tiled=True),
        lax.psum_scatter(total_qbias, ("dp", "fsdp"), scatter_dimension=0, tiled=True),
        lax.psum_scatter(total_vbias, ("dp", "fsdp"), scatter_dimension=0, tiled=True),
        lax.psum_scatter(total_outw, ("dp", "fsdp"), scatter_dimension=0, tiled=True),
        lax.psum_scatter(total_outb, ("dp", "fsdp"), scatter_dimension=0, tiled=True),
        lax.psum_scatter(total_gaina, ("dp", "fsdp"), scatter_dimension=0, tiled=True),
        lax.psum_scatter(total_shifta, ("dp", "fsdp"), scatter_dimension=0, tiled=True),
        lax.psum_scatter(total_upw, ("dp", "fsdp"), scatter_dimension=0, tiled=True),
        lax.psum_scatter(total_upb, ("dp", "fsdp"), scatter_dimension=0, tiled=True),
        lax.psum_scatter(total_downw, ("dp", "fsdp"), scatter_dimension=0, tiled=True),
        lax.psum_scatter(total_downb, ("dp", "fsdp"), scatter_dimension=0, tiled=True),
        lax.psum_scatter(total_gainf, ("dp", "fsdp"), scatter_dimension=0, tiled=True),
        lax.psum_scatter(total_shiftf, ("dp", "fsdp"), scatter_dimension=0, tiled=True),
    )
    (
        qkvw_grad,
        qbias_grad,
        vbias_grad,
        outw_grad,
        outb_grad,
        gaina_grad,
        shifta_grad,
        upw_grad,
        upb_grad,
        downw_grad,
        downb_grad,
        gainf_grad,
        shiftf_grad,
    ) = summed
    return (
        layer_out,
        input_grad,
        qkvw_grad,
        qbias_grad,
        vbias_grad,
        outw_grad,
        outb_grad,
        gaina_grad,
        shifta_grad,
        upw_grad,
        upb_grad,
        downw_grad,
        downb_grad,
        gainf_grad,
        shiftf_grad,
        branch_rms,
    )


def solution(mesh):
    in_specs = (
        P(("dp", "fsdp"), None, None),
        P(),
        P(),
        P(("dp", "fsdp"), None),
        P(("dp", "fsdp")),
        P(("dp", "fsdp")),
        P(("dp", "fsdp"), None),
        P(("dp", "fsdp")),
        P(("dp", "fsdp")),
        P(("dp", "fsdp")),
        P(("dp", "fsdp"), None),
        P(("dp", "fsdp")),
        P(("dp", "fsdp"), None),
        P(("dp", "fsdp")),
        P(("dp", "fsdp")),
        P(("dp", "fsdp")),
        P(("dp", "fsdp"), None, None),
    )
    out_specs = (
        P(("dp", "fsdp"), None, None),
        P(("dp", "fsdp"), None, None),
        P(("dp", "fsdp"), None),
        P(("dp", "fsdp")),
        P(("dp", "fsdp")),
        P(("dp", "fsdp"), None),
        P(("dp", "fsdp")),
        P(("dp", "fsdp")),
        P(("dp", "fsdp")),
        P(("dp", "fsdp"), None),
        P(("dp", "fsdp")),
        P(("dp", "fsdp"), None),
        P(("dp", "fsdp")),
        P(("dp", "fsdp")),
        P(("dp", "fsdp")),
        P(("dp", "fsdp"), None),
    )
    return jax.shard_map(body, mesh=mesh, in_specs=in_specs, out_specs=out_specs, check_vma=False)
```

profile of v0, /device:TPU:0, one launch (start us, length us, event | category | flops | bytes accessed | tf_op | source)
XLA Modules:
  0.0 1318.2 jit_solution(4339282446462313465)
XLA Ops:
  10.2 14.3 %convolution_convert_fusion.1 = bf16[4,1024,768]{2,0,1:T(4,128)(2,1)S(1)} fusion(bf16[2,1024,768]{2,1,0:T(8,128)(2,1)S(1)} %copy-done, s32[2]{0:T(128)S(1)} %and_select_fusion), kind=kOutput, calls=%fused_computation.104 | convolution fusion | flops 15728648 | bytes 9437192 | tf_op jit(solution)/shard_map/gk,kld->gld/dot_general | solution.py:358
  36.3 114.9 %all-reduce.19 = (bf16[768]{0:T(1024)(128)(2,1)S(1)}, bf16[768]{0:T(1024)(128)(2,1)S(1)}, bf16[768]{0:T(1024)(128)(2,1)S(1)}, bf16[768]{0:T(1024)(128)(2,1)S(1)}...) all-reduce(bf16[768]{0:T(1024)(128)(2,1)S(1)} %dynamic-update-slice, ...), channel_id=1, replica_groups=mesh['dp'=8,'fsdp'=4] {'dp','fsdp'}, use_global_device_ids=true, to_apply=%add | all-reduce | flops 9216 | bytes 36864
  164.8 7.9 fusion.44
  178.5 8.4 copy.152
  224.1 12.3 fusion.36
  236.5 20.8 %fusion = (f32[12,512]{1,0:T(8,128)S(1)}, f32[12,512]{1,0:T(8,128)S(1)}, f32[12,512,1024]{2,1,0:T(8,128)}) fusion(f32[12,512]{1,0:T(8,128)S(1)} %get-tuple-element.216, f32[12,512,1024]{2,1,0:T(8,128)} %get-tuple-element.217, pred[1024]{0:T(1024)(128)(4,1)S(1)} %iota_compare_fusion.1, bf16[512,12,64]{0,2,1:T(8,128)(2,1)} %bitcast.233, ...), kind=kOutput, calls=%fused_computation.24 | convolution fusion | flops 849334272 | bytes 52765696 | tf_op jit(solution)/shard_map/qhd,khd->hqk/dot_general | solution.py:46
  257.9 11.4 fusion.1
  270.0 12.4 fusion.103
  282.4 12.0 fusion.102
  300.5 12.2 fusion.38
  312.7 20.9 %fusion.2 = (f32[12,512]{1,0:T(8,128)S(1)}, f32[12,512]{1,0:T(8,128)S(1)}, f32[12,512,1024]{2,1,0:T(8,128)}) fusion(f32[12,512]{1,0:T(8,128)S(1)} %get-tuple-element.219, f32[12,512,1024]{2,1,0:T(8,128)} %get-tuple-element.220, pred[1024]{0:T(1024)(128)(4,1)S(1)} %iota_compare_fusion, bf16[512,12,64]{0,2,1:T(8,128)(2,1)} %bitcast.235, ...), kind=kOutput, calls=%fused_computation.26 | convolution fusion | flops 849334272 | bytes 52765696 | tf_op jit(solution)/shard_map/qhd,khd->hqk/dot_general | solution.py:46
  334.2 11.2 fusion.3
  346.1 11.3 fusion.105
  357.4 11.2 fusion.104
  382.7 7.7 fusion.147
  394.9 68.5 %multiply_convert_fusion.5 = (bf16[1024,3072]{1,0:T(8,128)(2,1)}, f32[1024,3072]{1,0:T(8,128)}, bf16[1024,3072]{1,0:T(8,128)(2,1)}, f32[1024,3072]{1,0:T(8,128)}, f32[1024,3072]{1,0:T(8,128)}) fusion(f32[3072]{0:T(1024)S(1)} %copy-done.118, f32[1024,3072]{1,0:T(8,128)S(1)} %fusion.147, bf16[768,3072]{1,0:T(8,128)(2,1)S(1)} %copy-done.45, ...), kind=kOutput, calls=%fused_computation.61 | convolution fusion | flops 5247074304 | bytes 69218304 | tf_op jit(solution)/shard_map/dot_general | solution.py:29
  463.5 10.0 fusion.171
  473.5 12.7 fusion.158
  489.5 9.5 fusion.73
  508.9 19.2 %convert_reduce_fusion = (f32[3072]{0:T(1024)}, bf16[1024,3072]{1,0:T(8,128)(2,1)}) fusion(f32[1024,3072]{1,0:T(8,128)} %get-tuple-element.193, bf16[1024,768]{0,1:T(8,128)(2,1)} %get-tuple-element.149, bf16[3072,768]{1,0:T(8,128)(2,1)} %all-gather.11.cloned.1.call-done, f32[1024,3072]{1,0:T(8,128)} %copy-done.21, f32[3072]{0:T(1024)S(1)} %copy-done.118), kind=kOutput, calls=%fused_computation.40 | convolution fusion | flops 4885312512 | bytes 37773312 | tf_op jit(solution)/shard_map/dot_general | solution.py:39
  528.1 11.5 add_add_fusion.4
  539.6 19.2 %convert_reduce_fusion.1 = (f32[3072]{0:T(1024)}, bf16[1024,3072]{1,0:T(8,128)(2,1)}) fusion(f32[1024,3072]{1,0:T(8,128)} %get-tuple-element.165, bf16[1024,768]{0,1:T(8,128)(2,1)} %get-tuple-element.196, bf16[3072,768]{1,0:T(8,128)(2,1)} %all-gather.11.cloned.1.call-done, f32[1024,3072]{1,0:T(8,128)} %get-tuple-element.223, f32[3072]{0:T(1024)S(1)} %copy-done.118), kind=kOutput, calls=%fused_computation.41 | convolution fusion | flops 4885312512 | bytes 37773312 | tf_op jit(solution)/shard_map/dot_general | solution.py:39
  558.8 13.6 %multiply_reduce_fusion.5 = (f32[768]{0:T(1024)}, f32[1024]{0:T(1024)S(1)}, f32[768]{0:T(1024)}, f32[768]{0:T(1024)}, f32[1024]{0:T(1024)S(1)}, /*index=5*/f32[768]{0:T(1024)}, f32[1024,768]{0,1:T(8,128)S(1)}) fusion(f32[1024,768]{0,1:T(8,128)S(1)} %copy-done.6, f32[1024]{0:T(1024)S(1)} %copy-done.97, f32[1024]{0:T(1024)S(1)} %copy-done.87, ...), kind=kOutput, calls=%fused_computation.147 | convolution fusion | flops 4852279296 | bytes 28375040 | tf_op jit(solution)/shard_map/dot_general | solution.py:39
  584.2 10.4 fusion.172
  594.6 12.6 fusion.14
  607.2 35.2 %multiply_reduce_fusion.2 = (f32[12,512]{1,0:T(8,128)S(1)}, f32[12,512]{1,0:T(8,128)S(1)}, f32[12,512,1024]{2,1,0:T(8,128)}) fusion(f32[12,512]{1,0:T(8,128)S(1)} %copy-done.84, f32[12,512,1024]{2,1,0:T(8,128)} %get-tuple-element.218, pred[1024]{0:T(1024)(128)(4,1)S(1)} %copy-done.117, f32[12,512,1024]{2,1,0:T(8,128)} %fusion.172, ...), kind=kOutput, calls=%fused_computation.7 | convolution fusion | flops 868208640 | bytes 103121920 | tf_op jit(solution)/shard_map/qhd,khd->hqk/dot_general | solution.py:67
  642.4 41.9 %multiply_convert_fusion.2 = (bf16[12,512,1024]{2,1,0:T(8,128)(2,1)}, bf16[12,512,1024]{2,1,0:T(8,128)(2,1)}) fusion(f32[12,512,1024]{2,1,0:T(8,128)} %get-tuple-element.227, f32[12,512]{1,0:T(8,128)S(1)} %get-tuple-element.120, f32[12,512]{1,0:T(8,128)S(1)} %copy-done.84, f32[12,512,1024]{2,1,0:T(8,128)} %get-tuple-element.218, ...), kind=kLoop, calls=%fused_computation.6 | loop fusion | flops 75497472 | bytes 125928448 | tf_op jit(solution)/shard_map/convert_element_type | solution.py:72
  684.4 9.5 fusion.98
  708.5 14.1 %add_convert_fusion.5 = bf16[12,64,1024]{2,1,0:T(8,128)(2,1)} fusion(f32[12,64,1024]{2,1,0:T(8,128)} %fusion.14, bf16[512,12,64]{0,2,1:T(8,128)(2,1)} %bitcast.226, f32[12,512]{1,0:T(8,128)S(1)} %copy-done.82, f32[12,512,1024]{2,1,0:T(8,128)} %get-tuple-element.217, pred[1024]{0:T(1024)(128)(4,1)S(1)} %copy-done.117), kind=kOutput, calls=%fused_computation.159 | convolution fusion | flops 832045056 | bytes 30696448 | tf_op jit(solution)/shard_map/hqk,qhd->khd/dot_general | solution.py:82
  722.6 10.4 fusion.174
  733.0 12.9 fusion.10
  745.9 36.7 %multiply_reduce_fusion = (f32[12,512]{1,0:T(8,128)S(1)}, f32[12,512]{1,0:T(8,128)S(1)}, f32[12,512,1024]{2,1,0:T(8,128)}) fusion(f32[12,512]{1,0:T(8,128)S(1)} %copy-done.83, f32[12,512,1024]{2,1,0:T(8,128)} %get-tuple-element.221, pred[1024]{0:T(1024)(128)(4,1)S(1)} %copy-done.115, f32[12,512,1024]{2,1,0:T(8,128)} %fusion.174, ...), kind=kOutput, calls=%fused_computation.1 | convolution fusion | flops 868208640 | bytes 103121920 | tf_op jit(solution)/shard_map/qhd,khd->hqk/dot_general | solution.py:67
  782.6 41.9 %multiply_convert_fusion = (bf16[12,512,1024]{2,1,0:T(8,128)(2,1)}, bf16[12,512,1024]{2,1,0:T(8,128)(2,1)}) fusion(f32[12,512,1024]{2,1,0:T(8,128)} %get-tuple-element.226, f32[12,512]{1,0:T(8,128)S(1)} %get-tuple-element.122, f32[12,512]{1,0:T(8,128)S(1)} %copy-done.83, f32[12,512,1024]{2,1,0:T(8,128)} %get-tuple-element.221, ...), kind=kLoop, calls=%fused_computation | loop fusion | flops 75497472 | bytes 125928448 | tf_op jit(solution)/shard_map/convert_element_type | solution.py:72
  824.6 10.0 fusion.101
  845.2 9.0 fusion.99
  864.4 9.6 fusion.78
  874.0 8.7 fusion.100
  883.8 11.9 add_convert_fusion.3
  896.9 11.7 convolution_add_fusion
  909.3 8.6 fusion.149
  917.9 10.8 convolution_add_fusion.2
  930.2 7.6 fusion.177
  937.8 10.7 convolution_add_fusion.1
  949.2 8.3 fusion.93
  1000.1 91.5 %all-reduce.18 = (f32[768]{0:T(1024)S(1)}, f32[768]{0:T(1024)S(1)}, f32[768]{0:T(1024)S(1)}, f32[768]{0:T(1024)S(1)}, f32[768]{0:T(1024)S(1)}, /*index=5*/f32[30...) all-reduce(f32[768]{0:T(1024)S(1)} %add.358, ...), channel_id=3, replica_groups=mesh['dp'=8,'fsdp'=4] {'dp','fsdp'}, use_global_device_ids=true, to_apply=%region_33.34.clone | all-reduce | flops 9216 | bytes 73728
  1097.7 9.7 fusion.47
  1111.3 57.4 %reduce-scatter.9.cloned.1.call-done = f32[24,3072]{1,0:T(8,128)} async-done(((f32[768,3072]{1,0:T(8,128)}), f32[24,3072]{1,0:T(8,128)}) %reduce-scatter.9.cloned.1.call-update) | async-done | bytes 294928 | tf_op jit(solution)/shard_map/reduce_scatter | solution.py:459
  1168.7 142.2 %reduce-scatter.11.cloned.1.call-done = f32[96,768]{1,0:T(8,128)} async-done(((f32[3072,768]{1,0:T(8,128)}), f32[96,768]{1,0:T(8,128)}) %reduce-scatter.11.cloned.1.call-update) | async-done | bytes 294928 | tf_op jit(solution)/shard_map/reduce_scatter | solution.py:461
  (452 shorter events, 209.8 us)
Async XLA Ops:
  7.2 186.0 %all-gather.5.cloned.1.call-start = ((), (), s32[]{:S(2)}) async-start(), calls=%async_computation.6 | async-start | bytes 3649536 | tf_op jit(solution)/shard_map/all_gather | solution.py:273
  7.9 362.4 %all-gather.7.cloned.1.call-start = ((), (), s32[]{:S(2)}) async-start(), calls=%async_computation.7 | async-start | bytes 1216512 | tf_op jit(solution)/shard_map/all_gather | solution.py:276
  8.7 373.9 %all-gather.9.cloned.1.call-start = ((), (), s32[]{:S(2)}) async-start(), calls=%async_computation.8 | async-start | bytes 4866048 | tf_op jit(solution)/shard_map/all_gather | solution.py:280
  10.2 14.4 %copy-start.136 = (s32[2]{0:T(128)}, s32[2]{0:T(128)S(1)}, u32[]{:S(2)}) copy-start(s32[2]{0:T(128)S(1)} %and_select_fusion) | copy-start | bytes 28
  28.1 136.7 %all-to-all-start = ((bf16[4,1024,768]{2,1,0:T(8,128)(2,1)}), bf16[4,1024,768]{2,1,0:T(8,128)(2,1)}, u32[]{:S(2)}, u32[]{:S(2)}) async-start(bf16[4,1024,768]{2,1,0:T(8,128)(2,1)} %copy.121), calls=%async_computation | async-start | bytes 12582912 | tf_op jit(solution)/shard_map/all_to_all | solution.py:361
  33.5 429.9 %all-gather.11.cloned.1.call-start = ((), (), s32[]{:S(2)}) async-start(), calls=%async_computation.9 | async-start | bytes 4866048 | tf_op jit(solution)/shard_map/all_gather | solution.py:282
  34.1 1077.3 %reduce-scatter.7.cloned.1.call-start = ((), (), s32[]{:S(2)}) async-start(), calls=%async_computation.11 | async-start | bytes 2433024 | tf_op jit(solution)/shard_map/reduce_scatter | solution.py:455
  162.2 120.2 %copy-start.116 = (pred[1024]{0:T(1024)(128)(4,1)}, pred[1024]{0:T(1024)(128)(4,1)S(1)}, u32[]{:S(2)}) copy-start(pred[1024]{0:T(1024)(128)(4,1)S(1)} %iota_compare_fusion.1) | copy-start | bytes 3076
  162.8 194.5 %copy-start.114 = (pred[1024]{0:T(1024)(128)(4,1)}, pred[1024]{0:T(1024)(128)(4,1)S(1)}, u32[]{:S(2)}) copy-start(pred[1024]{0:T(1024)(128)(4,1)S(1)} %iota_compare_fusion) | copy-start | bytes 3076
  204.9 31.6 %copy-start.9 = (bf16[1024,768]{0,1:T(8,128)(2,1)}, bf16[1024,768]{0,1:T(8,128)(2,1)S(1)}, u32[]{:S(2)}) copy-start(bf16[1024,768]{0,1:T(8,128)(2,1)S(1)} %copy.126) | copy-start | bytes 4718596
  224.1 58.3 %copy-start.17 = (bf16[1024,768]{0,1:T(8,128)(2,1)}, bf16[1024,768]{0,1:T(8,128)(2,1)S(1)}, u32[]{:S(2)}) copy-start(bf16[1024,768]{0,1:T(8,128)(2,1)S(1)} %copy.124) | copy-start | bytes 4718596
  296.2 16.5 %copy-start.11 = (bf16[1024,768]{0,1:T(8,128)(2,1)}, bf16[1024,768]{0,1:T(8,128)(2,1)S(1)}, u32[]{:S(2)}) copy-start(bf16[1024,768]{0,1:T(8,128)(2,1)S(1)} %copy.131) | copy-start | bytes 4718596
  300.5 56.9 %copy-start.15 = (bf16[1024,768]{0,1:T(8,128)(2,1)}, bf16[1024,768]{0,1:T(8,128)(2,1)S(1)}, u32[]{:S(2)}) copy-start(bf16[1024,768]{0,1:T(8,128)(2,1)S(1)} %copy.129) | copy-start | bytes 4718596
  357.4 11.3 copy-start.67
  357.4 11.3 copy-start.68
  382.6 12.3 copy-start.118
  382.6 12.2 copy-start.45
  382.6 12.2 copy-start.63
  473.5 12.7 copy-start.14
  473.5 12.7 copy-start.85
  473.5 12.7 copy-start.90
  558.8 13.6 %copy-start.94 = (f32[1024]{0:T(1024)S(1)}, f32[1024]{0:T(1024)}, u32[]{:S(2)}) copy-start(f32[1024]{0:T(1024)} %copy-done.93) | copy-start | bytes 12292
  558.8 13.6 %copy-start.92 = (f32[1024]{0:T(1024)S(1)}, f32[1024]{0:T(1024)}, u32[]{:S(2)}) copy-start(f32[1024]{0:T(1024)} %copy-done.91) | copy-start | bytes 12292
  558.8 13.6 %copy-start.55 = (f32[1024,768]{0,1:T(8,128)S(1)}, f32[1024,768]{0,1:T(8,128)}, u32[]{:S(2)}) copy-start(f32[1024,768]{0,1:T(8,128)} %add_add_fusion.4) | copy-start | bytes 9437188
  582.6 11.9 copy-start.35
  584.2 10.4 copy-start.84
  584.2 10.4 copy-start.117
  594.5 12.7 copy-start.82
  642.4 41.9 %copy-start.10 = (bf16[1024,768]{0,1:T(8,128)(2,1)S(1)}, bf16[1024,768]{0,1:T(8,128)(2,1)}, u32[]{:S(2)}) copy-start(bf16[1024,768]{0,1:T(8,128)(2,1)} %copy-done.9) | copy-start | bytes 4718596
  708.4 402.9 %reduce-scatter.5.cloned.1.call-start = ((), (), s32[]{:S(2)}) async-start(), calls=%async_computation.10 | async-start | bytes 7299072 | tf_op jit(solution)/shard_map/reduce_scatter | solution.py:452
  708.5 14.1 %copy-start.16 = (bf16[1024,768]{0,1:T(8,128)(2,1)S(1)}, bf16[1024,768]{0,1:T(8,128)(2,1)}, u32[]{:S(2)}) copy-start(bf16[1024,768]{0,1:T(8,128)(2,1)} %copy-done.15) | copy-start | bytes 4718596
  708.5 14.1 %copy-start.33 = (bf16[512,768]{0,1:T(8,128)(2,1)S(1)}, bf16[512,768]{0,1:T(8,128)(2,1)}, u32[]{:S(2)}) copy-start(bf16[512,768]{0,1:T(8,128)(2,1)} %get-tuple-element.184) | copy-start | bytes 2359300
  722.6 10.4 copy-start.49
  722.6 10.4 copy-start.83
  722.6 10.4 copy-start.115
  733.0 13.0 copy-start.81
  824.6 10.1 copy-start.29
  824.6 17.1 %slice-start = ((s8[12582912]{0:T(1024)(128)(4,1)}), s8[4194304]{0:T(1024)(128)(4,1)S(1)}, s32[]{:S(2)}) async-start(s8[12582912]{0:T(1024)(128)(4,1)} %bitcast.201), calls=%async_computation.14 | async-start | bytes 8388608
  824.6 17.1 %slice-start.1 = ((s8[12582912]{0:T(1024)(128)(4,1)}), s8[4194304]{0:T(1024)(128)(4,1)S(1)}, s32[]{:S(2)}) async-start(s8[12582912]{0:T(1024)(128)(4,1)} %bitcast.201), calls=%async_computation.15 | async-start | bytes 8388608
  861.6 12.4 copy-start.36
  883.8 11.9 copy-start.39
  883.8 13.1 copy-start.23
  883.8 13.1 copy-start.46
  908.6 260.1 %reduce-scatter.9.cloned.1.call-start = ((), (), s32[]{:S(2)}) async-start(), calls=%async_computation.12 | async-start | bytes 9732096 | tf_op jit(solution)/shard_map/reduce_scatter | solution.py:459
  928.8 382.2 %reduce-scatter.11.cloned.1.call-start = ((), (), s32[]{:S(2)}) async-start(), calls=%async_computation.13 | async-start | bytes 9732096 | tf_op jit(solution)/shard_map/reduce_scatter | solution.py:461
  977.4 120.2 %all-to-all-start.1 = ((bf16[4,1024,768]{2,1,0:T(8,128)(2,1)}), bf16[4,1024,768]{2,1,0:T(8,128)(2,1)}, u32[]{:S(2)}, u32[]{:S(2)}) async-start(bf16[4,1024,768]{2,1,0:T(8,128)(2,1)} %copy.140), calls=%async_computation.1 | async-start | bytes 12582912 | tf_op jit(solution)/shard_map/all_to_all | solution.py:432
  996.0 101.7 %copy-start.137 = (s32[2]{0:T(128)S(1)}, s32[2]{0:T(128)}, u32[]{:S(2)}) copy-start(s32[2]{0:T(128)} %copy-done.136) | copy-start | bytes 28
  1097.7 213.3 %copy-start.1 = (bf16[2,1024,768]{2,1,0:T(8,128)(2,1)S(1)}, bf16[2,1024,768]{2,1,0:T(8,128)(2,1)}, u32[]{:S(2)}) copy-start(bf16[2,1024,768]{2,1,0:T(8,128)(2,1)} %param.17) | copy-start | bytes 9437188
  (107 other events, 546.4 us)
Sparse Core Ops, SparseCore 0:
  10.9 70.8 all-gather.4
  84.7 53.5 all-gather.6
  141.2 62.4 all-gather.8
  206.5 62.4 all-gather.10
  708.6 98.2 reduce-scatter.6
  908.7 119.0 reduce-scatter.4
  1034.3 134.4 reduce-scatter.8
  1176.2 134.7 reduce-scatter.10
where the time goes:
time: 1330 us; the launch traced here: 1320 us
  matrix products  621 us (47%)
  blocking collectives  206 us (15%)
  waiting for transfers between devices  202 us (15%)
  other arithmetic  161 us (12%)
  local copies, waits for them, and re-layouts  94.4 us (7%)
  between operations  21.9 us (2%)
    unnamed x2, blocking collectives  206 us
    reduce_scatter x1, waiting for transfers between devices, body(): lax.psum_scatter(total_downw, ('dp', 'fsdp'), scatter_dimension=0, tiled=...  142 us
    dot_general x8, matrix products, lower_dot(): return jnp.dot(left, right, preferred_element_type=jnp.float32)  120 us
    dot_general x4, matrix products, backward_block(): jnp.einsum('qhd,khd->hqk', grad_rows, value_heads, preferred_element_type...  92.6 us
    convert_element_type x2, other arithmetic, backward_block(): grad_scores = (weights * (grad_weights - jnp.sum(weights * grad_weights,...  83.9 us
    dot_general x8, matrix products, back_dot(): lax.dot_general(left, right, (((1,), (1,)), ((), ())), preferred_element_...  78.4 us
    dot_general x4, matrix products, score_block(): jnp.einsum('qhd,khd->hqk', queries, key_heads, preferred_element_type=jnp...  66.2 us
    dot_general x8, matrix products, rows_dot(): lax.dot_general(left, right, (((0,), (0,)), ((), ())), preferred_element_...  64.8 us
  transfers between devices with their start and end apart: 10, of which 2 were waited for; matrix products, arithmetic and copies ran while one was open for 47% of the time, Pallas kernels for 0%

commit v1 on v0

v1 whole, which is shorter than its diff:
```python
import functools
import math

import jax
import jax.numpy as jnp
from jax import lax
from jax.experimental import pallas as pl
from jax.experimental.pallas import tpu as pltpu
from jax.sharding import PartitionSpec as P

HEADS = 12
HEAD_DIM = 64
PAIR = 2 * HEAD_DIM
PAIRS = HEADS // 2
BLOCK = 256

f32 = jnp.float32
bf16 = jnp.bfloat16
norm_eps = 1e-05
masked_fill = -1e30
BOTH = ("dp", "fsdp")


def nn(left, right):
    return lax.dot_general(left, right, (((1,), (0,)), ((), ())), preferred_element_type=f32)


def nt(left, right):
    return lax.dot_general(left, right, (((1,), (1,)), ((), ())), preferred_element_type=f32)


def tn(left, right):
    return lax.dot_general(left, right, (((0,), (0,)), ((), ())), preferred_element_type=f32)


def block_count(length):
    return (length + (BLOCK - 1)) // BLOCK


def forward_kernel(len_ref, x_ref, w_ref, bias_ref, qkv_ref, ctx_ref, lse_ref):
    seq, pair = pl.program_id(0), pl.program_id(1)
    length = len_ref[seq]
    blocks = block_count(length)
    rows_all, width = x_ref.shape[1], x_ref.shape[2]
    lane = lax.broadcasted_iota(jnp.int32, (1, PAIR), 1)

    @pl.when(pair == 0)
    def _():
        @pl.loop(0, blocks)
        def _(index):
            rows = pl.ds(pl.multiple_of(index * BLOCK, BLOCK), BLOCK)
            tokens = x_ref[0, rows, :]
            for part in range(3):
                cols = slice(part * width, (part + 1) * width)
                projected = nn(tokens, w_ref[:, cols])
                if part != 1:
                    projected = projected + bias_ref[part : part + 1, :].astype(f32)
                projected = projected.astype(bf16)
                if part == 0:
                    projected = projected * jnp.asarray(1.0 / math.sqrt(HEAD_DIM), bf16)
                for head in range(PAIRS):
                    qkv_ref[0, part * PAIRS + head, rows, :] = projected[:, head * PAIR : (head + 1) * PAIR]

    for keys in range(1, rows_all // BLOCK + 1):

        @pl.when(blocks == keys)
        def _(keys=keys):
            count = keys * BLOCK
            query = qkv_ref[0, pair, 0:count, :]
            key = qkv_ref[0, PAIRS + pair, 0:count, :]
            value = qkv_ref[0, 2 * PAIRS + pair, 0:count, :]
            usable = lax.broadcasted_iota(jnp.int32, (1, BLOCK), 1) + (count - BLOCK) < length
            outs = []
            for head in range(2):
                mine = (lane < HEAD_DIM) if head == 0 else (lane >= HEAD_DIM)
                scores = nt(jnp.where(mine, query, jnp.zeros_like(query)), key)
                last = jnp.where(usable, scores[:, count - BLOCK :], masked_fill)
                scores = jnp.concatenate([scores[:, : count - BLOCK], last], axis=1) if keys > 1 else last
                top = jnp.max(scores, axis=1, keepdims=True)
                powers = jnp.exp(scores - top)
                total = jnp.sum(powers, axis=1, keepdims=True)
                outs.append(nn(powers.astype(bf16), value) * (1.0 / total))
                lse_ref[0, 0, 0:count, head : head + 1] = top + jnp.log(total)
            ctx_ref[0, 0:count, :] = jnp.where(lane < HEAD_DIM, outs[0], outs[1]).astype(bf16)


def attention_forward(lengths, tokens, w_qkv, biases):
    seqs, rows, width = tokens.shape
    whole = lambda shape: pl.BlockSpec(shape, lambda s, p, *_: (0,) * len(shape), pipeline_mode=pl.Buffered(1))
    return pl.pallas_call(
        forward_kernel,
        out_shape=(
            jax.ShapeDtypeStruct((seqs, 3 * PAIRS, rows, PAIR), bf16),
            jax.ShapeDtypeStruct((seqs, rows, width), bf16),
            jax.ShapeDtypeStruct((seqs, PAIRS, rows, PAIR), f32),
        ),
        grid_spec=pltpu.PrefetchScalarGridSpec(
            num_scalar_prefetch=1,
            grid=(seqs, PAIRS),
            in_specs=[
                pl.BlockSpec((1, rows, width), lambda s, p, *_: (s, 0, 0)),
                whole(w_qkv.shape),
                whole(biases.shape),
            ],
            out_specs=[
                pl.BlockSpec((1, 3 * PAIRS, rows, PAIR), lambda s, p, *_: (s, 0, 0, 0)),
                pl.BlockSpec((1, rows, PAIR), lambda s, p, *_: (s, 0, p)),
                pl.BlockSpec((1, 1, rows, PAIR), lambda s, p, *_: (s, p, 0, 0)),
            ],
        ),
        compiler_params=pltpu.CompilerParams(vmem_limit_bytes=56 << 20),
        cost_estimate=pl.CostEstimate(
            flops=60_000_000_000, transcendentals=30_000_000, bytes_accessed=30_000_000
        ),
        name="attention_forward",
    )(lengths, tokens, w_qkv, biases)


def normal_tail(values):
    size = jnp.abs(values)
    bell = jnp.exp(-0.5 * values * values)
    t = 1.0 / (1.0 + (0.3275911 / math.sqrt(2.0)) * size)
    poly = t * (
        0.5 * 0.254829592
        + t * (0.5 * -0.284496736 + t * (0.5 * 1.421413741 + t * (0.5 * -1.453152027 + t * (0.5 * 1.061405429))))
    )
    tail = poly * bell
    return jnp.where(values >= 0, 1.0 - tail, tail), bell


def row_mean(values):
    return jnp.mean(values, axis=-1, keepdims=True)


def middle_kernel(
    len_ref, in_slot, out_slot, x_ref, ctx_ref, cot_ref, wo_ref, wu_ref, wd_ref, vec_ref, bu_ref,
    out_ref, gres_ref, gctx_ref, dwo_ref, dwu_ref, dwd_ref, dvec_ref, dbu_ref, sums_ref,
    acc_o, acc_u, acc_d, active, slope, stage, sems,
):
    seq, index = pl.program_id(0), pl.program_id(1)
    first = jnp.logical_and(seq == 0, index == 0)
    final = jnp.logical_and(seq == pl.num_programs(0) - 1, index == pl.num_programs(1) - 1)
    length = len_ref[seq]
    width = x_ref.shape[2]
    chunks = wd_ref.shape[0] // width

    @pl.when(first)
    def _():
        acc_o[...] = jnp.zeros_like(acc_o)
        acc_u[...] = jnp.zeros_like(acc_u)
        acc_d[...] = jnp.zeros_like(acc_d)
        dvec_ref[...] = jnp.zeros_like(dvec_ref)
        dbu_ref[...] = jnp.zeros_like(dbu_ref)

    @pl.when(index == 0)
    def _():
        sums_ref[...] = jnp.zeros_like(sums_ref)

    @pl.when(index * BLOCK >= length)
    def _():
        out_ref[...] = jnp.zeros_like(out_ref)

    @pl.when(index * BLOCK < length)
    def _():
        vec = lambda place: vec_ref[place : place + 1, :].astype(f32)
        bias_out, gain_a, shift_a, bias_down, gain_f, shift_f = (vec(place) for place in range(6))
        valid = (lax.broadcasted_iota(jnp.int32, (BLOCK, 1), 0) + index * BLOCK < length).astype(f32)
        tokens = x_ref[0].astype(f32)
        context = ctx_ref[0]
        branch_a = nn(context, wo_ref[...]) + bias_out
        mixed = tokens + branch_a
        center = mixed - row_mean(mixed)
        scale_a = lax.rsqrt(row_mean(center * center) + norm_eps)
        hat_a = center * scale_a
        hidden = hat_a * gain_a + shift_a
        hidden_low = hidden.astype(bf16)
        branch_f = bias_down
        for chunk in range(chunks):
            cols = slice(chunk * width, (chunk + 1) * width)
            gate = nn(hidden_low, wu_ref[:, cols]) + bu_ref[:, cols].astype(f32)
            share, bell = normal_tail(gate)
            act = (gate * share).astype(bf16)
            active[:, cols] = act
            slope[:, cols] = share + gate * bell * (1.0 / math.sqrt(2.0 * math.pi))
            branch_f = branch_f + nn(act, wd_ref[cols, :])
        mixed_f = hidden + branch_f
        center = mixed_f - row_mean(mixed_f)
        scale_f = lax.rsqrt(row_mean(center * center) + norm_eps)
        hat_f = center * scale_f
        out_ref[0] = ((hat_f * gain_f + shift_f) * valid).astype(bf16)
        g_result = cot_ref[0].astype(f32) * valid
        g_hat = g_result * gain_f
        g_res2 = scale_f * (g_hat - row_mean(g_hat) - hat_f * row_mean(g_hat * hat_f))
        g_ffn = g_res2.astype(bf16)
        g_hidden = g_res2
        for chunk in range(chunks):
            cols = slice(chunk * width, (chunk + 1) * width)
            g_gate = nt(g_ffn, wd_ref[cols, :]) * slope[:, cols]
            g_low = g_gate.astype(bf16)
            acc_d[cols, :] += tn(active[:, cols], g_ffn)
            acc_u[:, cols] += tn(hidden_low, g_low)
            dbu_ref[:, cols] += jnp.sum(g_low.astype(f32), axis=0, keepdims=True)
            g_hidden = g_hidden + nt(g_low, wu_ref[:, cols])
        g_hat = g_hidden * gain_a
        g_res1 = scale_a * (g_hat - row_mean(g_hat) - hat_a * row_mean(g_hat * hat_a))
        g_attn = g_res1.astype(bf16)
        gres_ref[0] = g_res1
        gctx_ref[0] = nt(g_attn, wo_ref[...]).astype(bf16)
        acc_o[...] += tn(context, g_attn)
        column = lambda values: jnp.sum(values, axis=0, keepdims=True)
        dvec_ref[0:1, :] += column(g_attn.astype(f32))
        dvec_ref[1:2, :] += column(g_hidden * hat_a)
        dvec_ref[2:3, :] += column(g_hidden)
        dvec_ref[3:4, :] += column(g_ffn.astype(f32))
        dvec_ref[4:5, :] += column(g_result * hat_f)
        dvec_ref[5:6, :] += column(g_result)
        sums_ref[0, 0:1, :] += column(tokens * tokens * valid)
        sums_ref[0, 1:2, :] += column(branch_a * branch_a * valid)
        sums_ref[0, 2:3, :] += column(branch_f * branch_f * valid)

    @pl.when(final)
    def _():
        pieces = [(acc_o, dwo_ref, slice(None), slice(None))]
        for chunk in range(chunks):
            cols = slice(chunk * width, (chunk + 1) * width)
            pieces.append((acc_u, dwu_ref, slice(None), cols))
            pieces.append((acc_d, dwd_ref, cols, slice(None)))
        copies = []
        for place, (acc, out, rows, cols) in enumerate(pieces):
            slot = place % 2
            if place >= 2:
                copies[place - 2].wait()
            stage[slot] = acc[rows, cols].astype(bf16)
            copies.append(pltpu.make_async_copy(stage.at[slot], out.at[rows, cols], sems.at[slot]))
            copies[-1].start()
        copies[-2].wait()
        copies[-1].wait()


def middle(lengths, in_slot, out_slot, tokens, context, cots, w_out, w_up, w_down, vectors, bias_up):
    seqs, rows, width = tokens.shape
    slots = cots.shape[0]
    hidden = w_up.shape[1]
    whole = lambda shape: pl.BlockSpec(shape, lambda s, i, *_: (0,) * len(shape), pipeline_mode=pl.Buffered(1))
    inside = lambda s, i, lens: jnp.minimum(i, block_count(lens[s]) - 1)
    here = pl.BlockSpec((1, BLOCK, width), lambda s, i, lens, a, b: (s, inside(s, i, lens), 0))
    kept = pl.BlockSpec((1, BLOCK, width), lambda s, i, lens, a, b: (s, inside(s, i, lens), 0))
    total = 2 * seqs * rows * (2 * width * width + 4 * width * hidden) * 2
    return pl.pallas_call(
        middle_kernel,
        out_shape=(
            jax.ShapeDtypeStruct((slots, rows, width), bf16),
            jax.ShapeDtypeStruct((seqs, rows, width), f32),
            jax.ShapeDtypeStruct((seqs, rows, width), bf16),
            jax.ShapeDtypeStruct(w_out.shape, bf16),
            jax.ShapeDtypeStruct(w_up.shape, bf16),
            jax.ShapeDtypeStruct(w_down.shape, bf16),
            jax.ShapeDtypeStruct((8, width), f32),
            jax.ShapeDtypeStruct((1, hidden), f32),
            jax.ShapeDtypeStruct((seqs, 8, width), f32),
        ),
        grid_spec=pltpu.PrefetchScalarGridSpec(
            num_scalar_prefetch=3,
            grid=(seqs, rows // BLOCK),
            in_specs=[
                here,
                here,
                pl.BlockSpec((1, BLOCK, width), lambda s, i, lens, a, b: (a[s], inside(s, i, lens), 0)),
                whole(w_out.shape),
                whole(w_up.shape),
                whole(w_down.shape),
                whole(vectors.shape),
                whole(bias_up.shape),
            ],
            out_specs=[
                pl.BlockSpec((1, BLOCK, width), lambda s, i, lens, a, b: (b[s], i, 0)),
                kept,
                kept,
                pl.BlockSpec(memory_space=pl.ANY),
                pl.BlockSpec(memory_space=pl.ANY),
                pl.BlockSpec(memory_space=pl.ANY),
                whole((8, width)),
                whole((1, hidden)),
                pl.BlockSpec((1, 8, width), lambda s, i, *_: (s, 0, 0)),
            ],
            scratch_shapes=[
                pltpu.VMEM(w_out.shape, f32),
                pltpu.VMEM(w_up.shape, f32),
                pltpu.VMEM(w_down.shape, f32),
                pltpu.VMEM((BLOCK, hidden), bf16),
                pltpu.VMEM((BLOCK, hidden), f32),
                pltpu.VMEM((2, width, width), bf16),
                pltpu.SemaphoreType.DMA((2,)),
            ],
        ),
        compiler_params=pltpu.CompilerParams(vmem_limit_bytes=60 << 20),
        cost_estimate=pl.CostEstimate(flops=total, transcendentals=seqs * rows * hidden, bytes_accessed=60_000_000),
        name="middle",
    )(lengths, in_slot, out_slot, tokens, context, cots, w_out, w_up, w_down, vectors, bias_up)


def backward_kernel(
    len_ref, x_ref, qkv_in, ctx_ref, gctx_ref, lse_ref, gres_ref, w_ref,
    gin_ref, dw_ref, dvec_ref, mixed, acc_w, acc_k, acc_v, stage, sems,
):
    seq, pair = pl.program_id(0), pl.program_id(1)
    length = len_ref[seq]
    blocks = block_count(length)
    rows_all, width = x_ref.shape[1], x_ref.shape[2]
    lane = lax.broadcasted_iota(jnp.int32, (1, PAIR), 1)
    factor = 1.0 / math.sqrt(HEAD_DIM)

    @pl.when(jnp.logical_and(seq == 0, pair == 0))
    def _():
        acc_w[...] = jnp.zeros_like(acc_w)
        dvec_ref[...] = jnp.zeros_like(dvec_ref)

    for keys in range(1, rows_all // BLOCK + 1):

        @pl.when(blocks == keys)
        def _(keys=keys):
            count = keys * BLOCK
            key = qkv_in[0, 1, 0, 0:count, :]
            value = qkv_in[0, 2, 0, 0:count, :]
            usable = lax.broadcasted_iota(jnp.int32, (1, BLOCK), 1) + (count - BLOCK) < length
            acc_k[0:count, :] = jnp.zeros((count, PAIR), f32)
            acc_v[0:count, :] = jnp.zeros((count, PAIR), f32)

            @pl.loop(0, keys)
            def _(index):
                rows = pl.ds(pl.multiple_of(index * BLOCK, BLOCK), BLOCK)
                query = qkv_in[0, 0, 0, rows, :]
                grad = gctx_ref[0, rows, :]
                agree = grad.astype(f32) * ctx_ref[0, rows, :].astype(f32)
                g_query = jnp.zeros((BLOCK, PAIR), f32)
                for head in range(2):
                    mine = (lane < HEAD_DIM) if head == 0 else (lane >= HEAD_DIM)
                    only = lambda values: jnp.where(mine, values, jnp.zeros_like(values))
                    query_h, grad_h, key_h = only(query), only(grad), only(key)
                    delta = jnp.sum(only(agree), axis=1, keepdims=True)
                    scores = nt(query_h, key)
                    last = jnp.where(usable, scores[:, count - BLOCK :], masked_fill)
                    scores = jnp.concatenate([scores[:, : count - BLOCK], last], axis=1) if keys > 1 else last
                    probs = jnp.exp(scores - lse_ref[0, 0, rows, head : head + 1])
                    g_probs = nt(grad_h, value)
                    g_scores = (probs * (g_probs - delta)).astype(bf16)
                    g_query = g_query + nn(g_scores, key_h)
                    acc_k[0:count, :] += tn(g_scores, query_h)
                    acc_v[0:count, :] += tn(probs.astype(bf16), grad_h)
                mixed[pair, rows, :] = (g_query * factor).astype(bf16)

            mixed[PAIRS + pair, 0:count, :] = acc_k[0:count, :].astype(bf16)
            mixed[2 * PAIRS + pair, 0:count, :] = acc_v[0:count, :].astype(bf16)

    @pl.when(pair == PAIRS - 1)
    def _():
        @pl.loop(0, rows_all // BLOCK)
        def _(index):
            rows = pl.ds(pl.multiple_of(index * BLOCK, BLOCK), BLOCK)

            @pl.when(index >= blocks)
            def _():
                gin_ref[0, rows, :] = jnp.zeros((BLOCK, width), bf16)

            @pl.when(index < blocks)
            def _():
                tokens = x_ref[0, rows, :]
                g_in = gres_ref[0, rows, :]
                for part in range(3):
                    cols = slice(part * width, (part + 1) * width)
                    piece = jnp.concatenate([mixed[part * PAIRS + head, rows, :] for head in range(PAIRS)], axis=1)
                    g_in = g_in + nt(piece, w_ref[:, cols])
                    acc_w[:, cols] += tn(tokens, piece)
                    dvec_ref[part : part + 1, :] += jnp.sum(piece.astype(f32), axis=0, keepdims=True)
                gin_ref[0, rows, :] = g_in.astype(bf16)

    @pl.when(jnp.logical_and(seq == pl.num_programs(0) - 1, pair == PAIRS - 1))
    def _():
        copies = []
        for part in range(3):
            cols = slice(part * width, (part + 1) * width)
            slot = part % 2
            if part >= 2:
                copies[part - 2].wait()
            stage[slot] = acc_w[:, cols].astype(bf16)
            copies.append(pltpu.make_async_copy(stage.at[slot], dw_ref.at[:, cols], sems.at[slot]))
            copies[-1].start()
        copies[-2].wait()
        copies[-1].wait()


def attention_backward(lengths, tokens, qkv, context, g_context, lse, g_res1, w_qkv):
    seqs, rows, width = tokens.shape
    whole = lambda shape: pl.BlockSpec(shape, lambda s, p, *_: (0,) * len(shape), pipeline_mode=pl.Buffered(1))
    pair_cols = pl.BlockSpec((1, rows, PAIR), lambda s, p, *_: (s, 0, p))
    seq_rows = pl.BlockSpec((1, rows, width), lambda s, p, *_: (s, 0, 0))
    return pl.pallas_call(
        backward_kernel,
        out_shape=(
            jax.ShapeDtypeStruct((seqs, rows, width), bf16),
            jax.ShapeDtypeStruct(w_qkv.shape, bf16),
            jax.ShapeDtypeStruct((8, width), f32),
        ),
        grid_spec=pltpu.PrefetchScalarGridSpec(
            num_scalar_prefetch=1,
            grid=(seqs, PAIRS),
            in_specs=[
                seq_rows,
                pl.BlockSpec((1, 3, 1, rows, PAIR), lambda s, p, *_: (s, 0, p, 0, 0)),
                pair_cols,
                pair_cols,
                pl.BlockSpec((1, 1, rows, PAIR), lambda s, p, *_: (s, p, 0, 0)),
                seq_rows,
                whole(w_qkv.shape),
            ],
            out_specs=[
                seq_rows,
                pl.BlockSpec(memory_space=pl.ANY),
                whole((8, width)),
            ],
            scratch_shapes=[
                pltpu.VMEM((3 * PAIRS, rows, PAIR), bf16),
                pltpu.VMEM(w_qkv.shape, f32),
                pltpu.VMEM((rows, PAIR), f32),
                pltpu.VMEM((rows, PAIR), f32),
                pltpu.VMEM((2, width, width), bf16),
                pltpu.SemaphoreType.DMA((2,)),
            ],
        ),
        compiler_params=pltpu.CompilerParams(vmem_limit_bytes=60 << 20),
        cost_estimate=pl.CostEstimate(
            flops=120_000_000_000, transcendentals=30_000_000, bytes_accessed=40_000_000
        ),
        name="attention_backward",
    )(lengths, tokens, qkv.reshape(seqs, 3, PAIRS, rows, PAIR), context, g_context, lse, g_res1, w_qkv)


def body(
    tokens, lengths, deal_order, qkv_weight, query_bias, value_bias, out_weight, out_bias, attn_gain, attn_shift,
    up_weight, up_bias, down_weight, down_bias, ffn_gain, ffn_shift, cotangent,
):
    shards = lax.axis_size("fsdp")
    devices = lax.axis_size("dp") * shards
    seqs, rows, width = tokens.shape
    column = shards * seqs
    base = lax.axis_index("dp") * column
    member = lax.axis_index("fsdp")
    order = lax.dynamic_slice_in_dim(deal_order, base, column) - base
    mine = member * seqs
    own_lengths = lax.dynamic_slice_in_dim(lengths, base + mine, seqs)
    target = lax.dynamic_slice_in_dim(order, mine, seqs) // seqs
    dealt_here = mine + jnp.arange(seqs, dtype=jnp.int32)
    matches = order[None, :] == dealt_here[:, None]
    places = jnp.arange(column, dtype=jnp.int32)
    source = jnp.sum(jnp.where(matches, places[None, :], 0), axis=1) // seqs
    peers = jnp.arange(shards, dtype=jnp.int32)

    outgoing = cotangent[0][None]
    for place in range(1, seqs):
        outgoing = jnp.where((source[place] == peers)[:, None, None], cotangent[place][None], outgoing)
    cots = lax.all_to_all(outgoing, "fsdp", split_axis=0, concat_axis=0, tiled=True)

    gather = lambda shard: lax.all_gather(shard, BOTH, axis=0, tiled=True)
    small = jnp.concatenate(
        [query_bias, value_bias, out_bias, attn_gain, attn_shift, down_bias, ffn_gain, ffn_shift, up_bias]
    )
    per = width // devices
    small = lax.all_gather(small, BOTH, axis=0, tiled=False)
    vectors = [small[:, place * per : (place + 1) * per].reshape(1, width) for place in range(8)]
    bias_up = small[:, 8 * per :].reshape(1, -1)
    zero = jnp.zeros((1, width), bf16)
    qkv_bias = jnp.concatenate([vectors[0], zero, vectors[1]] + [zero] * 5, axis=0)
    mid_vectors = jnp.concatenate(vectors[2:] + [zero, zero], axis=0)
    w_qkv, w_out, w_up, w_down = gather(qkv_weight), gather(out_weight), gather(up_weight), gather(down_weight)

    qkv, context, lse = attention_forward(own_lengths, tokens, w_qkv, qkv_bias)
    results, g_res1, g_context, dw_out, dw_up, dw_down, dvec, dbu, sums = middle(
        own_lengths, target, target, tokens, context, cots, w_out, w_up, w_down, mid_vectors, bias_up
    )
    input_grad, dw_qkv, dqv = attention_backward(own_lengths, tokens, qkv, context, g_context, lse, g_res1, w_qkv)

    rms = jnp.sqrt(jnp.sum(sums[:, :3, :], axis=2) / (own_lengths.astype(f32) * width)[:, None])
    rms_out = jnp.sum(jnp.where((target[:, None] == peers[None, :])[:, :, None], rms[:, None, :], 0.0), axis=0)
    rms_here = lax.all_to_all(rms_out, "fsdp", split_axis=0, concat_axis=0, tiled=True)
    arrived = lax.all_to_all(results, "fsdp", split_axis=0, concat_axis=0, tiled=True)
    layer_out = jnp.stack([lax.dynamic_index_in_dim(arrived, source[t], 0, keepdims=False) for t in range(seqs)])
    branch_rms = jnp.stack([lax.dynamic_index_in_dim(rms_here, source[t], 0, keepdims=False) for t in range(seqs)])

    scatter = lambda whole: lax.psum_scatter(whole, BOTH, scatter_dimension=0, tiled=True)
    grads = [dqv[0], dqv[2], dvec[0], dvec[1], dvec[2], dvec[3], dvec[4], dvec[5]]
    packed = jnp.concatenate([vector.reshape(devices, per) for vector in grads] + [dbu.reshape(devices, -1)], axis=1)
    packed = lax.psum_scatter(packed, BOTH, scatter_dimension=0, tiled=True)[0]
    shard = [packed[place * per : (place + 1) * per] for place in range(8)]
    return (
        layer_out, input_grad, scatter(dw_qkv).astype(f32), shard[0], shard[1], scatter(dw_out).astype(f32), shard[2],
        shard[3], shard[4], scatter(dw_up).astype(f32), packed[8 * per :], scatter(dw_down).astype(f32), shard[5],
        shard[6], shard[7], branch_rms,
    )


def solution(mesh):
    rows3, rows2, rows1 = P(BOTH, None, None), P(BOTH, None), P(BOTH)
    in_specs = (
        rows3, P(), P(), rows2, rows1, rows1, rows2, rows1, rows1, rows1, rows2, rows1, rows2, rows1, rows1, rows1, rows3,
    )
    out_specs = (
        rows3, rows3, rows2, rows1, rows1, rows2, rows1, rows1, rows1, rows2, rows1, rows2, rows1, rows1, rows1, rows2,
    )
    return jax.shard_map(body, mesh=mesh, in_specs=in_specs, out_specs=out_specs, check_vma=False)
```

time: 1330 us -> 844 us (0.63)
  matrix products: 621 us -> 0 us
  Pallas kernels: 0 us -> 281 us
  other arithmetic: 161 us -> 16.6 us
  local copies, waits for them, and re-layouts: 94.4 us -> 11.4 us
  waiting for transfers between devices: 202 us -> 267 us
  blocking collectives: 206 us -> 226 us
    dot_general x52 -> x0, matrix products: 621 us -> none  [the longest x8 120 us: lower_dot(): return jnp.dot(left, right, preferred_element_type=jnp.float32)]
    pallas_call x0 -> x3, Pallas kernels: none -> 281 us  [the longest x1 114 us: attention_backward(): pl.pallas_call(backward_kernel, out_shape=(jax.ShapeDtypeStruct((seqs, ro...]
    convert_element_type x14 -> x4, other arithmetic: 94 us -> 6.3 us  [the longest x1 1.64 us: body(): scatter(dw_down).astype(f32)]
    all_gather x4, waiting for transfers between devices: 0.05 us -> 64.4 us  [body(): gather = lambda shard: lax.all_gather(shard, BOTH, axis=0, tiled=True)]
    reduce_sum x18 -> x3, other arithmetic: 57.5 us -> 0.36 us  [the longest x1 0.18 us: body(): source = jnp.sum(jnp.where(matches, places[None, :], 0), axis=1) // seqs]
    unnamed x323 -> x32, local copies, waits for them, and re-layouts: 55.3 us -> 0.33 us
    slice x14 -> x7, local copies, waits for them, and re-layouts: 23.1 us -> 2.84 us  [the longest x1 0.84 us: body(): dqv[2]]
    unnamed x2, blocking collectives: 206 us -> 220 us
  transfers between devices with their start and end apart: 10 -> 10, of which waited for: 2 -> 3; matrix products, arithmetic and copies ran while one was open for 47% -> 3% of each run, Pallas kernels for 0% -> 21%
where the time goes in v1:
time: 844 us; the launch traced here: 832 us
  Pallas kernels  281 us (33%)
  waiting for transfers between devices  267 us (32%)
  blocking collectives  226 us (27%)
  between operations  18.6 us (2%)
  other arithmetic  16.6 us (2%)
  local copies, waits for them, and re-layouts  11.4 us (1%)
  starting transfers between devices  11.1 us (1%)
    unnamed x2, blocking collectives  220 us
    reduce_scatter x4, waiting for transfers between devices, body(): lax.psum_scatter(whole, BOTH, scatter_dimension=0, tiled=True)  199 us
    pallas_call x1, Pallas kernels, attention_backward(): pl.pallas_call(backward_kernel, out_shape=(jax.ShapeDtypeStruct((seqs, ro...  114 us
    pallas_call x1, Pallas kernels, middle(): pl.pallas_call(middle_kernel, out_shape=(jax.ShapeDtypeStruct((slots, row...  108 us
    all_gather x4, waiting for transfers between devices, body(): gather = lambda shard: lax.all_gather(shard, BOTH, axis=0, tiled=True)  64.4 us
    pallas_call x1, Pallas kernels, attention_forward(): pl.pallas_call(forward_kernel, out_shape=(jax.ShapeDtypeStruct((seqs, 3 *...  59.8 us
  transfers between devices with their start and end apart: 10, of which 3 were waited for; matrix products, arithmetic and copies ran while one was open for 3% of the time, Pallas kernels for 21%

profile of v1, /device:TPU:0, one launch (start us, length us, event | category | flops | bytes accessed | tf_op | source)
XLA Modules:
  0.0 832.1 jit_solution(16613953916209168651)
XLA Ops:
  7.2 0.7 all-gather.6.cloned.1.call-update
  8.0 0.7 all-gather.8.cloned.1.call-update
  8.7 0.7 all-gather.10.cloned.1.call-update
  9.4 0.5 all-gather.12.cloned.1.call-update
  10.0 0.7 dynamic-slice_subtract_fusion
  10.7 0.2 fusion
  10.9 0.6 fusion.4
  11.5 0.6 iota_compare_fusion.1
  12.2 2.1 slice_bitcast_fusion.1
  14.3 3.4 broadcast_select_fusion
  17.7 5.4 all-to-all-start
  23.3 0.1 concatenate.18
  23.4 0.2 dynamic-update-slice
  23.6 116.0 %all-reduce = bf16[9216]{0:T(1024)(128)(2,1)S(1)} all-reduce(bf16[9216]{0:T(1024)(128)(2,1)S(1)} %dynamic-update-slice), channel_id=2, replica_groups=mesh['dp'=8,'fsdp'=4] {'dp','fsdp'}, use_global_device_ids=true, to_apply=%add | all-reduce | flops 9216 | bytes 36864
  139.6 0.1 reshape.134
  140.0 0.1 reshape.124
  140.4 0.1 reshape.126
  140.9 0.7 reshape.131.bu_ref
  141.6 0.6 concatenate.22.vec_ref
  142.2 0.6 and_select_fusion.1.in_slot.out_slot
  142.8 0.6 convert_multiply_fusion
  143.4 0.7 maximum_maximum_fusion.bias_ref
  144.1 59.8 %attention_forward.1 = (bf16[2,18,1024,128]{3,2,1,0:T(8,128)(2,1)}, bf16[2,1024,768]{2,1,0:T(8,128)(2,1)}, f32[2,6,1024,128]{3,2,1,0:T(8,128)}) custom-call(s32[2]{0:T(128)} %get-tuple-element.55.len_ref, bf16[2,1024,768]{2,1,0:T(8,128)(2,1)} %x_ref.5, bf16[768,2304]{1,0:T(8,128)(2,1)} %all-gather.6.cloned.1.call-done.w_ref, ...), custom_call_target="tpu_custom_call" | custom-call | flops 60000002048 | bytes 30000000 | tf_op jit(solution)/shard_map/attention_forward/pallas_call | solution.py:90
  203.9 64.3 %all-gather.12.cloned.1.call-done.wd_ref = bf16[3072,768]{1,0:T(8,128)(2,1)} async-done(((bf16[96,768]{1,0:T(8,128)(2,1)}), bf16[3072,768]{1,0:T(8,128)(2,1)}) %all-gather.12.cloned.1.call-update) | async-done | bytes 4718608 | tf_op jit(solution)/shard_map/all_gather | solution.py:463
  268.3 107.7 %middle.1 = (bf16[4,1024,768]{2,1,0:T(8,128)(2,1)}, f32[2,1024,768]{2,1,0:T(8,128)}, bf16[2,1024,768]{2,1,0:T(8,128)(2,1)}, bf16[768,768]{1,0:T(8,128)(2,1)}, bf...) custom-call(s32[2]{0:T(128)} %get-tuple-element.55.len_ref, ...), custom_call_target="tpu_custom_call" | custom-call | flops 86973087744 | bytes 60000000 | tf_op jit(solution)/shard_map/middle/pallas_call | solution.py:249
  376.1 113.5 %attention_backward.1 = (bf16[2,1024,768]{2,1,0:T(8,128)(2,1)}, bf16[768,2304]{1,0:T(8,128)(2,1)}, f32[8,768]{1,0:T(8,128)}) custom-call(s32[2]{0:T(128)} %get-tuple-element.55.len_ref, bf16[2,1024,768]{2,1,0:T(8,128)(2,1)} %x_ref.5, bf16[2,3,6,1024,128]{4,3,2,1,0:T(8,128)(2,1)} %bitcast.32, bf16[2,1024,768]{2,1,0:T(8,128)(2,1)} %get-tuple-element.31.ctx_ref, ...), custom_call_target="tpu_custom_call" | custom-call | flops 120000004096 | bytes 40000000 | tf_op jit(solution)/shard_map/attention_backward/pallas_call | solution.py:397
  489.7 0.7 reduce-scatter.9.cloned.1.call-update
  490.5 0.7 reduce-scatter.11.cloned.1.call-update
  491.4 0.1 copy.36
  491.6 0.1 copy.38
  491.7 6.1 all_to_all.19
  497.8 5.4 all-to-all-start.1
  507.1 0.8 slice_reduce_fusion.7
  508.7 0.5 broadcast.72
  509.2 0.7 reduce.19
  510.0 0.1 concatenate.23
  510.1 104.1 %all-reduce.1 = f32[32,288]{1,0:T(8,128)S(1)} all-reduce(f32[32,288]{1,0:T(8,128)S(1)} %concatenate.23), channel_id=4, replica_groups=mesh['dp'=8,'fsdp'=4] {'dp','fsdp'}, use_global_device_ids=true, to_apply=%region_2.3.clone | all-reduce | flops 9216 | bytes 73728
  614.2 0.6 dynamic-slice_bitcast_fusion.3
  614.8 0.6 dynamic-slice_bitcast_fusion
  615.4 0.6 pad_maximum_fusion.1
  616.0 1.4 convert_element_type.16
  617.4 1.6 convert_element_type.15
  619.0 2.2 constant_dynamic-slice_fusion.3
  621.2 1.9 pad_maximum_fusion
  623.1 87.8 %reduce-scatter.9.cloned.1.call-done = bf16[24,3072]{1,0:T(8,128)(2,1)} async-done(((bf16[768,3072]{1,0:T(8,128)(2,1)}), bf16[24,3072]{1,0:T(8,128)(2,1)}) %reduce-scatter.9.cloned.1.call-update) | async-done | bytes 147472 | tf_op jit(solution)/shard_map/reduce_scatter | solution.py:489
  710.9 1.6 convert_element_type.17
  712.5 110.9 %reduce-scatter.11.cloned.1.call-done = bf16[96,768]{1,0:T(8,128)(2,1)} async-done(((bf16[3072,768]{1,0:T(8,128)(2,1)}), bf16[96,768]{1,0:T(8,128)(2,1)}) %reduce-scatter.11.cloned.1.call-update) | async-done | bytes 147472 | tf_op jit(solution)/shard_map/reduce_scatter | solution.py:489
  823.4 1.6 convert_element_type.18
  (77 shorter events, 2.4 us)
Async XLA Ops:
  7.2 136.9 %all-gather.6.cloned.1.call-start = ((), (), s32[]{:S(2)}) async-start(), calls=%async_computation.7 | async-start | bytes 3649536 | tf_op jit(solution)/shard_map/all_gather | solution.py:463
  7.9 196.0 %all-gather.8.cloned.1.call-start = ((), (), s32[]{:S(2)}) async-start(), calls=%async_computation.8 | async-start | bytes 1216512 | tf_op jit(solution)/shard_map/all_gather | solution.py:463
  8.7 195.3 %all-gather.10.cloned.1.call-start = ((), (), s32[]{:S(2)}) async-start(), calls=%async_computation.9 | async-start | bytes 4866048 | tf_op jit(solution)/shard_map/all_gather | solution.py:463
  9.4 258.9 %all-gather.12.cloned.1.call-start = ((), (), s32[]{:S(2)}) async-start(), calls=%async_computation.10 | async-start | bytes 4866048 | tf_op jit(solution)/shard_map/all_gather | solution.py:463
  17.6 5.6 copy-start.5
  17.6 5.6 copy-start.6
  17.6 5.6 copy-start.7
  17.6 5.6 copy-start.8
  17.6 5.6 copy-start.9
  17.7 5.6 copy-start.10
  17.7 5.6 copy-start.11
  17.7 5.6 copy-start.12
  17.7 5.6 copy-start.13
  17.7 125.1 %copy-start.4 = (s32[64]{0:T(128)S(1)}, s32[64]{0:T(128)}, u32[]{:S(2)}) copy-start(s32[64]{0:T(128)} %param.18) | copy-start | bytes 772
  17.7 186.2 %all-to-all-start = ((bf16[4,1024,768]{2,1,0:T(8,128)(2,1)}), bf16[4,1024,768]{2,1,0:T(8,128)(2,1)}, u32[]{:S(2)}, u32[]{:S(2)}) async-start(bf16[4,1024,768]{2,1,0:T(8,128)(2,1)} %broadcast_select_fusion), calls=%async_computation | async-start | bytes 12582912 | tf_op jit(solution)/shard_map/all_to_all | solution.py:461
  23.1 592.8 %reduce-scatter.7.cloned.1.call-start = ((), (), s32[]{:S(2)}) async-start(), calls=%async_computation.12 | async-start | bytes 1216512 | tf_op jit(solution)/shard_map/reduce_scatter | solution.py:489
  376.0 241.4 %reduce-scatter.5.cloned.1.call-start = ((), (), s32[]{:S(2)}) async-start(), calls=%async_computation.11 | async-start | bytes 3649536 | tf_op jit(solution)/shard_map/reduce_scatter | solution.py:489
  489.6 221.3 %reduce-scatter.9.cloned.1.call-start = ((), (), s32[]{:S(2)}) async-start(), calls=%async_computation.13 | async-start | bytes 4866048 | tf_op jit(solution)/shard_map/reduce_scatter | solution.py:489
  490.4 0.8 copy-start.14
  490.4 0.9 copy-start.1
  490.4 0.9 copy-start.3
  490.4 333.0 %reduce-scatter.11.cloned.1.call-start = ((), (), s32[]{:S(2)}) async-start(), calls=%async_computation.14 | async-start | bytes 4866048 | tf_op jit(solution)/shard_map/reduce_scatter | solution.py:489
  497.8 10.3 %copy-start = (f32[8,768]{1,0:T(8,128)S(1)}, f32[8,768]{1,0:T(8,128)}, u32[]{:S(2)}) copy-start(f32[8,768]{1,0:T(8,128)} %get-tuple-element.40) | copy-start | bytes 73732
  497.8 11.4 %copy-start.2 = (f32[1,3072]{1,0:T(1,128)S(1)}, f32[1,3072]{1,0:T(1,128)}, u32[]{:S(2)}) copy-start(f32[1,3072]{1,0:T(1,128)} %get-tuple-element.41) | copy-start | bytes 36868
  497.8 121.2 %all-to-all-start.1 = ((bf16[4,1024,768]{2,1,0:T(8,128)(2,1)}), bf16[4,1024,768]{2,1,0:T(8,128)(2,1)}, u32[]{:S(2)}, u32[]{:S(2)}) async-start(bf16[4,1024,768]{2,1,0:T(8,128)(2,1)} %get-tuple-element.32), calls=%async_computation.1 | async-start | bytes 12582912 | tf_op jit(solution)/shard_map/all_to_all | solution.py:485
Sparse Core Ops, SparseCore 0:
  10.9 70.7 all-gather.5
  84.6 52.8 all-gather.7
  140.4 62.5 all-gather.9
  205.8 62.4 all-gather.11
  376.1 95.0 reduce-scatter.6
  489.7 109.7 reduce-scatter.4
  605.0 105.8 reduce-scatter.8
  717.3 106.0 reduce-scatter.10

commit v2 on v1

--- a/solution.py
+++ b/solution.py
@@ -19,6 +19,7 @@
 norm_eps = 1e-05
 masked_fill = -1e30
 BOTH = ("dp", "fsdp")
+MESH = pl.DeviceIdType.MESH
 
 
 def nn(left, right):
@@ -54,7 +55,7 @@
                 cols = slice(part * width, (part + 1) * width)
                 projected = nn(tokens, w_ref[:, cols])
                 if part != 1:
-                    projected = projected + bias_ref[part : part + 1, :].astype(f32)
+                    projected = projected + bias_ref[part // 2 : part // 2 + 1, :].astype(f32)
                 projected = projected.astype(bf16)
                 if part == 0:
                     projected = projected * jnp.asarray(1.0 / math.sqrt(HEAD_DIM), bf16)
@@ -133,28 +134,29 @@
 
 
 def middle_kernel(
-    len_ref, in_slot, out_slot, x_ref, ctx_ref, cot_ref, wo_ref, wu_ref, wd_ref, vec_ref, bu_ref,
-    out_ref, gres_ref, gctx_ref, dwo_ref, dwu_ref, dwd_ref, dvec_ref, dbu_ref, sums_ref,
-    acc_o, acc_u, acc_d, active, slope, stage, sems,
+    len_ref, in_slot, out_slot, x_ref, ctx_ref, cot_ref, w_ref, vec_ref, bu_ref,
+    out_ref, gres_ref, gctx_ref, dw_ref, dvec_ref, dbu_ref, rms_ref,
+    acc, active, slope, sums, stage, sems,
 ):
     seq, index = pl.program_id(0), pl.program_id(1)
     first = jnp.logical_and(seq == 0, index == 0)
     final = jnp.logical_and(seq == pl.num_programs(0) - 1, index == pl.num_programs(1) - 1)
     length = len_ref[seq]
     width = x_ref.shape[2]
-    chunks = wd_ref.shape[0] // width
+    chunks = bu_ref.shape[1] // width
+    tile = lambda place: slice(place * width, (place + 1) * width)
+    up = lambda chunk: tile(1 + chunk)
+    down = lambda chunk: tile(1 + chunks + chunk)
 
     @pl.when(first)
     def _():
-        acc_o[...] = jnp.zeros_like(acc_o)
-        acc_u[...] = jnp.zeros_like(acc_u)
-        acc_d[...] = jnp.zeros_like(acc_d)
+        acc[...] = jnp.zeros_like(acc)
         dvec_ref[...] = jnp.zeros_like(dvec_ref)
         dbu_ref[...] = jnp.zeros_like(dbu_ref)
 
     @pl.when(index == 0)
     def _():
-        sums_ref[...] = jnp.zeros_like(sums_ref)
+        sums[...] = jnp.zeros_like(sums)
 
     @pl.when(index * BLOCK >= length)
     def _():
@@ -163,11 +165,11 @@
     @pl.when(index * BLOCK < length)
     def _():
         vec = lambda place: vec_ref[place : place + 1, :].astype(f32)
-        bias_out, gain_a, shift_a, bias_down, gain_f, shift_f = (vec(place) for place in range(6))
+        bias_out, gain_a, shift_a, bias_down, gain_f, shift_f = (vec(place) for place in range(2, 8))
         valid = (lax.broadcasted_iota(jnp.int32, (BLOCK, 1), 0) + index * BLOCK < length).astype(f32)
         tokens = x_ref[0].astype(f32)
         context = ctx_ref[0]
-        branch_a = nn(context, wo_ref[...]) + bias_out
+        branch_a = nn(context, w_ref[:, tile(0)]) + bias_out
         mixed = tokens + branch_a
         center = mixed - row_mean(mixed)
         scale_a = lax.rsqrt(row_mean(center * center) + norm_eps)
@@ -176,13 +178,13 @@
         hidden_low = hidden.astype(bf16)
         branch_f = bias_down
         for chunk in range(chunks):
-            cols = slice(chunk * width, (chunk + 1) * width)
-            gate = nn(hidden_low, wu_ref[:, cols]) + bu_ref[:, cols].astype(f32)
+            cols = tile(chunk)
+            gate = nn(hidden_low, w_ref[:, up(chunk)]) + bu_ref[:, cols].astype(f32)
             share, bell = normal_tail(gate)
             act = (gate * share).astype(bf16)
             active[:, cols] = act
             slope[:, cols] = share + gate * bell * (1.0 / math.sqrt(2.0 * math.pi))
-            branch_f = branch_f + nn(act, wd_ref[cols, :])
+            branch_f = branch_f + nn(act, w_ref[:, down(chunk)])
         mixed_f = hidden + branch_f
         center = mixed_f - row_mean(mixed_f)
         scale_f = lax.rsqrt(row_mean(center * center) + norm_eps)
@@ -194,70 +196,67 @@
         g_ffn = g_res2.astype(bf16)
         g_hidden = g_res2
         for chunk in range(chunks):
-            cols = slice(chunk * width, (chunk + 1) * width)
-            g_gate = nt(g_ffn, wd_ref[cols, :]) * slope[:, cols]
+            cols = tile(chunk)
+            g_gate = nt(g_ffn, w_ref[:, down(chunk)]) * slope[:, cols]
             g_low = g_gate.astype(bf16)
-            acc_d[cols, :] += tn(active[:, cols], g_ffn)
-            acc_u[:, cols] += tn(hidden_low, g_low)
+            acc[:, down(chunk)] += tn(active[:, cols], g_ffn)
+            acc[:, up(chunk)] += tn(hidden_low, g_low)
             dbu_ref[:, cols] += jnp.sum(g_low.astype(f32), axis=0, keepdims=True)
-            g_hidden = g_hidden + nt(g_low, wu_ref[:, cols])
+            g_hidden = g_hidden + nt(g_low, w_ref[:, up(chunk)])
         g_hat = g_hidden * gain_a
         g_res1 = scale_a * (g_hat - row_mean(g_hat) - hat_a * row_mean(g_hat * hat_a))
         g_attn = g_res1.astype(bf16)
         gres_ref[0] = g_res1
-        gctx_ref[0] = nt(g_attn, wo_ref[...]).astype(bf16)
-        acc_o[...] += tn(context, g_attn)
+        gctx_ref[0] = nt(g_attn, w_ref[:, tile(0)]).astype(bf16)
+        acc[:, tile(0)] += tn(context, g_attn)
         column = lambda values: jnp.sum(values, axis=0, keepdims=True)
-        dvec_ref[0:1, :] += column(g_attn.astype(f32))
-        dvec_ref[1:2, :] += column(g_hidden * hat_a)
-        dvec_ref[2:3, :] += column(g_hidden)
-        dvec_ref[3:4, :] += column(g_ffn.astype(f32))
-        dvec_ref[4:5, :] += column(g_result * hat_f)
-        dvec_ref[5:6, :] += column(g_result)
-        sums_ref[0, 0:1, :] += column(tokens * tokens * valid)
-        sums_ref[0, 1:2, :] += column(branch_a * branch_a * valid)
-        sums_ref[0, 2:3, :] += column(branch_f * branch_f * valid)
+        dvec_ref[2:3, :] += column(g_attn.astype(f32))
+        dvec_ref[3:4, :] += column(g_hidden * hat_a)
+        dvec_ref[4:5, :] += column(g_hidden)
+        dvec_ref[5:6, :] += column(g_ffn.astype(f32))
+        dvec_ref[6:7, :] += column(g_result * hat_f)
+        dvec_ref[7:8, :] += column(g_result)
+        sums[0:1, :] += column(tokens * tokens * valid)
+        sums[1:2, :] += column(branch_a * branch_a * valid)
+        sums[2:3, :] += column(branch_f * branch_f * valid)
+
+    @pl.when(index == pl.num_programs(1) - 1)
+    def _():
+        mean = jnp.sum(sums[...], axis=1, keepdims=True) / (length * width).astype(f32)
+        rms_ref[0] = jnp.broadcast_to(jnp.sqrt(mean), rms_ref.shape[1:])
 
     @pl.when(final)
     def _():
-        pieces = [(acc_o, dwo_ref, slice(None), slice(None))]
-        for chunk in range(chunks):
-            cols = slice(chunk * width, (chunk + 1) * width)
-            pieces.append((acc_u, dwu_ref, slice(None), cols))
-            pieces.append((acc_d, dwd_ref, cols, slice(None)))
         copies = []
-        for place, (acc, out, rows, cols) in enumerate(pieces):
+        for place in range(1 + 2 * chunks):
             slot = place % 2
             if place >= 2:
                 copies[place - 2].wait()
-            stage[slot] = acc[rows, cols].astype(bf16)
-            copies.append(pltpu.make_async_copy(stage.at[slot], out.at[rows, cols], sems.at[slot]))
+            stage[slot] = acc[:, tile(place)].astype(bf16)
+            copies.append(pltpu.make_async_copy(stage.at[slot], dw_ref.at[:, tile(place)], sems.at[slot]))
             copies[-1].start()
         copies[-2].wait()
         copies[-1].wait()
 
 
-def middle(lengths, in_slot, out_slot, tokens, context, cots, w_out, w_up, w_down, vectors, bias_up):
+def middle(lengths, in_slot, out_slot, tokens, context, cots, weights, vectors, bias_up):
     seqs, rows, width = tokens.shape
     slots = cots.shape[0]
-    hidden = w_up.shape[1]
+    hidden = bias_up.shape[1]
     whole = lambda shape: pl.BlockSpec(shape, lambda s, i, *_: (0,) * len(shape), pipeline_mode=pl.Buffered(1))
     inside = lambda s, i, lens: jnp.minimum(i, block_count(lens[s]) - 1)
     here = pl.BlockSpec((1, BLOCK, width), lambda s, i, lens, a, b: (s, inside(s, i, lens), 0))
-    kept = pl.BlockSpec((1, BLOCK, width), lambda s, i, lens, a, b: (s, inside(s, i, lens), 0))
-    total = 2 * seqs * rows * (2 * width * width + 4 * width * hidden) * 2
+    flops = 6 * seqs * rows * (width * width + 2 * width * hidden)
     return pl.pallas_call(
         middle_kernel,
         out_shape=(
             jax.ShapeDtypeStruct((slots, rows, width), bf16),
             jax.ShapeDtypeStruct((seqs, rows, width), f32),
             jax.ShapeDtypeStruct((seqs, rows, width), bf16),
-            jax.ShapeDtypeStruct(w_out.shape, bf16),
-            jax.ShapeDtypeStruct(w_up.shape, bf16),
-            jax.ShapeDtypeStruct(w_down.shape, bf16),
+            jax.ShapeDtypeStruct(weights.shape, bf16),
             jax.ShapeDtypeStruct((8, width), f32),
             jax.ShapeDtypeStruct((1, hidden), f32),
-            jax.ShapeDtypeStruct((seqs, 8, width), f32),
+            jax.ShapeDtypeStruct((seqs, 8, 128), f32),
         ),
         grid_spec=pltpu.PrefetchScalarGridSpec(
             num_scalar_prefetch=3,
@@ -266,37 +265,32 @@
                 here,
                 here,
                 pl.BlockSpec((1, BLOCK, width), lambda s, i, lens, a, b: (a[s], inside(s, i, lens), 0)),
-                whole(w_out.shape),
-                whole(w_up.shape),
-                whole(w_down.shape),
+                whole(weights.shape),
                 whole(vectors.shape),
                 whole(bias_up.shape),
             ],
             out_specs=[
                 pl.BlockSpec((1, BLOCK, width), lambda s, i, lens, a, b: (b[s], i, 0)),
-                kept,
-                kept,
-                pl.BlockSpec(memory_space=pl.ANY),
-                pl.BlockSpec(memory_space=pl.ANY),
+                here,
+                here,
                 pl.BlockSpec(memory_space=pl.ANY),
                 whole((8, width)),
                 whole((1, hidden)),
-                pl.BlockSpec((1, 8, width), lambda s, i, *_: (s, 0, 0)),
+                pl.BlockSpec((1, 8, 128), lambda s, i, *_: (s, 0, 0)),
             ],
             scratch_shapes=[
-                pltpu.VMEM(w_out.shape, f32),
-                pltpu.VMEM(w_up.shape, f32),
-                pltpu.VMEM(w_down.shape, f32),
+                pltpu.VMEM(weights.shape, f32),
                 pltpu.VMEM((BLOCK, hidden), bf16),
                 pltpu.VMEM((BLOCK, hidden), f32),
+                pltpu.VMEM((8, width), f32),
                 pltpu.VMEM((2, width, width), bf16),
                 pltpu.SemaphoreType.DMA((2,)),
             ],
         ),
         compiler_params=pltpu.CompilerParams(vmem_limit_bytes=60 << 20),
-        cost_estimate=pl.CostEstimate(flops=total, transcendentals=seqs * rows * hidden, bytes_accessed=60_000_000),
+        cost_estimate=pl.CostEstimate(flops=flops, transcendentals=seqs * rows * hidden, bytes_accessed=60_000_000),
         name="middle",
-    )(lengths, in_slot, out_slot, tokens, context, cots, w_out, w_up, w_down, vectors, bias_up)
+    )(lengths, in_slot, out_slot, tokens, context, cots, weights, vectors, bias_up)
 
 
 def backward_kernel(
@@ -371,7 +365,8 @@
                     piece = jnp.concatenate([mixed[part * PAIRS + head, rows, :] for head in range(PAIRS)], axis=1)
                     g_in = g_in + nt(piece, w_ref[:, cols])
                     acc_w[:, cols] += tn(tokens, piece)
-                    dvec_ref[part : part + 1, :] += jnp.sum(piece.astype(f32), axis=0, keepdims=True)
+                    if part != 1:
+                        dvec_ref[part // 2 : part // 2 + 1, :] += jnp.sum(piece.astype(f32), axis=0, keepdims=True)
                 gin_ref[0, rows, :] = g_in.astype(bf16)
 
     @pl.when(jnp.logical_and(seq == pl.num_programs(0) - 1, pair == PAIRS - 1))
@@ -435,13 +430,301 @@
     )(lengths, tokens, qkv.reshape(seqs, 3, PAIRS, rows, PAIR), context, g_context, lse, g_res1, w_qkv)
 
 
+def mesh_axes(dp, fsdp):
+    if (dp, fsdp) == (8, 4):
+        return (("dp", 2, 4), ("dp", 1, 2), ("fsdp", 2, 2), ("fsdp", 1, 2))
+    return None
+
+
+class Place:
+    def __init__(self, axes):
+        self.axes = axes
+        self.at = {name: lax.axis_index(name) for name in BOTH}
+        self.own = [lax.rem(self.at[name] // stride, size) for name, stride, size in axes]
+
+    def shifted(self, dim, step):
+        size = self.axes[dim][2]
+        return lax.rem(self.own[dim] + step + size, size)
+
+    def device(self, dim, step):
+        name, stride, _ = self.axes[dim]
+        moved = self.at[name] + (self.shifted(dim, step) - self.own[dim]) * stride
+        return tuple(moved if name == axis else self.at[axis] for axis in BOTH)
+
+    def steps(self, dim):
+        return range(1, self.axes[dim][2])
+
+
+def meet(place, others=()):
+    barrier = pltpu.get_barrier_semaphore()
+    peers = [place.device(dim, step) for dim in range(len(place.axes)) for step in place.steps(dim)] + list(others)
+    for peer in peers:
+        pl.semaphore_signal(barrier, inc=1, device_id=peer, device_id_type=MESH)
+    pl.semaphore_wait(barrier, len(peers))
+
+
+def gather_kernel(axes, parts, waves, count, *refs):
+    shards, outs = refs[:count], refs[count : 2 * count]
+    send, recv, core_send, core_recv, local = refs[2 * count :]
+    place = Place(axes)
+    own = place.own
+    core = len(axes) - 1
+    meet(place)
+    mine = [pltpu.make_async_copy(shards[i], outs[i].at[tuple(own)], local.at[i]) for i in range(count)]
+    for copy in mine:
+        copy.start()
+    sent, crossed = [], []
+    spots = [list(own) for _ in parts]
+    arriving = [[] for _ in parts]
+    pieces = [0] * len(parts)
+    used = [0] * len(parts)
+
+    def cross(number, spot, source=None):
+        array, cols, _ = parts[number]
+        there = outs[array].at[tuple(spot) + (slice(None), cols)]
+        copy = pltpu.make_async_remote_copy(
+            there if source is None else source,
+            there,
+            core_send.at[number, pieces[number]],
+            core_recv.at[number, pieces[number]],
+            device_id=place.device(core, 1),
+            device_id_type=MESH,
+        )
+        pieces[number] += 1
+        copy.start()
+        sent.append(copy)
+        crossed.append(copy)
+
+    stages = core
+    waiting = list(mine)
+    for time in range(max(waves) + stages + 1):
+        for number, (array, cols, order) in enumerate(parts):
+            stage = time - waves[number]
+            if not 0 <= stage <= stages:
+                continue
+            spot = spots[number]
+            fresh = []
+            if stage == 0:
+                source = shards[array].at[:, cols]
+            else:
+                while waiting:
+                    waiting.pop().wait()
+                dim = order[stage - 1]
+                for step, copy in enumerate(arriving[number], 1):
+                    copy.wait_recv()
+                    fresh.append(spot[:dim] + [place.shifted(dim, -step)] + spot[dim + 1 :])
+                spot[dim] = slice(None)
+                source = outs[array].at[tuple(spot) + (slice(None), cols)]
+            if stage < stages:
+                dim = order[stage]
+                arriving[number] = []
+                for step in place.steps(dim):
+                    copy = pltpu.make_async_remote_copy(
+                        source,
+                        outs[array].at[tuple(spot) + (slice(None), cols)],
+                        send.at[number, used[number]],
+                        recv.at[number, used[number]],
+                        device_id=place.device(dim, step),
+                        device_id_type=MESH,
+                    )
+                    used[number] += 1
+                    copy.start()
+                    sent.append(copy)
+                    arriving[number].append(copy)
+            if stage == 0:
+                cross(number, own, source)
+            for block in fresh:
+                cross(number, block)
+    for copy in crossed:
+        copy.wait_recv()
+    for copy in sent:
+        copy.wait_send()
+
+
+def gather_blocks(axes, parts, waves, shards):
+    sizes = tuple(size for _, _, size in axes)
+    hops = sum(size - 1 for size in sizes[:-1])
+    count = len(shards)
+    sems = lambda *shape: pltpu.SemaphoreType.DMA(shape)
+    return pl.pallas_call(
+        functools.partial(gather_kernel, axes, parts, waves, count),
+        out_shape=tuple(jax.ShapeDtypeStruct(sizes + shard.shape, shard.dtype) for shard in shards),
+        in_specs=[pl.BlockSpec(memory_space=pl.ANY)] * count,
+        out_specs=tuple([pl.BlockSpec(memory_space=pl.ANY)] * count),
+        scratch_shapes=[
+            sems(len(parts), hops),
+            sems(len(parts), hops),
+            sems(len(parts), hops + 1),
+            sems(len(parts), hops + 1),
+            sems(count),
+        ],
+        compiler_params=pltpu.CompilerParams(collective_id=1, has_side_effects=True),
+        name="gather_blocks",
+    )(*shards)
+
+
+def scatter_kernel(axes, parts, waves, count, *refs):
+    grads, note, outs, notes = refs[:count], refs[count], refs[count + 1 : 2 * count + 1], refs[2 * count + 1]
+    bufs, small, (send, recv, local, note_send, note_recv) = refs[-15:-10], refs[-10:-5], refs[-5:]
+    place = Place(axes)
+    own = place.own
+    depth = axes[0][2]
+    core = len(axes) - 1
+    shards = notes.shape[0]
+    member = place.at["fsdp"]
+    friends = [lax.rem(member + step, shards) for step in range(1, shards)]
+    meet(place, [(place.at["dp"], friend) for friend in friends])
+    sent, told = [], []
+    live = [{} for _ in parts]
+    for step, friend in enumerate(friends):
+        copy = pltpu.make_async_remote_copy(
+            note,
+            notes.at[member],
+            note_send.at[step],
+            note_recv.at[step],
+            device_id=(place.at["dp"], friend),
+            device_id_type=MESH,
+        )
+        copy.start()
+        sent.append(copy)
+        told.append(copy)
+    notes[member] = note[...]
+
+    def buffers(number):
+        if parts[number][1] is None:
+            return small
+        return [buf.at[number] for buf in bufs]
+
+    def push(number, piece, source, target, dim, step):
+        copy = pltpu.make_async_remote_copy(
+            source,
+            target,
+            send.at[number, piece],
+            recv.at[number, piece],
+            device_id=place.device(dim, step),
+            device_id_type=MESH,
+        )
+        copy.start()
+        sent.append(copy)
+        return copy
+
+    def plus(acc, spot, extra):
+        acc[spot] = (acc[spot].astype(f32) + extra.astype(f32)).astype(acc.dtype)
+
+    def advance(number, stage):
+        array, cols, (one, two) = parts[number]
+        acc, from_core, from_one, from_two, from_z = buffers(number)
+        state = live[number]
+        own_one, own_two = own[one], own[two]
+        peer_one, peer_two = place.shifted(one, 1), place.shifted(two, 1)
+
+        def spot(first, second, z):
+            index = [z, None, None]
+            index[one], index[two] = first, second
+            return tuple(index)
+
+        if stage == 0:
+            rows = (slice(None),) * core
+            last = (slice(None), slice(None) if cols is None else cols)
+            state["core"] = push(number, 0, grads[array].at[rows + (place.shifted(core, 1),) + last], from_core, core, 1)
+            state["own"] = pltpu.make_async_copy(grads[array].at[rows + (own[core],) + last], acc, local.at[number])
+            state["own"].start()
+        elif stage == 1:
+            state["own"].wait()
+            state["core"].wait_recv()
+            for first in (peer_one, own_one):
+
+                def both(z, carry, first=first):
+                    for second in range(axes[two][2]):
+                        plus(acc, spot(first, second, z), from_core[spot(first, second, z)])
+                    return carry
+
+                lax.fori_loop(0, depth, both, 0)
+                if first is peer_one:
+                    state["one"] = push(number, 1, acc.at[spot(peer_one, slice(None), slice(None))], from_one, one, 1)
+        elif stage == 2:
+            state["one"].wait_recv()
+            for second in (peer_two, own_two):
+
+                def single(z, carry, second=second):
+                    plus(acc, spot(own_one, second, z), from_one[z, second])
+                    return carry
+
+                lax.fori_loop(0, depth, single, 0)
+                if second is peer_two:
+                    state["two"] = push(number, 2, acc.at[spot(own_one, peer_two, slice(None))], from_two, two, 1)
+        elif stage == 3:
+            state["two"].wait_recv()
+            state["z"] = []
+            for step in list(range(1, depth)) + [0]:
+                z = place.shifted(0, step)
+                plus(acc, spot(own_one, own_two, z), from_two[z])
+                if step:
+                    source = acc.at[spot(own_one, own_two, z)]
+                    state["z"].append(push(number, 2 + step, source, from_z.at[step - 1], 0, step))
+        else:
+            total = acc[spot(own_one, own_two, own[0])].astype(f32)
+            for step, copy in enumerate(state["z"]):
+                copy.wait_recv()
+                total = total + from_z[step].astype(f32)
+            if cols is None:
+                outs[array][...] = total
+            else:
+                outs[array][:, cols] = total
+
+    for time in range(max(waves) + 5):
+        for number in range(len(parts)):
+            if 0 <= time - waves[number] <= 4:
+                advance(number, time - waves[number])
+    for copy in told:
+        copy.wait_recv()
+    for copy in sent:
+        copy.wait_send()
+
+
+def scatter_sums(axes, parts, waves, grads, note):
+    sizes = tuple(size for _, _, size in axes)
+    depth, across, along, _ = sizes
+    blocks = [grad.reshape(sizes + (-1, grad.shape[1])) for grad in grads]
+    tiles = sum(1 for part in parts if part[1] is not None)
+    rows, width = blocks[0].shape[4], parts[0][1].size
+    shards = along * sizes[3]
+    big = lambda *lead: pltpu.VMEM((tiles,) + lead + (rows, width), bf16)
+    tiny = lambda *lead: pltpu.VMEM(lead + blocks[-1].shape[4:], f32)
+    sems = lambda *shape: pltpu.SemaphoreType.DMA(shape)
+    vmem = pl.BlockSpec(memory_space=pltpu.VMEM)
+    leads = ((depth, across, along), (depth, across, along), (depth, 2), (depth,), (depth - 1,))
+    return pl.pallas_call(
+        functools.partial(scatter_kernel, axes, parts, waves, len(grads)),
+        out_shape=tuple(jax.ShapeDtypeStruct(block.shape[4:], f32) for block in blocks)
+        + (jax.ShapeDtypeStruct((shards,) + note.shape, f32),),
+        in_specs=[pl.BlockSpec(memory_space=pl.ANY)] * len(grads) + [vmem],
+        out_specs=tuple([vmem] * (len(grads) + 1)),
+        scratch_shapes=[big(*lead) for lead in leads]
+        + [tiny(*lead) for lead in leads]
+        + [
+            sems(len(parts), 2 + depth),
+            sems(len(parts), 2 + depth),
+            sems(len(parts)),
+            sems(shards - 1),
+            sems(shards - 1),
+        ],
+        compiler_params=pltpu.CompilerParams(collective_id=2, has_side_effects=True, vmem_limit_bytes=56 << 20),
+        name="scatter_sums",
+    )(*blocks, note)
+
+
 def body(
     tokens, lengths, deal_order, qkv_weight, query_bias, value_bias, out_weight, out_bias, attn_gain, attn_shift,
     up_weight, up_bias, down_weight, down_bias, ffn_gain, ffn_shift, cotangent,
 ):
     shards = lax.axis_size("fsdp")
+    axes = mesh_axes(lax.axis_size("dp"), shards)
     devices = lax.axis_size("dp") * shards
     seqs, rows, width = tokens.shape
+    hidden = up_weight.shape[1]
+    chunks = hidden // width
+    per = width // devices
     column = shards * seqs
     base = lax.axis_index("dp") * column
     member = lax.axis_index("fsdp")
@@ -451,50 +734,75 @@
     target = lax.dynamic_slice_in_dim(order, mine, seqs) // seqs
     dealt_here = mine + jnp.arange(seqs, dtype=jnp.int32)
     matches = order[None, :] == dealt_here[:, None]
-    places = jnp.arange(column, dtype=jnp.int32)
-    source = jnp.sum(jnp.where(matches, places[None, :], 0), axis=1) // seqs
+    source = jnp.sum(jnp.where(matches, jnp.arange(column, dtype=jnp.int32)[None, :], 0), axis=1)
     peers = jnp.arange(shards, dtype=jnp.int32)
+
+    up_mixed = up_weight.reshape(per, width, chunks).transpose(0, 2, 1).reshape(per, hidden)
+    rest = jnp.concatenate([out_weight, up_mixed, down_weight.reshape(per, hidden)], axis=1)
+    weights = lax.all_gather(rest, BOTH, axis=0, tiled=True)
 
     outgoing = cotangent[0][None]
     for place in range(1, seqs):
-        outgoing = jnp.where((source[place] == peers)[:, None, None], cotangent[place][None], outgoing)
+        outgoing = jnp.where((source[place] // seqs == peers)[:, None, None], cotangent[place][None], outgoing)
     cots = lax.all_to_all(outgoing, "fsdp", split_axis=0, concat_axis=0, tiled=True)
 
-    gather = lambda shard: lax.all_gather(shard, BOTH, axis=0, tiled=True)
     small = jnp.concatenate(
         [query_bias, value_bias, out_bias, attn_gain, attn_shift, down_bias, ffn_gain, ffn_shift, up_bias]
     )
-    per = width // devices
-    small = lax.all_gather(small, BOTH, axis=0, tiled=False)
-    vectors = [small[:, place * per : (place + 1) * per].reshape(1, width) for place in range(8)]
-    bias_up = small[:, 8 * per :].reshape(1, -1)
-    zero = jnp.zeros((1, width), bf16)
-    qkv_bias = jnp.concatenate([vectors[0], zero, vectors[1]] + [zero] * 5, axis=0)
-    mid_vectors = jnp.concatenate(vectors[2:] + [zero, zero], axis=0)
-    w_qkv, w_out, w_up, w_down = gather(qkv_weight), gather(out_weight), gather(up_weight), gather(down_weight)
-
-    qkv, context, lse = attention_forward(own_lengths, tokens, w_qkv, qkv_bias)
-    results, g_res1, g_context, dw_out, dw_up, dw_down, dvec, dbu, sums = middle(
-        own_lengths, target, target, tokens, context, cots, w_out, w_up, w_down, mid_vectors, bias_up
+    small = jnp.pad(small, (0, 8 * 128 - small.shape[0])).reshape(8, 128)
+    if axes is None:
+        w_qkv = lax.all_gather(qkv_weight, BOTH, axis=0, tiled=True)
+        small = lax.all_gather(small, BOTH, axis=0, tiled=False)
+    else:
+        cut = qkv_weight.shape[1] // 6
+        orders = ((0, 2, 1), (0, 2, 1), (1, 0, 2))
+        parts = [(1, slice(None), orders[0])] + [(0, pl.ds(i * cut, cut), orders[i % 3]) for i in range(6)]
+        w_qkv, small = gather_blocks(axes, parts, [0] * 7, [qkv_weight, small])
+        w_qkv = w_qkv.reshape(width, -1)
+    small = small.reshape(devices, -1)
+    vectors = small[:, : 8 * per].reshape(devices, 8, per).transpose(1, 0, 2).reshape(8, width)
+    bias_up = small[:, 8 * per : 8 * per + chunks * per].reshape(width, chunks).T.reshape(1, hidden)
+
+    qkv, context, lse = attention_forward(own_lengths, tokens, w_qkv, vectors)
+    results, g_res1, g_context, dw_rest, dvec, dbu, rms = middle(
+        own_lengths, target, target, tokens, context, cots, weights, vectors, bias_up
     )
+    arrived = lax.all_to_all(results, "fsdp", split_axis=0, concat_axis=0, tiled=True)
     input_grad, dw_qkv, dqv = attention_backward(own_lengths, tokens, qkv, context, g_context, lse, g_res1, w_qkv)
-
-    rms = jnp.sqrt(jnp.sum(sums[:, :3, :], axis=2) / (own_lengths.astype(f32) * width)[:, None])
-    rms_out = jnp.sum(jnp.where((target[:, None] == peers[None, :])[:, :, None], rms[:, None, :], 0.0), axis=0)
-    rms_here = lax.all_to_all(rms_out, "fsdp", split_axis=0, concat_axis=0, tiled=True)
-    arrived = lax.all_to_all(results, "fsdp", split_axis=0, concat_axis=0, tiled=True)
-    layer_out = jnp.stack([lax.dynamic_index_in_dim(arrived, source[t], 0, keepdims=False) for t in range(seqs)])
-    branch_rms = jnp.stack([lax.dynamic_index_in_dim(rms_here, source[t], 0, keepdims=False) for t in range(seqs)])
-
-    scatter = lambda whole: lax.psum_scatter(whole, BOTH, scatter_dimension=0, tiled=True)
-    grads = [dqv[0], dqv[2], dvec[0], dvec[1], dvec[2], dvec[3], dvec[4], dvec[5]]
-    packed = jnp.concatenate([vector.reshape(devices, per) for vector in grads] + [dbu.reshape(devices, -1)], axis=1)
-    packed = lax.psum_scatter(packed, BOTH, scatter_dimension=0, tiled=True)[0]
-    shard = [packed[place * per : (place + 1) * per] for place in range(8)]
+    layer_out = jnp.stack(
+        [lax.dynamic_index_in_dim(arrived, source[t] // seqs, 0, keepdims=False) for t in range(seqs)]
+    )
+
+    dvec = (dvec + dqv).reshape(8, devices, per).transpose(1, 0, 2).reshape(devices, 8 * per)
+    dbu = dbu.reshape(chunks, devices, per).transpose(1, 2, 0).reshape(devices, chunks * per)
+    packed = jnp.pad(jnp.concatenate([dvec, dbu], axis=1), ((0, 0), (0, 8 * 128 - (8 + chunks) * per)))
+    rms = rms.reshape(seqs * 8, 128)
+    if axes is None:
+        scatter = lambda whole: lax.psum_scatter(whole, BOTH, scatter_dimension=0, tiled=True)
+        qkvw_grad, rest_grad = scatter(dw_qkv).astype(f32), scatter(dw_rest).astype(f32)
+        packed = scatter(packed)
+        rms = lax.all_gather(rms, "fsdp", axis=0, tiled=False)
+    else:
+        parts = [
+            (array, pl.ds(place, width), ((2, 1), (1, 2))[place // width % 2])
+            for array, grad in enumerate((dw_qkv, dw_rest))
+            for place in range(0, grad.shape[1], width)
+        ]
+        waves = [place // 4 for place in range(len(parts))] + [0]
+        parts.append((2, None, (2, 1)))
+        qkvw_grad, rest_grad, packed, rms = scatter_sums(
+            axes, parts, waves, [dw_qkv, dw_rest, packed.reshape(devices * 8, 128)], rms
+        )
+    packed = packed.reshape(-1)
+    vector = [packed[place * per : (place + 1) * per] for place in range(8)]
+    rms = rms.reshape(column, 8, 128)[:, :3, 0]
+    branch_rms = jnp.sum(jnp.where((source[:, None] == jnp.arange(column))[:, :, None], rms[None], 0.0), axis=1)
+    outw_grad = rest_grad[:, :width]
+    upw_grad = rest_grad[:, width : width + hidden].reshape(per, chunks, width).transpose(0, 2, 1).reshape(per, hidden)
+    downw_grad = rest_grad[:, width + hidden :].reshape(per * chunks, width)
     return (
-        layer_out, input_grad, scatter(dw_qkv).astype(f32), shard[0], shard[1], scatter(dw_out).astype(f32), shard[2],
-        shard[3], shard[4], scatter(dw_up).astype(f32), packed[8 * per :], scatter(dw_down).astype(f32), shard[5],
-        shard[6], shard[7], branch_rms,
+        layer_out, input_grad, qkvw_grad, vector[0], vector[1], outw_grad, vector[2], vector[3], vector[4], upw_grad,
+        packed[8 * per : 8 * per + chunks * per], downw_grad, vector[5], vector[6], vector[7], branch_rms,
     )
 
 

time: 844 us -> 562 us (0.67)
  waiting for transfers between devices: 267 us -> 0.03 us
  blocking collectives: 226 us -> 0 us
  Pallas kernels: 281 us -> 440 us
  starting transfers between devices: 11.1 us -> 61.3 us
  local copies, waits for them, and re-layouts: 11.4 us -> 21.6 us
    pallas_call x0 -> x2, Pallas kernels: none -> 287 us  [the longest x1 167 us: scatter_sums(): pl.pallas_call(functools.partial(scatter_kernel, axes, parts, waves, len(...]
    unnamed x2 -> x0, blocking collectives: 220 us -> none
    reduce_scatter x4 -> x0, waiting for transfers between devices: 199 us -> none  [body(): lax.psum_scatter(whole, BOTH, scatter_dimension=0, tiled=True)]
    all_gather x4 -> x1, waiting for transfers between devices: 64.4 us -> 0.01 us  [body(): weights = lax.all_gather(rest, BOTH, axis=0, tiled=True)]
    pallas_call x1, Pallas kernels: 114 us -> 51.9 us  [attention_backward(): pl.pallas_call(backward_kernel, out_shape=(jax.ShapeDtypeStruct((seqs, ro...]
    all_to_all x1, starting transfers between devices: 5.41 us -> 55.9 us  [body(): lax.all_to_all(results, 'fsdp', split_axis=0, concat_axis=0, tiled=True)]
    pallas_call x1, Pallas kernels: 108 us -> 72.5 us  [middle(): pl.pallas_call(middle_kernel, out_shape=(jax.ShapeDtypeStruct((slots, row...]
    pallas_call x1, Pallas kernels: 59.8 us -> 28.8 us  [attention_forward(): pl.pallas_call(forward_kernel, out_shape=(jax.ShapeDtypeStruct((seqs, 3 *...]
  transfers between devices with their start and end apart: 10 -> 3, of which waited for: 3 -> 0; matrix products, arithmetic and copies ran while one was open for 3% -> 4% of each run, Pallas kernels for 21% -> 67%
where the time goes in v2:
time: 562 us; the launch traced here: 553 us
  Pallas kernels  440 us (78%)
  starting transfers between devices  61.3 us (11%)
  local copies, waits for them, and re-layouts  21.6 us (4%)
  between operations  19.9 us (4%)
  other arithmetic  9.83 us (2%)
    pallas_call x1, Pallas kernels, scatter_sums(): pl.pallas_call(functools.partial(scatter_kernel, axes, parts, waves, len(...  167 us
    pallas_call x1, Pallas kernels, gather_blocks(): pl.pallas_call(functools.partial(gather_kernel, axes, parts, waves, count...  120 us
    pallas_call x1, Pallas kernels, middle(): pl.pallas_call(middle_kernel, out_shape=(jax.ShapeDtypeStruct((slots, row...  72.5 us
    all_to_all x1, starting transfers between devices, body(): lax.all_to_all(results, 'fsdp', split_axis=0, concat_axis=0, tiled=True)  55.9 us
    pallas_call x1, Pallas kernels, attention_backward(): pl.pallas_call(backward_kernel, out_shape=(jax.ShapeDtypeStruct((seqs, ro...  51.9 us
    pallas_call x1, Pallas kernels, attention_forward(): pl.pallas_call(forward_kernel, out_shape=(jax.ShapeDtypeStruct((seqs, 3 *...  28.8 us
  transfers between devices with their start and end apart: 3, of which 0 were waited for; matrix products, arithmetic and copies ran while one was open for 4% of the time, Pallas kernels for 67%

profile of v2, /device:TPU:0, one launch (start us, length us, event | category | flops | bytes accessed | tf_op | source)
XLA Modules:
  0.0 552.6 jit_solution(5846481996945834626)
XLA Ops:
  7.2 2.2 copy.51
  9.5 1.6 copy.52
  11.1 1.0 reshape.139
  12.1 1.5 pad_maximum_fusion.1
  13.8 0.2 fusion.1
  13.9 0.6 fusion.4
  17.2 0.2 slice_bitcast_fusion.1
  17.4 3.3 broadcast_select_fusion
  20.8 5.4 all-to-all-start
  26.3 0.1 concatenate.9
  26.4 0.6 pad_bitcast_fusion.refs_1_
  27.0 119.6 %gather_blocks.1 = (bf16[4,2,2,2,24,2304]{5,4,3,2,1,0:T(8,128)(2,1)}, bf16[4,2,2,2,8,128]{5,4,3,2,1,0:T(8,128)(2,1)}) custom-call(bf16[24,2304]{1,0:T(8,128)(2,1)} %refs_0_.1, bf16[8,128]{1,0:T(8,128)(2,1)} %pad_bitcast_fusion.refs_1_), custom_call_target="tpu_custom_call" | custom-call | tf_op jit(solution)/shard_map/gather_blocks/pallas_call | solution.py:549
  146.6 0.9 copy.67
  150.2 0.1 reshape.135
  150.3 0.7 reshape.136.bias_ref.vec_ref
  151.0 0.2 reshape.140
  151.2 0.1 copy.53
  151.3 0.6 copy.64
  152.0 0.6 dynamic_slice.16.len_ref
  152.6 0.6 and_select_fusion.in_slot.out_slot
  153.2 0.6 iota_compare_fusion.1
  153.7 28.8 %attention_forward.1 = (bf16[2,18,1024,128]{3,2,1,0:T(8,128)(2,1)}, bf16[2,1024,768]{2,1,0:T(8,128)(2,1)}, f32[2,6,1024,128]{3,2,1,0:T(8,128)}) custom-call(s32[2]{0:T(128)} %dynamic_slice.16.len_ref, bf16[2,1024,768]{2,1,0:T(8,128)(2,1)} %x_ref.5, bf16[768,2304]{1,0:T(8,128)(2,1)} %bitcast.63, bf16[8,768]{1,0:T(8,128)(2,1)} %reshape.136.bias_ref.vec_ref), custom_call_target="tpu_custom_call" | custom-call | flops 60000002048 | bytes 30000000 | tf_op jit(solution)/shard_map/attention_forward/pallas_call | solution.py:91
  182.6 72.5 %middle.1 = (bf16[4,1024,768]{2,1,0:T(8,128)(2,1)}, f32[2,1024,768]{2,1,0:T(8,128)}, bf16[2,1024,768]{2,1,0:T(8,128)(2,1)}, bf16[768,6912]{1,0:T(8,128)(2,1)}, f...) custom-call(s32[2]{0:T(128)} %dynamic_slice.16.len_ref, s32[2]{0:T(128)} %and_select_fusion.in_slot.out_slot, ...), custom_call_target="tpu_custom_call" | custom-call | flops 65229815808 | bytes 60000000 | tf_op jit(solution)/shard_map/middle/pallas_call | solution.py:250
  255.1 55.9 %all-to-all-start.1 = ((bf16[4,1024,768]{2,1,0:T(8,128)(2,1)}), bf16[4,1024,768]{2,1,0:T(8,128)(2,1)}, u32[]{:S(2)}, u32[]{:S(2)}) async-start(bf16[4,1024,768]{2,1,0:T(8,128)(2,1)} %get-tuple-element.38), calls=%async_computation.1 | async-start | bytes 12582912 | tf_op jit(solution)/shard_map/all_to_all | solution.py:770
  311.0 51.9 %attention_backward.1 = (bf16[2,1024,768]{2,1,0:T(8,128)(2,1)}, bf16[768,2304]{1,0:T(8,128)(2,1)}, f32[8,768]{1,0:T(8,128)}) custom-call(s32[2]{0:T(128)} %dynamic_slice.16.len_ref, bf16[2,1024,768]{2,1,0:T(8,128)(2,1)} %x_ref.5, bf16[2,3,6,1024,128]{4,3,2,1,0:T(8,128)(2,1)} %bitcast.65, bf16[2,1024,768]{2,1,0:T(8,128)(2,1)} %get-tuple-element.37.ctx_ref, ...), custom_call_target="tpu_custom_call" | custom-call | flops 120000004096 | bytes 40000000 | tf_op jit(solution)/shard_map/attention_backward/pallas_call | solution.py:392
  362.9 0.7 add.47
  363.7 0.1 reshape.145
  363.9 0.1 reshape.146
  364.0 0.5 broadcast.51
  364.5 0.7 reduce.3
  365.3 0.1 copy.55
  365.4 0.1 fusion
  365.5 0.7 copy.65
  366.2 167.2 %scatter_sums.1 = (f32[24,2304]{1,0:T(8,128)}, f32[24,6912]{1,0:T(8,128)}, f32[8,128]{1,0:T(8,128)}, f32[4,16,128]{2,1,0:T(8,128)}) custom-call(bf16[4,2,2,2,24,2304]{5,4,3,2,1,0:T(8,128)(2,1)} %bitcast.43, bf16[4,2,2,2,24,6912]{5,4,3,2,1,0:T(8,128)(2,1)} %bitcast.41, f32[4,2,2,2,8,128]{5,4,3,2,1,0:T(8,128)} %bitcast.48, f32[16,128]{1,0:T(8,128)} %bitcast.58), custom_call_target="tpu_custom_call" | custom-call | tf_op jit(solution)/shard_map/scatter_sums/pallas_call | solution.py:697
  533.4 1.5 slice.66
  534.9 1.1 fusion.2
  536.0 0.1 reshape.151
  536.2 0.7 copy.57
  536.9 1.2 copy.59
  538.0 0.8 reshape.153
  538.8 0.1 copy.61
  538.9 0.1 select_reduce_fusion
  539.0 0.7 copy.60
  539.7 0.6 slice.71
  540.3 0.6 fusion.3
  540.9 2.1 constant_dynamic-slice_fusion
  543.0 1.9 pad_maximum_fusion
  544.9 0.7 copy.69
  (52 shorter events, 0.6 us)
Async XLA Ops:
  7.2 6.5 %copy-start.7 = (s32[64]{0:T(128)S(1)}, s32[64]{0:T(128)}, u32[]{:S(2)}) copy-start(s32[64]{0:T(128)} %param.19) | copy-start | bytes 772
  7.2 10.0 %copy-start = (bf16[2,1024,768]{2,1,0:T(8,128)(2,1)S(1)}, bf16[2,1024,768]{2,1,0:T(8,128)(2,1)}, u32[]{:S(2)}) copy-start(bf16[2,1024,768]{2,1,0:T(8,128)(2,1)} %param.33) | copy-start | bytes 9437188
  7.2 175.4 %all-gather.2.cloned.1.call-start = ((), (), s32[]{:S(2)}) async-start(), calls=%async_computation.2 | async-start | bytes 10948608 | tf_op jit(solution)/shard_map/all_gather | solution.py:742
  20.7 5.5 copy-start.8
  20.7 5.5 copy-start.9
  20.7 5.5 copy-start.10
  20.7 5.5 copy-start.11
  20.7 5.5 copy-start.12
  20.7 5.5 copy-start.13
  20.7 5.5 copy-start.14
  20.7 5.5 copy-start.15
  20.8 5.5 copy-start.16
  20.8 131.2 %copy-start.17 = (s32[64]{0:T(128)S(1)}, s32[64]{0:T(128)}, u32[]{:S(2)}) copy-start(s32[64]{0:T(128)} %param.18) | copy-start | bytes 772
  20.8 161.8 %all-to-all-start = ((bf16[4,1024,768]{2,1,0:T(8,128)(2,1)}), bf16[4,1024,768]{2,1,0:T(8,128)(2,1)}, u32[]{:S(2)}, u32[]{:S(2)}) async-start(bf16[4,1024,768]{2,1,0:T(8,128)(2,1)} %broadcast_select_fusion), calls=%async_computation | async-start | bytes 12582912 | tf_op jit(solution)/shard_map/all_to_all | solution.py:747
  255.1 285.8 %all-to-all-start.1 = ((bf16[4,1024,768]{2,1,0:T(8,128)(2,1)}), bf16[4,1024,768]{2,1,0:T(8,128)(2,1)}, u32[]{:S(2)}, u32[]{:S(2)}) async-start(bf16[4,1024,768]{2,1,0:T(8,128)(2,1)} %get-tuple-element.38), calls=%async_computation.1 | async-start | bytes 12582912 | tf_op jit(solution)/shard_map/all_to_all | solution.py:770
  311.0 51.9 %copy-start.2 = (f32[8,768]{1,0:T(8,128)S(1)}, f32[8,768]{1,0:T(8,128)}, u32[]{:S(2)}) copy-start(f32[8,768]{1,0:T(8,128)} %get-tuple-element.46) | copy-start | bytes 73732
  311.0 53.5 %copy-start.3 = (f32[1,3072]{1,0:T(1,128)S(1)}, f32[1,3072]{1,0:T(1,128)}, u32[]{:S(2)}) copy-start(f32[1,3072]{1,0:T(1,128)} %get-tuple-element.48) | copy-start | bytes 36868
  533.4 5.5 copy-start.4
  533.4 5.6 %copy-start.6 = (pred[2,8]{1,0:T(4,128)(4,1)S(1)}, pred[2,8]{1,0:T(4,128)(4,1)}, u32[]{:S(2)}) copy-start(pred[2,8]{1,0:T(4,128)(4,1)} %iota_compare_fusion.1) | copy-start | bytes 52
  533.4 6.3 %copy-start.5 = (f32[8,128]{1,0:T(8,128)S(1)}, f32[8,128]{1,0:T(8,128)}, u32[]{:S(2)}) copy-start(f32[8,128]{1,0:T(8,128)} %get-tuple-element.51) | copy-start | bytes 12292
  543.0 1.9 copy-start.1
Sparse Core Ops, SparseCore 0:
  13.8 122.6 all-gather.1

commit v3 on v1

v3 whole, which is shorter than its diff:
```python
import functools
import math

import jax
import jax.numpy as jnp
from jax import lax
from jax.experimental import pallas as pl
from jax.experimental.pallas import tpu as pltpu
from jax.sharding import PartitionSpec as P

HEADS = 12
HEAD_DIM = 64
PAIR = 2 * HEAD_DIM
PAIRS = HEADS // 2
BLOCK = 256
ROWS = 512
PIECES = 8

f32 = jnp.float32
bf16 = jnp.bfloat16
norm_eps = 1e-05
masked_fill = -1e30
BOTH = ("dp", "fsdp")
MESH = pl.DeviceIdType.MESH


def nn(left, right):
    return lax.dot_general(left, right, (((1,), (0,)), ((), ())), preferred_element_type=f32)


def nt(left, right):
    return lax.dot_general(left, right, (((1,), (1,)), ((), ())), preferred_element_type=f32)


def tn(left, right):
    return lax.dot_general(left, right, (((0,), (0,)), ((), ())), preferred_element_type=f32)


def block_count(length):
    return (length + (BLOCK - 1)) // BLOCK


def whole(shape):
    return pl.BlockSpec(shape, lambda *_: (0,) * len(shape), pipeline_mode=pl.Buffered(1))


def sems(*shape):
    return pltpu.SemaphoreType.DMA(shape)


ANY = pl.BlockSpec(memory_space=pl.ANY)
VMEM = pl.BlockSpec(memory_space=pltpu.VMEM)


def mesh_axes(dp, fsdp):
    if (dp, fsdp) == (8, 4):
        return (("dp", 2, 4), ("dp", 1, 2), ("fsdp", 2, 2), ("fsdp", 1, 2))
    return None


class Place:
    def __init__(self, axes):
        self.axes = axes
        self.core = len(axes) - 1
        self.at = {name: lax.axis_index(name) for name in BOTH}
        self.own = [lax.rem(self.at[name] // stride, size) for name, stride, size in axes]

    def shifted(self, dim, step):
        size = self.axes[dim][2]
        return lax.rem(self.own[dim] + step + size, size)

    def device(self, dim, step):
        name, stride, _ = self.axes[dim]
        moved = self.at[name] + (self.shifted(dim, step) - self.own[dim]) * stride
        return tuple(moved if name == axis else self.at[axis] for axis in BOTH)

    def steps(self, dim):
        return range(1, self.axes[dim][2])

    def friends(self, count):
        member = self.at["fsdp"]
        return [lax.rem(member + step, count) for step in range(1, count)]


def meet(place, friends=()):
    barrier = pltpu.get_barrier_semaphore()
    peers = [place.device(dim, step) for dim in range(len(place.axes)) for step in place.steps(dim)]
    peers += [(place.at["dp"], friend) for friend in friends]
    for peer in peers:
        pl.semaphore_signal(barrier, inc=1, device_id=peer, device_id_type=MESH)
    pl.semaphore_wait(barrier, len(peers))


def push(source, target, send, recv, device):
    return pltpu.make_async_remote_copy(source, target, send, recv, device_id=device, device_id_type=MESH)


class Exchange:
    def __init__(self, place, mine, theirs, pieces, send, recv, local):
        self.place, self.mine, self.theirs, self.pieces = place, mine, theirs, pieces
        self.send, self.recv, self.local = send, recv, local

    def copies(self, piece):
        member = self.place.at["fsdp"]
        height = self.mine.shape[1] // self.pieces
        rows = pl.ds(piece * height, height)
        made = [
            push(
                self.mine.at[friend, rows],
                self.theirs.at[member, rows],
                self.send.at[step, piece],
                self.recv.at[step, piece],
                (self.place.at["dp"], friend),
            )
            for step, friend in enumerate(self.place.friends(self.mine.shape[0]))
        ]
        return made + [pltpu.make_async_copy(self.mine.at[member, rows], self.theirs.at[member, rows], self.local.at[piece])]

    def start(self, piece):
        for copy in self.copies(piece):
            copy.start()

    def wait(self):
        for piece in range(self.pieces):
            for copy in self.copies(piece):
                copy.wait()


def exchange_sems(friends):
    return [sems(friends, PIECES), sems(friends, PIECES), sems(PIECES)]


class Gather:
    def __init__(self, place, parts, shards, outs, send, recv, core_send, core_recv, local):
        self.place, self.parts, self.shards, self.outs = place, parts, shards, outs
        self.sems = send, recv
        self.core_sems = core_send, core_recv
        self.mine = [
            pltpu.make_async_copy(shard, out.at[tuple(place.own)], local.at[i])
            for i, (shard, out) in enumerate(zip(shards, outs))
        ]

    def start(self):
        for copy in self.mine:
            copy.start()

    def local(self):
        for copy in self.mine:
            copy.wait()

    def view(self, number, spot):
        array, cols, _ = self.parts[number]
        return self.outs[array].at[tuple(spot) + (slice(None), cols)]

    def shard(self, number):
        array, cols, _ = self.parts[number]
        return self.shards[array].at[:, cols]

    def known(self, number, stage):
        order = self.parts[number][2]
        return [slice(None) if dim in order[:stage] else own for dim, own in enumerate(self.place.own)]

    def link(self, number, stage):
        order = self.parts[number][2]
        spot = self.known(number, stage)
        source = self.view(number, spot) if stage else self.shard(number)
        first = sum(self.place.axes[dim][2] - 1 for dim in order[:stage])
        send, recv = self.sems
        return [
            push(
                source,
                self.view(number, spot),
                send.at[number, first + step - 1],
                recv.at[number, first + step - 1],
                self.place.device(order[stage], step),
            )
            for step in self.place.steps(order[stage])
        ]

    def across(self, number, stage):
        order = self.parts[number][2]
        core_send, core_recv = self.core_sems
        peer = self.place.device(self.place.core, 1)
        if stage == 0:
            spot = self.known(number, 0)
            return [push(self.shard(number), self.view(number, spot), core_send.at[number, 0], core_recv.at[number, 0], peer)]
        first = sum(self.place.axes[dim][2] - 1 for dim in order[: stage - 1])
        dim = order[stage - 1]
        copies = []
        for step in self.place.steps(dim):
            spot = self.known(number, stage - 1)
            spot[dim] = self.place.shifted(dim, -step)
            view, piece = self.view(number, spot), first + step
            copies.append(push(view, view, core_send.at[number, piece], core_recv.at[number, piece], peer))
        return copies

    def advance(self, number, stage):
        if stage:
            for copy in self.link(number, stage - 1):
                copy.wait_recv()
        if stage < self.place.core:
            for copy in self.link(number, stage):
                copy.start()
        for copy in self.across(number, stage):
            copy.start()

    def finish(self, number):
        for stage in range(self.place.core + 1):
            if stage < self.place.core:
                for copy in self.link(number, stage):
                    copy.wait_send()
            for copy in self.across(number, stage):
                copy.wait()


def gather_sems(axes, parts, count):
    hops = sum(size - 1 for _, _, size in axes[:-1])
    shapes = (len(parts), hops), (len(parts), hops), (len(parts), hops + 1), (len(parts), hops + 1), (count,)
    return [sems(*shape) for shape in shapes]


class Scatter:
    def __init__(self, place, parts, grads, outs, bufs, send, recv, local):
        self.place, self.parts, self.grads, self.outs = place, parts, grads, outs
        self.bufs = bufs
        self.send, self.recv, self.local = send, recv, local

    def refs(self, number):
        _, _, order, slot = self.parts[number]
        own, *came = self.bufs[order if self.parts[number][1] is not None else None]
        held = own.shape[0]
        return [own.at[slot % held]] + [buf.at[slot] for buf in came]

    def first(self, number, stage):
        order = self.parts[number][2]
        return 1 + sum(self.place.axes[dim][2] - 1 for dim in order[:stage])

    def block(self, number, core):
        array, cols, _, _ = self.parts[number]
        lead = (slice(None),) * self.place.core + (core,)
        return self.grads[array].at[lead + (slice(None), slice(None) if cols is None else cols)]

    def across(self, number):
        place = self.place
        return push(
            self.block(number, place.shifted(place.core, 1)),
            self.refs(number)[1],
            self.send.at[number, 0],
            self.recv.at[number, 0],
            place.device(place.core, 1),
        )

    def own(self, number):
        return pltpu.make_async_copy(
            self.block(number, self.place.own[self.place.core]), self.refs(number)[0], self.local.at[number]
        )

    def spot(self, number, stage, at):
        order = self.parts[number][2]
        dims = [slice(None)] * self.place.core
        for dim in order[:stage]:
            dims[dim] = self.place.own[dim]
        if at is not None:
            dims[order[stage]] = at
        return dims

    def link(self, number, stage, step):
        dim = self.parts[number][2][stage]
        place, refs = self.place, self.refs(number)
        piece = self.first(number, stage) + step - 1
        return push(
            refs[0].at[tuple(self.spot(number, stage, place.shifted(dim, step)))],
            refs[2 + stage].at[step - 1],
            self.send.at[number, piece],
            self.recv.at[number, piece],
            place.device(dim, step),
        )

    def add(self, number, spot, extras):
        acc = self.refs(number)[0]
        free = [dim for dim, index in enumerate(spot) if isinstance(index, slice)]
        sizes = [self.place.axes[dim][2] for dim in free]
        total = math.prod(sizes)

        def one(place, carry):
            index, where = list(spot), []
            rest = place
            for dim, size in zip(reversed(free), reversed(sizes)):
                index[dim] = lax.rem(rest, size)
                where.insert(0, index[dim])
                rest = rest // size
            index = tuple(index)
            value = acc[index].astype(f32)
            for extra in extras:
                value = value + extra[tuple(where)].astype(f32)
            acc[index] = value.astype(acc.dtype)
            return carry

        if total == 1:
            one(0, 0)
        else:
            lax.fori_loop(0, total, one, 0)

    def advance(self, number, stage):
        array, cols, order, _ = self.parts[number]
        place, refs = self.place, self.refs(number)
        if stage == 0:
            self.across(number).start()
            self.own(number).start()
            return
        if stage == 1:
            self.own(number).wait()
            self.across(number).wait_recv()
            came = [refs[1]]
        else:
            dim = order[stage - 2]
            for step in place.steps(dim):
                self.link(number, stage - 2, step).wait_recv()
            came = [refs[stage].at[step - 1] for step in place.steps(dim)]
        if stage <= place.core:
            dim = order[stage - 1]
            for step in list(place.steps(dim)) + [0]:
                at = place.shifted(dim, step)
                spot = self.spot(number, stage - 1, at)
                where = self.within(number, stage - 1, at)
                self.add(number, spot, [extra.at[where] for extra in came])
                if step:
                    self.link(number, stage - 1, step).start()
        else:
            total = refs[0][tuple(place.own[:-1])].astype(f32)
            for extra in came:
                total = total + extra[...].astype(f32)
            if cols is None:
                self.outs[array][...] = total
            else:
                self.outs[array][:, cols] = total

    def within(self, number, stage, at):
        order = self.parts[number][2]
        rest = [dim for dim in range(self.place.core) if dim not in order[:stage]]
        return tuple(at if dim == order[stage] else slice(None) for dim in rest)

    def finish(self, number):
        self.across(number).wait_send()
        order = self.parts[number][2]
        for stage, dim in enumerate(order):
            for step in self.place.steps(dim):
                self.link(number, stage, step).wait_send()


def scatter_buffers(axes, order, tiles, held, block, dtype):
    sizes = [size for _, _, size in axes[:-1]]
    leads = [(held,) + tuple(sizes), (tiles,) + tuple(sizes)]
    left = list(range(len(sizes)))
    for dim in order:
        left.remove(dim)
        leads.append((tiles, sizes[dim] - 1) + tuple(sizes[other] for other in left))
    return [pltpu.VMEM(lead + tuple(block), dtype) for lead in leads]


def scatter_sems(axes, count):
    hops = 1 + sum(size - 1 for _, _, size in axes[:-1])
    return [sems(count, hops), sems(count, hops), sems(count)]


def run_steps(mover, exchange, plan, time, steps):
    for step in range(steps):
        todo = [(part, stage) for part, row in enumerate(plan) for stage, at in enumerate(row) if at == step]

        @pl.when(time == step)
        def _(todo=todo, step=step):
            for part, stage in todo:
                mover.advance(part, stage)
            if 1 <= step <= PIECES:
                exchange.start(step - 1)


def run_rest(mover, exchange, plan, steps):
    for part, row in enumerate(plan):
        for stage, at in enumerate(row):
            if at >= steps:
                mover.advance(part, stage)
    for part in range(len(plan)):
        mover.finish(part)
    exchange.wait()


def forward_kernel(axes, seqs, parts, plan, len_ref, x_ref, w_ref, bias_ref, *refs):
    if axes is None:
        qkv_ref, ctx_ref, probs_ref = refs
    else:
        rest_ref, cot_ref, qkv_ref, ctx_ref, probs_ref, weights_ref, cots_ref = refs[:7]
        place = Place(axes)
        gather = Gather(place, parts, [rest_ref], [weights_ref], *refs[7:12])
        exchange = Exchange(place, cot_ref, cots_ref, PIECES, *refs[12:15])
    seq, pair = pl.program_id(0), pl.program_id(1)
    time = seq * PAIRS + pair
    steps = seqs * PAIRS
    length = len_ref[seq]
    count, width = x_ref.shape[1], x_ref.shape[2]
    lane = lax.broadcasted_iota(jnp.int32, (1, PAIR), 1)

    if axes is not None:

        @pl.when(time == 0)
        def _():
            meet(place, place.friends(cot_ref.shape[0]))
            gather.start()
            gather.local()

        run_steps(gather, exchange, plan, time, steps)

    @pl.when(pair == 0)
    def _():
        tokens = x_ref[0]
        step = 2 * PAIR
        for start in range(0, 3 * width, step):
            part = start // width
            projected = nn(tokens, w_ref[:, start : start + step])
            if part != 1:
                cols = slice(start - part * width, start - part * width + step)
                projected = projected + bias_ref[part // 2 : part // 2 + 1, cols].astype(f32)
            projected = projected.astype(bf16)
            if part == 0:
                projected = projected * jnp.asarray(1.0 / math.sqrt(HEAD_DIM), bf16)
            for half in range(2):
                qkv_ref[0, start // PAIR + half] = projected[:, half * PAIR : (half + 1) * PAIR]

    key = qkv_ref[0, PAIRS + pair]
    value = qkv_ref[0, 2 * PAIRS + pair]
    unusable = lax.broadcasted_iota(jnp.int32, (count, 1), 0) >= length
    mask = jnp.where(unusable, masked_fill, 0.0).astype(bf16)
    keys = [jnp.where(lane == spare, mask, key) for spare in (PAIR - 1, 0)]
    for start in range(0, count, ROWS):
        rows = slice(start, start + ROWS)
        query = qkv_ref[0, pair, rows, :]
        outs = []
        for head in range(2):
            mine = (lane < HEAD_DIM) if head == 0 else (lane >= HEAD_DIM)
            spare = jnp.where(lane == (PAIR - 1 if head == 0 else 0), 1.0, 0.0).astype(bf16)
            scores = nt(jnp.where(mine, query, spare), keys[head])
            top = jnp.max(scores, axis=1, keepdims=True)
            powers = jnp.exp(scores - top)
            total = jnp.sum(powers, axis=1, keepdims=True)
            probs = (powers * (1.0 / total)).astype(bf16)
            probs_ref[0, 0, head, rows, :] = probs
            outs.append(nn(probs, value))
        ctx_ref[0, rows, :] = jnp.where(lane < HEAD_DIM, outs[0], outs[1]).astype(bf16)

    if axes is not None:

        @pl.when(time == steps - 1)
        def _():
            run_rest(gather, exchange, plan, steps)


def attention_forward(axes, lengths, tokens, w_qkv, biases, rest, outgoing):
    seqs, rows, width = tokens.shape
    out_shape = [
        jax.ShapeDtypeStruct((seqs, 3 * PAIRS, rows, PAIR), bf16),
        jax.ShapeDtypeStruct((seqs, rows, width), bf16),
        jax.ShapeDtypeStruct((seqs, PAIRS, 2, rows, rows), bf16),
    ]
    in_specs = [pl.BlockSpec((1, rows, width), lambda s, p, *_: (s, 0, 0)), whole(w_qkv.shape), whole(biases.shape)]
    out_specs = [
        pl.BlockSpec((1, 3 * PAIRS, rows, PAIR), lambda s, p, *_: (s, 0, 0, 0)),
        pl.BlockSpec((1, rows, PAIR), lambda s, p, *_: (s, 0, p)),
        pl.BlockSpec((1, 1, 2, rows, rows), lambda s, p, *_: (s, p, 0, 0, 0)),
    ]
    scratch, extra, parts, plan, talk = [], [], [], [], {}
    if axes is not None:
        parts = [(0, pl.ds(start, width), (2, 0, 1)) for start in range(0, rest.shape[1], width)]
        plan = [[0] + [2 * stage - 1 + max(0, place - 2) for stage in range(1, 4)] for place in range(len(parts))]
        extra = [rest, outgoing]
        in_specs += [ANY, ANY]
        sizes = tuple(size for _, _, size in axes)
        out_shape += [jax.ShapeDtypeStruct(sizes + rest.shape, bf16), jax.ShapeDtypeStruct(outgoing.shape, bf16)]
        out_specs += [ANY, ANY]
        friends = outgoing.shape[0] - 1
        scratch = gather_sems(axes, parts, 1) + exchange_sems(friends)
        talk = {"collective_id": 3, "has_side_effects": True}
    return pl.pallas_call(
        functools.partial(forward_kernel, axes, seqs, parts, plan),
        out_shape=tuple(out_shape),
        grid_spec=pltpu.PrefetchScalarGridSpec(
            num_scalar_prefetch=1,
            grid=(seqs, PAIRS),
            in_specs=in_specs,
            out_specs=tuple(out_specs),
            scratch_shapes=scratch,
        ),
        compiler_params=pltpu.CompilerParams(vmem_limit_bytes=58 << 20, **talk),
        cost_estimate=pl.CostEstimate(flops=60_000_000_000, transcendentals=30_000_000, bytes_accessed=80_000_000),
        name="attention_forward",
    )(lengths, tokens, w_qkv, biases, *extra)


def normal_tail(values):
    size = jnp.abs(values)
    bell = jnp.exp(-0.5 * values * values)
    t = 1.0 / (1.0 + (0.3275911 / math.sqrt(2.0)) * size)
    poly = t * (
        0.5 * 0.254829592
        + t * (0.5 * -0.284496736 + t * (0.5 * 1.421413741 + t * (0.5 * -1.453152027 + t * (0.5 * 1.061405429))))
    )
    tail = poly * bell
    return jnp.where(values >= 0, 1.0 - tail, tail), bell


def row_mean(values):
    return jnp.mean(values, axis=-1, keepdims=True)


def middle_kernel(
    len_ref, in_slot, out_slot, x_ref, ctx_ref, cot_ref, w_ref, vec_ref, bu_ref,
    out_ref, gres_ref, gctx_ref, dw_ref, dvec_ref, dbu_ref, rms_ref,
    acc, active, slope, sums, stage, sems,
):
    seq, index = pl.program_id(0), pl.program_id(1)
    first = jnp.logical_and(seq == 0, index == 0)
    final = jnp.logical_and(seq == pl.num_programs(0) - 1, index == pl.num_programs(1) - 1)
    length = len_ref[seq]
    width = x_ref.shape[2]
    chunks = bu_ref.shape[1] // width
    tile = lambda place: slice(place * width, (place + 1) * width)
    up = lambda chunk: tile(1 + chunk)
    down = lambda chunk: tile(1 + chunks + chunk)

    @pl.when(first)
    def _():
        acc[...] = jnp.zeros_like(acc)
        dvec_ref[...] = jnp.zeros_like(dvec_ref)
        dbu_ref[...] = jnp.zeros_like(dbu_ref)

    @pl.when(index == 0)
    def _():
        sums[...] = jnp.zeros_like(sums)

    @pl.when(index * BLOCK >= length)
    def _():
        out_ref[...] = jnp.zeros_like(out_ref)
        gres_ref[...] = jnp.zeros_like(gres_ref)
        gctx_ref[...] = jnp.zeros_like(gctx_ref)

    @pl.when(index * BLOCK < length)
    def _():
        vec = lambda place: vec_ref[place : place + 1, :].astype(f32)
        bias_out, gain_a, shift_a, bias_down, gain_f, shift_f = (vec(place) for place in range(2, 8))
        valid = (lax.broadcasted_iota(jnp.int32, (BLOCK, 1), 0) + index * BLOCK < length).astype(f32)
        tokens = x_ref[0].astype(f32)
        context = ctx_ref[0]
        branch_a = nn(context, w_ref[:, tile(0)]) + bias_out
        mixed = tokens + branch_a
        center = mixed - row_mean(mixed)
        scale_a = lax.rsqrt(row_mean(center * center) + norm_eps)
        hat_a = center * scale_a
        hidden = hat_a * gain_a + shift_a
        hidden_low = hidden.astype(bf16)
        branch_f = bias_down
        for chunk in range(chunks):
            cols = tile(chunk)
            gate = nn(hidden_low, w_ref[:, up(chunk)]) + bu_ref[:, cols].astype(f32)
            share, bell = normal_tail(gate)
            act = (gate * share).astype(bf16)
            active[:, cols] = act
            slope[:, cols] = share + gate * bell * (1.0 / math.sqrt(2.0 * math.pi))
            branch_f = branch_f + nn(act, w_ref[:, down(chunk)])
        mixed_f = hidden + branch_f
        center = mixed_f - row_mean(mixed_f)
        scale_f = lax.rsqrt(row_mean(center * center) + norm_eps)
        hat_f = center * scale_f
        out_ref[0] = ((hat_f * gain_f + shift_f) * valid).astype(bf16)
        g_result = cot_ref[0].astype(f32) * valid
        g_hat = g_result * gain_f
        g_res2 = scale_f * (g_hat - row_mean(g_hat) - hat_f * row_mean(g_hat * hat_f))
        g_ffn = g_res2.astype(bf16)
        g_hidden = g_res2
        for chunk in range(chunks):
            cols = tile(chunk)
            g_gate = nt(g_ffn, w_ref[:, down(chunk)]) * slope[:, cols]
            g_low = g_gate.astype(bf16)
            acc[:, down(chunk)] += tn(active[:, cols], g_ffn)
            acc[:, up(chunk)] += tn(hidden_low, g_low)
            dbu_ref[:, cols] += jnp.sum(g_low.astype(f32), axis=0, keepdims=True)
            g_hidden = g_hidden + nt(g_low, w_ref[:, up(chunk)])
        g_hat = g_hidden * gain_a
        g_res1 = scale_a * (g_hat - row_mean(g_hat) - hat_a * row_mean(g_hat * hat_a))
        g_attn = g_res1.astype(bf16)
        gres_ref[0] = g_res1
        gctx_ref[0] = nt(g_attn, w_ref[:, tile(0)]).astype(bf16)
        acc[:, tile(0)] += tn(context, g_attn)
        column = lambda values: jnp.sum(values, axis=0, keepdims=True)
        dvec_ref[2:3, :] += column(g_attn.astype(f32))
        dvec_ref[3:4, :] += column(g_hidden * hat_a)
        dvec_ref[4:5, :] += column(g_hidden)
        dvec_ref[5:6, :] += column(g_ffn.astype(f32))
        dvec_ref[6:7, :] += column(g_result * hat_f)
        dvec_ref[7:8, :] += column(g_result)
        sums[0:1, :] += column(tokens * tokens * valid)
        sums[1:2, :] += column(branch_a * branch_a * valid)
        sums[2:3, :] += column(branch_f * branch_f * valid)

    @pl.when(index == pl.num_programs(1) - 1)
    def _():
        mean = jnp.sum(sums[...], axis=1, keepdims=True) / (length * width).astype(f32)
        rms_ref[0] = jnp.broadcast_to(jnp.sqrt(mean), rms_ref.shape[1:])

    @pl.when(final)
    def _():
        copies = []
        for place in range(1 + 2 * chunks):
            slot = place % 2
            if place >= 2:
                copies[place - 2].wait()
            stage[slot] = acc[:, tile(place)].astype(bf16)
            copies.append(pltpu.make_async_copy(stage.at[slot], dw_ref.at[:, tile(place)], sems.at[slot]))
            copies[-1].start()
        copies[-2].wait()
        copies[-1].wait()


def middle(lengths, in_slot, out_slot, tokens, context, cots, weights, vectors, bias_up):
    seqs, rows, width = tokens.shape
    slots = cots.shape[0]
    hidden = bias_up.shape[1]
    inside = lambda s, i, lens: jnp.minimum(i, block_count(lens[s]) - 1)
    here = pl.BlockSpec((1, BLOCK, width), lambda s, i, lens, a, b: (s, inside(s, i, lens), 0))
    there = pl.BlockSpec((1, BLOCK, width), lambda s, i, *_: (s, i, 0))
    flops = 6 * seqs * rows * (width * width + 2 * width * hidden)
    return pl.pallas_call(
        middle_kernel,
        out_shape=(
            jax.ShapeDtypeStruct((slots, rows, width), bf16),
            jax.ShapeDtypeStruct((seqs, rows, width), f32),
            jax.ShapeDtypeStruct((seqs, rows, width), bf16),
            jax.ShapeDtypeStruct(weights.shape, bf16),
            jax.ShapeDtypeStruct((8, width), f32),
            jax.ShapeDtypeStruct((1, hidden), f32),
            jax.ShapeDtypeStruct((seqs, 8, 128), f32),
        ),
        grid_spec=pltpu.PrefetchScalarGridSpec(
            num_scalar_prefetch=3,
            grid=(seqs, rows // BLOCK),
            in_specs=[
                here,
                here,
                pl.BlockSpec((1, BLOCK, width), lambda s, i, lens, a, b: (a[s], inside(s, i, lens), 0)),
                whole(weights.shape),
                whole(vectors.shape),
                whole(bias_up.shape),
            ],
            out_specs=[
                pl.BlockSpec((1, BLOCK, width), lambda s, i, lens, a, b: (b[s], i, 0)),
                there,
                there,
                pl.BlockSpec(memory_space=pl.ANY),
                whole((8, width)),
                whole((1, hidden)),
                pl.BlockSpec((1, 8, 128), lambda s, i, *_: (s, 0, 0)),
            ],
            scratch_shapes=[
                pltpu.VMEM(weights.shape, f32),
                pltpu.VMEM((BLOCK, hidden), bf16),
                pltpu.VMEM((BLOCK, hidden), f32),
                pltpu.VMEM((8, width), f32),
                pltpu.VMEM((2, width, width), bf16),
                pltpu.SemaphoreType.DMA((2,)),
            ],
        ),
        compiler_params=pltpu.CompilerParams(vmem_limit_bytes=60 << 20),
        cost_estimate=pl.CostEstimate(flops=flops, transcendentals=seqs * rows * hidden, bytes_accessed=60_000_000),
        name="middle",
    )(lengths, in_slot, out_slot, tokens, context, cots, weights, vectors, bias_up)


def backward_kernel(axes, seqs, parts, plan, x_ref, qkv_in, ctx_ref, gctx_ref, probs_ref, gres_ref, w_ref, *refs):
    if axes is None:
        gin_ref, dw_ref, dvec_ref = refs[:3]
        mixed, acc_w, stage, copy_sems = refs[3:]
    else:
        grad_ref, result_ref, gin_ref, dw_ref, dvec_ref, sum_ref, arrived_ref = refs[:7]
        mixed, acc_w, stage, copy_sems = refs[7:11]
        place = Place(axes)
        bufs = {parts[0][2]: refs[11:16]}
        scatter = Scatter(place, parts, [grad_ref], [sum_ref], bufs, *refs[16:19])
        exchange = Exchange(place, result_ref, arrived_ref, PIECES, *refs[19:22])
    seq, pair = pl.program_id(0), pl.program_id(1)
    time = seq * PAIRS + pair
    steps = seqs * PAIRS
    count, width = x_ref.shape[1], x_ref.shape[2]
    lane = lax.broadcasted_iota(jnp.int32, (1, PAIR), 1)

    if axes is not None:

        @pl.when(time == 0)
        def _():
            meet(place, place.friends(result_ref.shape[0]))

        run_steps(scatter, exchange, plan, time, steps)

    @pl.when(time == 0)
    def _():
        acc_w[...] = jnp.zeros_like(acc_w)
        dvec_ref[...] = jnp.zeros_like(dvec_ref)

    key = qkv_in[0, 1, 0]
    value = qkv_in[0, 2, 0]
    g_key, g_value = [0.0, 0.0], [0.0, 0.0]
    for start in range(0, count, ROWS):
        rows = slice(start, start + ROWS)
        query = qkv_in[0, 0, 0, rows, :]
        grad = gctx_ref[0, rows, :]
        agree = grad.astype(f32) * ctx_ref[0, rows, :].astype(f32)
        query_t, grad_t = query.T, grad.T
        g_query = jnp.zeros((ROWS, PAIR), f32)
        for head in range(2):
            mine = (lane < HEAD_DIM) if head == 0 else (lane >= HEAD_DIM)
            only = lambda values: jnp.where(mine, values, jnp.zeros_like(values))
            lanes = slice(head * HEAD_DIM, (head + 1) * HEAD_DIM)
            delta = jnp.sum(only(agree), axis=1, keepdims=True)
            probs = probs_ref[0, 0, head, rows, :]
            g_probs = nt(only(grad), value)
            g_scores = (probs.astype(f32) * (g_probs - delta)).astype(bf16)
            g_query = g_query + nn(g_scores, only(key))
            g_key[head] = g_key[head] + nn(query_t[lanes], g_scores)
            g_value[head] = g_value[head] + nn(grad_t[lanes], probs)
        mixed[pair, rows, :] = (g_query * (1.0 / math.sqrt(HEAD_DIM))).astype(bf16)
    mixed[PAIRS + pair] = jnp.concatenate(g_key, axis=0).T.astype(bf16)
    mixed[2 * PAIRS + pair] = jnp.concatenate(g_value, axis=0).T.astype(bf16)

    @pl.when(pair == PAIRS - 1)
    def _():
        @pl.loop(0, count // BLOCK)
        def _(index):
            rows = pl.ds(pl.multiple_of(index * BLOCK, BLOCK), BLOCK)
            tokens = x_ref[0, rows, :]
            g_in = gres_ref[0, rows, :]
            for part in range(3):
                cols = slice(part * width, (part + 1) * width)
                piece = jnp.concatenate([mixed[part * PAIRS + head, rows, :] for head in range(PAIRS)], axis=1)
                g_in = g_in + nt(piece, w_ref[:, cols])
                acc_w[:, cols] += tn(tokens, piece)
                if part != 1:
                    dvec_ref[part // 2 : part // 2 + 1, :] += jnp.sum(piece.astype(f32), axis=0, keepdims=True)
            gin_ref[0, rows, :] = g_in.astype(bf16)

    @pl.when(time == steps - 1)
    def _():
        copies = []
        for part in range(3):
            cols = slice(part * width, (part + 1) * width)
            slot = part % 2
            if part >= 2:
                copies[part - 2].wait()
            stage[slot] = acc_w[:, cols].astype(bf16)
            copies.append(pltpu.make_async_copy(stage.at[slot], dw_ref.at[:, cols], copy_sems.at[slot]))
            copies[-1].start()
        copies[-2].wait()
        copies[-1].wait()
        if axes is not None:
            run_rest(scatter, exchange, plan, steps)


def attention_backward(axes, tokens, qkv, context, g_context, probs, g_res1, w_qkv, dw_rest, results):
    seqs, rows, width = tokens.shape
    pair_cols = pl.BlockSpec((1, rows, PAIR), lambda s, p: (s, 0, p))
    seq_rows = pl.BlockSpec((1, rows, width), lambda s, p: (s, 0, 0))
    in_specs = [
        seq_rows,
        pl.BlockSpec((1, 3, 1, rows, PAIR), lambda s, p: (s, 0, p, 0, 0)),
        pair_cols,
        pair_cols,
        pl.BlockSpec((1, 1, 2, rows, rows), lambda s, p: (s, p, 0, 0, 0)),
        seq_rows,
        whole(w_qkv.shape),
    ]
    out_shape = [
        jax.ShapeDtypeStruct((seqs, rows, width), bf16),
        jax.ShapeDtypeStruct(w_qkv.shape, bf16),
        jax.ShapeDtypeStruct((8, width), f32),
    ]
    out_specs = [seq_rows, ANY, whole((8, width))]
    scratch = [
        pltpu.VMEM((3 * PAIRS, rows, PAIR), bf16),
        pltpu.VMEM(w_qkv.shape, f32),
        pltpu.VMEM((2, width, width), bf16),
        sems(2),
    ]
    extra, parts, plan, talk = [], [], [], {}
    if axes is not None:
        sizes = tuple(size for _, _, size in axes)
        order = (1, 0, 2)
        grads = dw_rest.reshape(sizes + (-1, dw_rest.shape[1]))
        block = grads.shape[4:]
        parts = [(0, pl.ds(start, width), order, start // width) for start in range(0, block[1], width)]
        plan = [
            [max(0, place - 2)] + [2 * stage - 1 + max(0, place - 2) for stage in range(1, 5)] for place in range(len(parts))
        ]
        extra = [grads, results]
        in_specs += [ANY, ANY]
        out_shape += [jax.ShapeDtypeStruct(block, f32), jax.ShapeDtypeStruct(results.shape, bf16)]
        out_specs += [whole(block), ANY]
        friends = results.shape[0] - 1
        scratch += scatter_buffers(axes, order, len(parts), len(parts), (block[0], width), bf16)
        scratch += scatter_sems(axes, len(parts)) + exchange_sems(friends)
        talk = {"collective_id": 4, "has_side_effects": True}
    return pl.pallas_call(
        functools.partial(backward_kernel, axes, seqs, parts, plan),
        out_shape=tuple(out_shape),
        grid_spec=pltpu.PrefetchScalarGridSpec(
            num_scalar_prefetch=0,
            grid=(seqs, PAIRS),
            in_specs=in_specs,
            out_specs=tuple(out_specs),
            scratch_shapes=scratch,
        ),
        compiler_params=pltpu.CompilerParams(vmem_limit_bytes=62 << 20, **talk),
        cost_estimate=pl.CostEstimate(flops=120_000_000_000, transcendentals=1, bytes_accessed=100_000_000),
        name="attention_backward",
    )(tokens, qkv.reshape(seqs, 3, PAIRS, rows, PAIR), context, g_context, probs, g_res1, w_qkv, *extra)


def gather_kernel(axes, parts, count, *refs):
    place = Place(axes)
    gather = Gather(place, parts, refs[:count], refs[count : 2 * count], *refs[2 * count :])
    meet(place)
    gather.start()
    for stage in range(place.core + 1):
        if stage == 1:
            gather.local()
        for part in range(len(parts)):
            gather.advance(part, stage)
    for part in range(len(parts)):
        gather.finish(part)


def gather_blocks(axes, parts, shards):
    sizes = tuple(size for _, _, size in axes)
    return pl.pallas_call(
        functools.partial(gather_kernel, axes, parts, len(shards)),
        out_shape=tuple(jax.ShapeDtypeStruct(sizes + shard.shape, shard.dtype) for shard in shards),
        in_specs=[ANY] * len(shards),
        out_specs=tuple([ANY] * len(shards)),
        scratch_shapes=gather_sems(axes, parts, len(shards)),
        compiler_params=pltpu.CompilerParams(collective_id=1, has_side_effects=True),
        name="gather_blocks",
    )(*shards)


def scatter_kernel(axes, parts, orders, *refs):
    grad_ref, small_ref, note_ref, out_ref, out_small, notes_ref = refs[:6]
    place = Place(axes)
    member = place.at["fsdp"]
    friends = place.friends(notes_ref.shape[0])
    bufs = {order: refs[6 + 5 * i : 11 + 5 * i] for i, order in enumerate(orders + (None,))}
    rest = refs[6 + 5 * (len(orders) + 1) :]
    scatter = Scatter(place, parts, [grad_ref, small_ref], [out_ref, out_small], bufs, *rest[:3])
    meet(place, friends)
    told = [
        push(note_ref, notes_ref.at[member], rest[3].at[step], rest[4].at[step], (place.at["dp"], friend))
        for step, friend in enumerate(friends)
    ]
    for copy in told:
        copy.start()
    notes_ref[member] = note_ref[...]
    for stage in range(place.core + 2):
        for part in range(len(parts)):
            scatter.advance(part, stage)
    for copy in told:
        copy.wait()
    for part in range(len(parts)):
        scatter.finish(part)


def scatter_sums(axes, grad, small, note, shards):
    sizes = tuple(size for _, _, size in axes)
    grad = grad.reshape(sizes + (-1, grad.shape[1]))
    small = small.reshape(sizes + (-1, small.shape[1]))
    block = grad.shape[4:]
    orders = ((2, 1, 0), (1, 2, 0))
    cut = block[1] // 6
    parts = [(0, pl.ds(place * cut, cut), orders[place % 2], place // 2) for place in range(6)]
    parts.insert(0, (1, None, orders[0], 0))
    bufs = [buf for order in orders for buf in scatter_buffers(axes, order, 3, 3, (block[0], cut), bf16)]
    bufs += scatter_buffers(axes, orders[0], 1, 1, small.shape[4:], f32)
    return pl.pallas_call(
        functools.partial(scatter_kernel, axes, parts, orders),
        out_shape=(
            jax.ShapeDtypeStruct(block, f32),
            jax.ShapeDtypeStruct(small.shape[4:], f32),
            jax.ShapeDtypeStruct((shards,) + note.shape, f32),
        ),
        in_specs=[ANY, ANY, VMEM],
        out_specs=(VMEM, VMEM, VMEM),
        scratch_shapes=bufs + scatter_sems(axes, len(parts)) + [sems(shards - 1), sems(shards - 1)],
        compiler_params=pltpu.CompilerParams(collective_id=2, has_side_effects=True, vmem_limit_bytes=56 << 20),
        name="scatter_sums",
    )(grad, small, note)


def body(
    tokens, lengths, deal_order, qkv_weight, query_bias, value_bias, out_weight, out_bias, attn_gain, attn_shift,
    up_weight, up_bias, down_weight, down_bias, ffn_gain, ffn_shift, cotangent,
):
    shards = lax.axis_size("fsdp")
    axes = mesh_axes(lax.axis_size("dp"), shards)
    devices = lax.axis_size("dp") * shards
    seqs, rows, width = tokens.shape
    hidden = up_weight.shape[1]
    chunks = hidden // width
    per = width // devices
    column = shards * seqs
    base = lax.axis_index("dp") * column
    member = lax.axis_index("fsdp")
    order = lax.dynamic_slice_in_dim(deal_order, base, column) - base
    mine = member * seqs
    own_lengths = lax.dynamic_slice_in_dim(lengths, base + mine, seqs)
    target = lax.dynamic_slice_in_dim(order, mine, seqs) // seqs
    dealt_here = mine + jnp.arange(seqs, dtype=jnp.int32)
    matches = order[None, :] == dealt_here[:, None]
    source = jnp.sum(jnp.where(matches, jnp.arange(column, dtype=jnp.int32)[None, :], 0), axis=1)
    peers = jnp.arange(shards, dtype=jnp.int32)

    up_mixed = up_weight.reshape(per, width, chunks).transpose(0, 2, 1).reshape(per, hidden)
    rest = jnp.concatenate([out_weight, up_mixed, down_weight.reshape(per, hidden)], axis=1)
    outgoing = cotangent[0][None]
    for place in range(1, seqs):
        outgoing = jnp.where((source[place] // seqs == peers)[:, None, None], cotangent[place][None], outgoing)
    small = jnp.concatenate(
        [query_bias, value_bias, out_bias, attn_gain, attn_shift, down_bias, ffn_gain, ffn_shift, up_bias]
    )
    small = jnp.pad(small, (0, 8 * 128 - small.shape[0])).reshape(8, 128)
    if axes is None:
        w_qkv = lax.all_gather(qkv_weight, BOTH, axis=0, tiled=True)
        small = lax.all_gather(small, BOTH, axis=0, tiled=False)
    else:
        cut = qkv_weight.shape[1] // 6
        orders = ((0, 2, 1), (0, 2, 1), (1, 0, 2))
        parts = [(1, slice(None), orders[0])] + [(0, pl.ds(i * cut, cut), orders[i % 3]) for i in range(6)]
        w_qkv, small = gather_blocks(axes, parts, [qkv_weight, small])
        w_qkv = w_qkv.reshape(width, -1)
    small = small.reshape(devices, -1)
    vectors = small[:, : 8 * per].reshape(devices, 8, per).transpose(1, 0, 2).reshape(8, width)
    bias_up = small[:, 8 * per : 8 * per + chunks * per].reshape(width, chunks).T.reshape(1, hidden)

    if axes is None:
        weights = lax.all_gather(rest, BOTH, axis=0, tiled=True)
        cots = lax.all_to_all(outgoing, "fsdp", split_axis=0, concat_axis=0, tiled=True)
        qkv, context, probs = attention_forward(axes, own_lengths, tokens, w_qkv, vectors, rest, outgoing)
    else:
        qkv, context, probs, weights, cots = attention_forward(
            axes, own_lengths, tokens, w_qkv, vectors, rest, outgoing
        )
        weights = weights.reshape(width, -1)
    results, g_res1, g_context, dw_rest, dvec, dbu, rms = middle(
        own_lengths, target, target, tokens, context, cots, weights, vectors, bias_up
    )
    outs = attention_backward(axes, tokens, qkv, context, g_context, probs, g_res1, w_qkv, dw_rest, results)
    input_grad, dw_qkv, dqv = outs[:3]
    if axes is None:
        arrived = lax.all_to_all(results, "fsdp", split_axis=0, concat_axis=0, tiled=True)
    else:
        rest_grad, arrived = outs[3:]
    layer_out = jnp.stack(
        [lax.dynamic_index_in_dim(arrived, source[t] // seqs, 0, keepdims=False) for t in range(seqs)]
    )

    dvec = (dvec + dqv).reshape(8, devices, per).transpose(1, 0, 2).reshape(devices, 8 * per)
    dbu = dbu.reshape(chunks, devices, per).transpose(1, 2, 0).reshape(devices, chunks * per)
    packed = jnp.pad(jnp.concatenate([dvec, dbu], axis=1), ((0, 0), (0, 8 * 128 - (8 + chunks) * per)))
    rms = rms.reshape(seqs * 8, 128)
    if axes is None:
        scatter = lambda whole: lax.psum_scatter(whole, BOTH, scatter_dimension=0, tiled=True)
        qkvw_grad, rest_grad = scatter(dw_qkv).astype(f32), scatter(dw_rest).astype(f32)
        packed = scatter(packed)
        rms = lax.all_gather(rms, "fsdp", axis=0, tiled=False)
    else:
        qkvw_grad, packed, rms = scatter_sums(axes, dw_qkv, packed.reshape(devices * 8, 128), rms, shards)
    packed = packed.reshape(-1)
    vector = [packed[place * per : (place + 1) * per] for place in range(8)]
    rms = rms.reshape(column, 8, 128)[:, :3, 0]
    branch_rms = jnp.sum(jnp.where((source[:, None] == jnp.arange(column))[:, :, None], rms[None], 0.0), axis=1)
    outw_grad = rest_grad[:, :width]
    upw_grad = rest_grad[:, width : width + hidden].reshape(per, chunks, width).transpose(0, 2, 1).reshape(per, hidden)
    downw_grad = rest_grad[:, width + hidden :].reshape(per * chunks, width)
    return (
        layer_out, input_grad, qkvw_grad, vector[0], vector[1], outw_grad, vector[2], vector[3], vector[4], upw_grad,
        packed[8 * per : 8 * per + chunks * per], downw_grad, vector[5], vector[6], vector[7], branch_rms,
    )


def solution(mesh):
    rows3, rows2, rows1 = P(BOTH, None, None), P(BOTH, None), P(BOTH)
    in_specs = (
        rows3, P(), P(), rows2, rows1, rows1, rows2, rows1, rows1, rows1, rows2, rows1, rows2, rows1, rows1, rows1, rows3,
    )
    out_specs = (
        rows3, rows3, rows2, rows1, rows1, rows2, rows1, rows1, rows1, rows2, rows1, rows2, rows1, rows1, rows1, rows2,
    )
    return jax.shard_map(body, mesh=mesh, in_specs=in_specs, out_specs=out_specs, check_vma=False)
```

time: 844 us -> 442 us (0.52)
  waiting for transfers between devices: 267 us -> 0 us
  blocking collectives: 226 us -> 0 us
  Pallas kernels: 281 us -> 395 us
  local copies, waits for them, and re-layouts: 11.4 us -> 24.4 us
  between operations: 18.6 us -> 6.15 us
  starting transfers between devices: 11.1 us -> 0 us
    unnamed x2 -> x0, blocking collectives: 220 us -> none
    reduce_scatter x4 -> x0, waiting for transfers between devices: 199 us -> none  [body(): lax.psum_scatter(whole, BOTH, scatter_dimension=0, tiled=True)]
    pallas_call x2 -> x4, Pallas kernels: 173 us -> 289 us  [the longest x1 120 us: attention_backward(): pl.pallas_call(functools.partial(backward_kernel, axes, seqs, parts, plan...]
    all_gather x4 -> x0, waiting for transfers between devices: 64.4 us -> none  [body(): gather = lambda shard: lax.all_gather(shard, BOTH, axis=0, tiled=True)]
    all_to_all x2 -> x0, starting transfers between devices: 10.8 us -> none  [the longest x1 5.42 us: body(): lax.all_to_all(outgoing, 'fsdp', split_axis=0, concat_axis=0, tiled=True)]
    unnamed x32 -> x48, local copies, waits for them, and re-layouts: 0.33 us -> 9.59 us
  transfers between devices with their start and end apart: 10 -> 0, of which waited for: 3 -> 0; matrix products, arithmetic and copies ran while one was open for 3% -> 0% of each run, Pallas kernels for 21% -> 0%
where the time goes in v3:
time: 442 us; the launch traced here: 435 us
  Pallas kernels  395 us (89%)
  local copies, waits for them, and re-layouts  24.4 us (6%)
  other arithmetic  9.16 us (2%)
  between operations  6.15 us (1%)
    pallas_call x1, Pallas kernels, attention_backward(): pl.pallas_call(functools.partial(backward_kernel, axes, seqs, parts, plan...  120 us
    pallas_call x1, Pallas kernels, middle(): pl.pallas_call(middle_kernel, out_shape=(jax.ShapeDtypeStruct((slots, row...  106 us
    pallas_call x1, Pallas kernels, attention_forward(): pl.pallas_call(functools.partial(forward_kernel, axes, seqs, parts, plan)...  104 us
    pallas_call x1, Pallas kernels, scatter_sums(): pl.pallas_call(functools.partial(scatter_kernel, axes, parts, orders), ou...  33.9 us
    pallas_call x1, Pallas kernels, gather_blocks(): pl.pallas_call(functools.partial(gather_kernel, axes, parts, len(shards))...  30.9 us
    unnamed x48, local copies, waits for them, and re-layouts  9.59 us

profile of v3, /device:TPU:0, one launch (start us, length us, event | category | flops | bytes accessed | tf_op | source)
XLA Modules:
  0.0 434.8 jit_solution(6474080858351007495)
XLA Ops:
  0.7 0.7 dynamic-slice_subtract_fusion
  1.4 0.2 fusion.1
  1.6 0.5 copy-done.7
  2.1 0.6 fusion.4
  5.3 2.1 slice_bitcast_fusion.1
  7.5 3.3 broadcast_select_fusion.refs_1_
  10.8 0.6 dynamic_slice.16.len_ref
  11.5 0.1 concatenate.9
  11.6 0.6 pad_bitcast_fusion.refs_1_
  12.2 30.9 %gather_blocks.1 = (bf16[4,2,2,2,24,2304]{5,4,3,2,1,0:T(8,128)(2,1)}, bf16[4,2,2,2,8,128]{5,4,3,2,1,0:T(8,128)(2,1)}) custom-call(bf16[24,2304]{1,0:T(8,128)(2,1)} %refs_0_.1, bf16[8,128]{1,0:T(8,128)(2,1)} %pad_bitcast_fusion.refs_1_), custom_call_target="tpu_custom_call" | custom-call | tf_op jit(solution)/shard_map/gather_blocks/pallas_call | solution.py:839
  43.1 0.9 copy.67
  44.0 0.1 reshape.138
  44.1 0.7 reshape.139.bias_ref.vec_ref
  44.8 0.4 copy.51
  45.2 0.5 copy.52
  45.8 0.1 reshape.142
  45.9 0.7 pad_maximum_fusion.1.refs_0_
  46.6 103.7 %attention_forward.1 = (bf16[2,18,1024,128]{3,2,1,0:T(8,128)(2,1)}, bf16[2,1024,768]{2,1,0:T(8,128)(2,1)}, bf16[2,6,2,1024,1024]{4,3,2,1,0:T(8,128)(2,1)}, bf16[...) custom-call(s32[2]{0:T(128)} %dynamic_slice.16.len_ref, bf16[2,1024,768]{2,1,0:T(8,128)(2,1)} %x_ref.5, ...), custom_call_target="tpu_custom_call" | custom-call | flops 60000002048 | bytes 80000000 | tf_op jit(solution)/shard_map/attention_forward/pallas_call | solution.py:482
  150.3 0.6 and_select_fusion.in_slot.out_slot
  151.0 0.2 reshape.145
  151.2 0.1 copy.53
  151.3 0.6 copy.64
  151.9 106.3 %middle.1 = (bf16[4,1024,768]{2,1,0:T(8,128)(2,1)}, f32[2,1024,768]{2,1,0:T(8,128)}, bf16[2,1024,768]{2,1,0:T(8,128)(2,1)}, bf16[768,6912]{1,0:T(8,128)(2,1)}, f...) custom-call(s32[2]{0:T(128)} %dynamic_slice.16.len_ref, s32[2]{0:T(128)} %and_select_fusion.in_slot.out_slot, ...), custom_call_target="tpu_custom_call" | custom-call | flops 65229815808 | bytes 60000000 | tf_op jit(solution)/shard_map/middle/pallas_call | solution.py:630
  258.2 120.4 %attention_backward.1 = (bf16[2,1024,768]{2,1,0:T(8,128)(2,1)}, bf16[768,2304]{1,0:T(8,128)(2,1)}, f32[8,768]{1,0:T(8,128)}, f32[24,6912]{1,0:T(8,128)}, bf16[4,1024,768]{2,1,0:T(8,128)(2,1)}) custom-call(bf16[2,1024,768]{2,1,0:T(8,128)(2,1)} %x_ref.5, bf16[2,3,6,1024,128]{4,3,2,1,0:T(8,128)(2,1)} %bitcast.67, ...), custom_call_target="tpu_custom_call" | custom-call | flops 120000004096 | bytes 100000000 | tf_op jit(solution)/shard_map/attention_backward/pallas_call | solution.py:807
  378.6 0.7 add.47
  379.4 0.1 reshape.149
  379.6 0.1 reshape.150
  379.7 0.5 broadcast.51
  380.2 0.7 reduce.3
  381.0 0.1 copy.55
  381.1 0.1 fusion
  381.2 0.7 copy.65
  381.9 33.9 %scatter_sums.1 = (f32[24,2304]{1,0:T(8,128)}, f32[8,128]{1,0:T(8,128)}, f32[4,16,128]{2,1,0:T(8,128)}) custom-call(bf16[4,2,2,2,24,2304]{5,4,3,2,1,0:T(8,128)(2,1)} %bitcast.43, f32[4,2,2,2,8,128]{5,4,3,2,1,0:T(8,128)} %bitcast.48, f32[16,128]{1,0:T(8,128)} %bitcast.58), custom_call_target="tpu_custom_call" | custom-call | tf_op jit(solution)/shard_map/scatter_sums/pallas_call | solution.py:886
  415.8 0.8 slice.79
  416.6 0.1 copy.61
  416.8 0.1 select_reduce_fusion
  416.8 0.7 copy.60
  417.5 1.6 fusion.3
  419.1 1.2 slice.71
  422.6 2.1 constant_dynamic-slice_fusion
  424.7 1.9 pad_maximum_fusion
  426.7 0.1 reshape.155
  426.8 0.7 copy.57
  427.6 1.2 copy.59
  428.7 0.8 reshape.157
  429.5 0.6 slice.66
  430.2 3.8 copy.70
  434.0 0.7 copy.71
  (48 shorter events, 0.6 us)
Async XLA Ops:
  1.6 0.5 copy-start.7
  7.4 3.4 copy-start.18
  7.4 4.0 copy-start.9
  7.4 4.0 copy-start.10
  7.4 4.0 copy-start.11
  7.4 4.0 copy-start.12
  7.4 4.0 copy-start.13
  7.4 4.0 copy-start.14
  7.5 4.0 copy-start.15
  7.5 4.0 copy-start.16
  7.5 4.0 copy-start.17
  7.5 37.3 %copy-start.2 = (bf16[24,3072]{1,0:T(8,128)(2,1)S(1)}, bf16[24,3072]{1,0:T(8,128)(2,1)}, u32[]{:S(2)}) copy-start(bf16[24,3072]{1,0:T(8,128)(2,1)} %param.27) | copy-start | bytes 442372
  7.5 38.3 %copy-start.3 = (bf16[96,768]{1,0:T(8,128)(2,1)S(1)}, bf16[96,768]{1,0:T(8,128)(2,1)}, u32[]{:S(2)}) copy-start(bf16[96,768]{1,0:T(8,128)(2,1)} %param.29) | copy-start | bytes 442372
  7.5 38.4 %copy-start.4 = (bf16[24,768]{1,0:T(8,128)(2,1)S(1)}, bf16[24,768]{1,0:T(8,128)(2,1)}, u32[]{:S(2)}) copy-start(bf16[24,768]{1,0:T(8,128)(2,1)} %param.23) | copy-start | bytes 110596
  258.2 120.4 %copy-start.5 = (f32[8,768]{1,0:T(8,128)S(1)}, f32[8,768]{1,0:T(8,128)}, u32[]{:S(2)}) copy-start(f32[8,768]{1,0:T(8,128)} %get-tuple-element.52) | copy-start | bytes 73732
  258.2 122.0 %copy-start.6 = (f32[1,3072]{1,0:T(1,128)S(1)}, f32[1,3072]{1,0:T(1,128)}, u32[]{:S(2)}) copy-start(f32[1,3072]{1,0:T(1,128)} %get-tuple-element.54) | copy-start | bytes 36868
  378.6 38.1 %copy-start.8 = (s32[2]{0:T(128)S(1)}, s32[2]{0:T(128)}, u32[]{:S(2)}) copy-start(s32[2]{0:T(128)} %copy-done.7) | copy-start | bytes 28
  424.7 1.9 copy-start
  430.2 3.8 copy-start.1

commit v4 on v3

--- a/solution.py
+++ b/solution.py
@@ -15,6 +15,8 @@
 BLOCK = 256
 ROWS = 512
 PIECES = 8
+ALL = slice(None)
+EVERY = (ALL, ALL)
 
 f32 = jnp.float32
 bf16 = jnp.bfloat16
@@ -46,6 +48,14 @@
 
 def sems(*shape):
     return pltpu.SemaphoreType.DMA(shape)
+
+
+def tiles(shape, block):
+    return [
+        (pl.ds(top, block[0]), pl.ds(left, block[1]))
+        for top in range(0, shape[0], block[0])
+        for left in range(0, shape[1], block[1])
+    ]
 
 
 ANY = pl.BlockSpec(memory_space=pl.ANY)
@@ -120,6 +130,10 @@
         for copy in self.copies(piece):
             copy.start()
 
+    def fill(self, source, choice):
+        for slot in range(self.mine.shape[0]):
+            self.mine[slot] = source[choice[slot]]
+
     def wait(self):
         for piece in range(self.pieces):
             for copy in self.copies(piece):
@@ -149,12 +163,12 @@
             copy.wait()
 
     def view(self, number, spot):
-        array, cols, _ = self.parts[number]
-        return self.outs[array].at[tuple(spot) + (slice(None), cols)]
+        array, cut, _ = self.parts[number]
+        return self.outs[array].at[tuple(spot) + cut]
 
     def shard(self, number):
-        array, cols, _ = self.parts[number]
-        return self.shards[array].at[:, cols]
+        array, cut, _ = self.parts[number]
+        return self.shards[array].at[cut]
 
     def known(self, number, stage):
         order = self.parts[number][2]
@@ -236,9 +250,9 @@
         return 1 + sum(self.place.axes[dim][2] - 1 for dim in order[:stage])
 
     def block(self, number, core):
-        array, cols, _, _ = self.parts[number]
+        array, cut, _, _ = self.parts[number]
         lead = (slice(None),) * self.place.core + (core,)
-        return self.grads[array].at[lead + (slice(None), slice(None) if cols is None else cols)]
+        return self.grads[array].at[lead + (EVERY if cut is None else cut)]
 
     def across(self, number):
         place = self.place
@@ -302,7 +316,7 @@
             lax.fori_loop(0, total, one, 0)
 
     def advance(self, number, stage):
-        array, cols, order, _ = self.parts[number]
+        array, cut, order, _ = self.parts[number]
         place, refs = self.place, self.refs(number)
         if stage == 0:
             self.across(number).start()
@@ -330,10 +344,7 @@
             total = refs[0][tuple(place.own[:-1])].astype(f32)
             for extra in came:
                 total = total + extra[...].astype(f32)
-            if cols is None:
-                self.outs[array][...] = total
-            else:
-                self.outs[array][:, cols] = total
+            self.outs[array][EVERY if cut is None else cut] = total
 
     def within(self, number, stage, at):
         order = self.parts[number][2]
@@ -363,52 +374,88 @@
     return [sems(count, hops), sems(count, hops), sems(count)]
 
 
-def run_steps(mover, exchange, plan, time, steps):
-    for step in range(steps):
-        todo = [(part, stage) for part, row in enumerate(plan) for stage, at in enumerate(row) if at == step]
+def run_steps(mover, exchange, plan, dealt, time, steps, first=0):
+    for step in range(first, steps):
+        todo = [(part, stage) for part, row in plan.items() for stage, at in enumerate(row) if at == step]
+        pieces = [piece for piece, at in enumerate(dealt) if at == step]
 
         @pl.when(time == step)
-        def _(todo=todo, step=step):
+        def _(todo=todo, pieces=pieces):
             for part, stage in todo:
                 mover.advance(part, stage)
-            if 1 <= step <= PIECES:
-                exchange.start(step - 1)
+            for piece in pieces:
+                exchange.start(piece)
 
 
 def run_rest(mover, exchange, plan, steps):
-    for part, row in enumerate(plan):
+    for part, row in plan.items():
         for stage, at in enumerate(row):
             if at >= steps:
                 mover.advance(part, stage)
-    for part in range(len(plan)):
+    for part in plan:
         mover.finish(part)
     exchange.wait()
 
 
-def forward_kernel(axes, seqs, parts, plan, len_ref, x_ref, w_ref, bias_ref, *refs):
-    if axes is None:
-        qkv_ref, ctx_ref, probs_ref = refs
-    else:
-        rest_ref, cot_ref, qkv_ref, ctx_ref, probs_ref, weights_ref, cots_ref = refs[:7]
-        place = Place(axes)
-        gather = Gather(place, parts, [rest_ref], [weights_ref], *refs[7:12])
-        exchange = Exchange(place, cot_ref, cots_ref, PIECES, *refs[12:15])
+def forward_kernel(axes, seqs, parts, early, plan, dealt, len_ref, choice_ref, x_ref, *refs):
     seq, pair = pl.program_id(0), pl.program_id(1)
     time = seq * PAIRS + pair
     steps = seqs * PAIRS
     length = len_ref[seq]
     count, width = x_ref.shape[1], x_ref.shape[2]
     lane = lax.broadcasted_iota(jnp.int32, (1, PAIR), 1)
-
-    if axes is not None:
+    if axes is None:
+        w_ref, vec_ref, qkv_ref, ctx_ref, probs_ref = refs
+    else:
+        shards, cot_ref, qkv_ref, ctx_ref, probs_ref = refs[:5], refs[5], refs[6], refs[7], refs[8]
+        gathered, cots_ref, vec_ref = refs[9:14], refs[14], refs[15]
+        w_ref, raw_ref, small_ref, held_ref, going_ref, copy_sems = refs[16:22]
+        place = Place(axes)
+        gather = Gather(place, parts, shards, gathered, *refs[22:27])
+        exchange = Exchange(place, going_ref, cots_ref, PIECES, *refs[27:30])
 
         @pl.when(time == 0)
         def _():
-            meet(place, place.friends(cot_ref.shape[0]))
+            now = [
+                pltpu.make_async_copy(cot_ref, held_ref, copy_sems.at[0]),
+                pltpu.make_async_copy(gathered[0], raw_ref, copy_sems.at[1]),
+                pltpu.make_async_copy(gathered[1], small_ref, copy_sems.at[2]),
+            ]
+            now[0].start()
+            meet(place, place.friends(cots_ref.shape[0]))
             gather.start()
+            for part in list(early) + list(plan):
+                gather.advance(part, 0)
+            now[0].wait()
+            exchange.fill(held_ref, choice_ref)
             gather.local()
-
-        run_steps(gather, exchange, plan, time, steps)
+            for stage in range(1, place.core + 1):
+                for part in early:
+                    gather.advance(part, stage)
+                for part, row in plan.items():
+                    if stage == 1 and row[1] == 0:
+                        gather.advance(part, 1)
+                for piece, at in enumerate(dealt):
+                    if stage == 2 and at == 0:
+                        exchange.start(piece)
+            for part in early:
+                gather.finish(part)
+            for copy in now[1:]:
+                copy.start()
+            for copy in now[1:]:
+                copy.wait()
+            depth, across, along, _ = raw_ref.shape[:4]
+            height = 2 * raw_ref.shape[4]
+
+            def one(block, total):
+                spot = block // (across * along), lax.rem(block // along, across), lax.rem(block, along)
+                both = jnp.concatenate([raw_ref[spot + (half,)].astype(f32) for half in range(2)], axis=0)
+                w_ref[pl.ds(pl.multiple_of(block * height, height), height), :] = both.astype(bf16)
+                return total + small_ref[spot + (0,)].astype(f32) + small_ref[spot + (1,)].astype(f32)
+
+            vec_ref[...] = lax.fori_loop(0, depth * across * along, one, jnp.zeros((16, width), f32))
+
+        run_steps(gather, exchange, plan, dealt, time, steps, 1)
 
     @pl.when(pair == 0)
     def _():
@@ -419,7 +466,7 @@
             projected = nn(tokens, w_ref[:, start : start + step])
             if part != 1:
                 cols = slice(start - part * width, start - part * width + step)
-                projected = projected + bias_ref[part // 2 : part // 2 + 1, cols].astype(f32)
+                projected = projected + vec_ref[part // 2 : part // 2 + 1, cols]
             projected = projected.astype(bf16)
             if part == 0:
                 projected = projected * jnp.asarray(1.0 / math.sqrt(HEAD_DIM), bf16)
@@ -454,45 +501,66 @@
             run_rest(gather, exchange, plan, steps)
 
 
-def attention_forward(axes, lengths, tokens, w_qkv, biases, rest, outgoing):
+def attention_forward(axes, lengths, choice, tokens, operands, cotangent, shards):
     seqs, rows, width = tokens.shape
     out_shape = [
         jax.ShapeDtypeStruct((seqs, 3 * PAIRS, rows, PAIR), bf16),
         jax.ShapeDtypeStruct((seqs, rows, width), bf16),
         jax.ShapeDtypeStruct((seqs, PAIRS, 2, rows, rows), bf16),
     ]
-    in_specs = [pl.BlockSpec((1, rows, width), lambda s, p, *_: (s, 0, 0)), whole(w_qkv.shape), whole(biases.shape)]
+    in_specs = [pl.BlockSpec((1, rows, width), lambda s, p, *_: (s, 0, 0))]
     out_specs = [
         pl.BlockSpec((1, 3 * PAIRS, rows, PAIR), lambda s, p, *_: (s, 0, 0, 0)),
         pl.BlockSpec((1, rows, PAIR), lambda s, p, *_: (s, 0, p)),
         pl.BlockSpec((1, 1, 2, rows, rows), lambda s, p, *_: (s, p, 0, 0, 0)),
     ]
-    scratch, extra, parts, plan, talk = [], [], [], [], {}
-    if axes is not None:
-        parts = [(0, pl.ds(start, width), (2, 0, 1)) for start in range(0, rest.shape[1], width)]
-        plan = [[0] + [2 * stage - 1 + max(0, place - 2) for stage in range(1, 4)] for place in range(len(parts))]
-        extra = [rest, outgoing]
-        in_specs += [ANY, ANY]
+    scratch, parts, early, plan, dealt, talk = [], [], [], {}, [], {}
+    extra = list(operands)
+    if axes is None:
+        in_specs += [whole(array.shape) for array in operands]
+    else:
+        orders = ((0, 2, 1), (0, 2, 1), (1, 0, 2))
+        first, small, *later = operands
+        parts.append((1, EVERY, orders[0]))
+        for cut in tiles(first.shape, (first.shape[0], first.shape[1] // 6)):
+            parts.append((0, cut, orders[(len(parts) - 1) % 3]))
+        early = range(len(parts))
+        for array, shard in enumerate(later, 2):
+            parts += [(array, cut, (2, 0, 1)) for cut in tiles(shard.shape, (first.shape[0], width))]
+        for place in range(len(parts) - len(early)):
+            at = max(0, place - 2)
+            plan[place + len(early)] = [0, at, at + (1 if place < 2 else 2), at + (3 if place < 2 else 4)]
+        dealt = [max(0, piece - 1) for piece in range(PIECES)]
+        extra += [cotangent]
+        in_specs += [ANY] * len(extra)
         sizes = tuple(size for _, _, size in axes)
-        out_shape += [jax.ShapeDtypeStruct(sizes + rest.shape, bf16), jax.ShapeDtypeStruct(outgoing.shape, bf16)]
-        out_specs += [ANY, ANY]
-        friends = outgoing.shape[0] - 1
-        scratch = gather_sems(axes, parts, 1) + exchange_sems(friends)
+        out_shape += [jax.ShapeDtypeStruct(sizes + shard.shape, bf16) for shard in operands]
+        out_shape += [jax.ShapeDtypeStruct((shards, rows, width), bf16), jax.ShapeDtypeStruct(small.shape, f32)]
+        out_specs += [ANY] * (len(operands) + 1) + [whole(small.shape)]
+        scratch = [
+            pltpu.VMEM((width, first.shape[1]), bf16),
+            pltpu.VMEM(sizes + first.shape, bf16),
+            pltpu.VMEM(sizes + small.shape, bf16),
+            pltpu.VMEM(cotangent.shape, bf16),
+            pltpu.VMEM((shards, rows, width), bf16),
+            sems(3),
+        ]
+        scratch += gather_sems(axes, parts, len(operands)) + exchange_sems(shards - 1)
         talk = {"collective_id": 3, "has_side_effects": True}
     return pl.pallas_call(
-        functools.partial(forward_kernel, axes, seqs, parts, plan),
+        functools.partial(forward_kernel, axes, seqs, parts, early, plan, dealt),
         out_shape=tuple(out_shape),
         grid_spec=pltpu.PrefetchScalarGridSpec(
-            num_scalar_prefetch=1,
+            num_scalar_prefetch=2,
             grid=(seqs, PAIRS),
             in_specs=in_specs,
             out_specs=tuple(out_specs),
             scratch_shapes=scratch,
         ),
-        compiler_params=pltpu.CompilerParams(vmem_limit_bytes=58 << 20, **talk),
+        compiler_params=pltpu.CompilerParams(vmem_limit_bytes=60 << 20, **talk),
         cost_estimate=pl.CostEstimate(flops=60_000_000_000, transcendentals=30_000_000, bytes_accessed=80_000_000),
         name="attention_forward",
-    )(lengths, tokens, w_qkv, biases, *extra)
+    )(lengths, choice, tokens, *extra)
 
 
 def normal_tail(values):
@@ -512,25 +580,24 @@
 
 
 def middle_kernel(
-    len_ref, in_slot, out_slot, x_ref, ctx_ref, cot_ref, w_ref, vec_ref, bu_ref,
-    out_ref, gres_ref, gctx_ref, dw_ref, dvec_ref, dbu_ref, rms_ref,
-    acc, active, slope, sums, stage, sems,
+    len_ref, in_slot, out_slot, x_ref, ctx_ref, cot_ref, wo_ref, wu_ref, wd_ref, vec_ref,
+    out_ref, gres_ref, gctx_ref, dwo_ref, dwu_ref, dwd_ref, dvec_ref, rms_ref,
+    acc_o, acc_u, acc_d, active, slope, sums, stage, sems,
 ):
     seq, index = pl.program_id(0), pl.program_id(1)
     first = jnp.logical_and(seq == 0, index == 0)
     final = jnp.logical_and(seq == pl.num_programs(0) - 1, index == pl.num_programs(1) - 1)
     length = len_ref[seq]
     width = x_ref.shape[2]
-    chunks = bu_ref.shape[1] // width
+    chunks = wu_ref.shape[1] // width
     tile = lambda place: slice(place * width, (place + 1) * width)
-    up = lambda chunk: tile(1 + chunk)
-    down = lambda chunk: tile(1 + chunks + chunk)
 
     @pl.when(first)
     def _():
-        acc[...] = jnp.zeros_like(acc)
+        acc_o[...] = jnp.zeros_like(acc_o)
+        acc_u[...] = jnp.zeros_like(acc_u)
+        acc_d[...] = jnp.zeros_like(acc_d)
         dvec_ref[...] = jnp.zeros_like(dvec_ref)
-        dbu_ref[...] = jnp.zeros_like(dbu_ref)
 
     @pl.when(index == 0)
     def _():
@@ -544,12 +611,12 @@
 
     @pl.when(index * BLOCK < length)
     def _():
-        vec = lambda place: vec_ref[place : place + 1, :].astype(f32)
+        vec = lambda place: vec_ref[place : place + 1, :]
         bias_out, gain_a, shift_a, bias_down, gain_f, shift_f = (vec(place) for place in range(2, 8))
         valid = (lax.broadcasted_iota(jnp.int32, (BLOCK, 1), 0) + index * BLOCK < length).astype(f32)
         tokens = x_ref[0].astype(f32)
         context = ctx_ref[0]
-        branch_a = nn(context, w_ref[:, tile(0)]) + bias_out
+        branch_a = nn(context, wo_ref[...]) + bias_out
         mixed = tokens + branch_a
         center = mixed - row_mean(mixed)
         scale_a = lax.rsqrt(row_mean(center * center) + norm_eps)
@@ -559,12 +626,12 @@
         branch_f = bias_down
         for chunk in range(chunks):
             cols = tile(chunk)
-            gate = nn(hidden_low, w_ref[:, up(chunk)]) + bu_ref[:, cols].astype(f32)
+            gate = nn(hidden_low, wu_ref[:, cols]) + vec(8 + chunk)
             share, bell = normal_tail(gate)
             act = (gate * share).astype(bf16)
             active[:, cols] = act
             slope[:, cols] = share + gate * bell * (1.0 / math.sqrt(2.0 * math.pi))
-            branch_f = branch_f + nn(act, w_ref[:, down(chunk)])
+            branch_f = branch_f + nn(act, wd_ref[cols, :])
         mixed_f = hidden + branch_f
         center = mixed_f - row_mean(mixed_f)
         scale_f = lax.rsqrt(row_mean(center * center) + norm_eps)
@@ -577,18 +644,18 @@
         g_hidden = g_res2
         for chunk in range(chunks):
             cols = tile(chunk)
-            g_gate = nt(g_ffn, w_ref[:, down(chunk)]) * slope[:, cols]
+            g_gate = nt(g_ffn, wd_ref[cols, :]) * slope[:, cols]
             g_low = g_gate.astype(bf16)
-            acc[:, down(chunk)] += tn(active[:, cols], g_ffn)
-            acc[:, up(chunk)] += tn(hidden_low, g_low)
-            dbu_ref[:, cols] += jnp.sum(g_low.astype(f32), axis=0, keepdims=True)
-            g_hidden = g_hidden + nt(g_low, w_ref[:, up(chunk)])
+            acc_d[cols, :] += tn(active[:, cols], g_ffn)
+            acc_u[:, cols] += tn(hidden_low, g_low)
+            dvec_ref[8 + chunk : 9 + chunk, :] += jnp.sum(g_low.astype(f32), axis=0, keepdims=True)
+            g_hidden = g_hidden + nt(g_low, wu_ref[:, cols])
         g_hat = g_hidden * gain_a
         g_res1 = scale_a * (g_hat - row_mean(g_hat) - hat_a * row_mean(g_hat * hat_a))
         g_attn = g_res1.astype(bf16)
         gres_ref[0] = g_res1
-        gctx_ref[0] = nt(g_attn, w_ref[:, tile(0)]).astype(bf16)
-        acc[:, tile(0)] += tn(context, g_attn)
+        gctx_ref[0] = nt(g_attn, wo_ref[...]).astype(bf16)
+        acc_o[...] += tn(context, g_attn)
         column = lambda values: jnp.sum(values, axis=0, keepdims=True)
         dvec_ref[2:3, :] += column(g_attn.astype(f32))
         dvec_ref[3:4, :] += column(g_hidden * hat_a)
@@ -607,22 +674,25 @@
 
     @pl.when(final)
     def _():
+        pieces = [(acc_o, dwo_ref, EVERY)]
+        pieces += [(acc_u, dwu_ref, (ALL, tile(chunk))) for chunk in range(chunks)]
+        pieces += [(acc_d, dwd_ref, (tile(chunk), ALL)) for chunk in range(chunks)]
         copies = []
-        for place in range(1 + 2 * chunks):
+        for place, (acc, out, cut) in enumerate(pieces):
             slot = place % 2
             if place >= 2:
                 copies[place - 2].wait()
-            stage[slot] = acc[:, tile(place)].astype(bf16)
-            copies.append(pltpu.make_async_copy(stage.at[slot], dw_ref.at[:, tile(place)], sems.at[slot]))
+            stage[slot] = acc[cut].astype(bf16)
+            copies.append(pltpu.make_async_copy(stage.at[slot], out.at[cut], sems.at[slot]))
             copies[-1].start()
         copies[-2].wait()
         copies[-1].wait()
 
 
-def middle(lengths, in_slot, out_slot, tokens, context, cots, weights, vectors, bias_up):
+def middle(lengths, in_slot, out_slot, tokens, context, cots, w_out, w_up, w_down, vectors):
     seqs, rows, width = tokens.shape
     slots = cots.shape[0]
-    hidden = bias_up.shape[1]
+    hidden = w_up.shape[1]
     inside = lambda s, i, lens: jnp.minimum(i, block_count(lens[s]) - 1)
     here = pl.BlockSpec((1, BLOCK, width), lambda s, i, lens, a, b: (s, inside(s, i, lens), 0))
     there = pl.BlockSpec((1, BLOCK, width), lambda s, i, *_: (s, i, 0))
@@ -633,9 +703,10 @@
             jax.ShapeDtypeStruct((slots, rows, width), bf16),
             jax.ShapeDtypeStruct((seqs, rows, width), f32),
             jax.ShapeDtypeStruct((seqs, rows, width), bf16),
-            jax.ShapeDtypeStruct(weights.shape, bf16),
-            jax.ShapeDtypeStruct((8, width), f32),
-            jax.ShapeDtypeStruct((1, hidden), f32),
+            jax.ShapeDtypeStruct(w_out.shape, bf16),
+            jax.ShapeDtypeStruct(w_up.shape, bf16),
+            jax.ShapeDtypeStruct(w_down.shape, bf16),
+            jax.ShapeDtypeStruct((16, width), f32),
             jax.ShapeDtypeStruct((seqs, 8, 128), f32),
         ),
         grid_spec=pltpu.PrefetchScalarGridSpec(
@@ -645,21 +716,25 @@
                 here,
                 here,
                 pl.BlockSpec((1, BLOCK, width), lambda s, i, lens, a, b: (a[s], inside(s, i, lens), 0)),
-                whole(weights.shape),
+                whole(w_out.shape),
+                whole(w_up.shape),
+                whole(w_down.shape),
                 whole(vectors.shape),
-                whole(bias_up.shape),
             ],
             out_specs=[
                 pl.BlockSpec((1, BLOCK, width), lambda s, i, lens, a, b: (b[s], i, 0)),
                 there,
                 there,
-                pl.BlockSpec(memory_space=pl.ANY),
-                whole((8, width)),
-                whole((1, hidden)),
+                ANY,
+                ANY,
+                ANY,
+                whole((16, width)),
                 pl.BlockSpec((1, 8, 128), lambda s, i, *_: (s, 0, 0)),
             ],
             scratch_shapes=[
-                pltpu.VMEM(weights.shape, f32),
+                pltpu.VMEM(w_out.shape, f32),
+                pltpu.VMEM(w_up.shape, f32),
+                pltpu.VMEM(w_down.shape, f32),
                 pltpu.VMEM((BLOCK, hidden), bf16),
                 pltpu.VMEM((BLOCK, hidden), f32),
                 pltpu.VMEM((8, width), f32),
@@ -670,20 +745,21 @@
         compiler_params=pltpu.CompilerParams(vmem_limit_bytes=60 << 20),
         cost_estimate=pl.CostEstimate(flops=flops, transcendentals=seqs * rows * hidden, bytes_accessed=60_000_000),
         name="middle",
-    )(lengths, in_slot, out_slot, tokens, context, cots, weights, vectors, bias_up)
-
-
-def backward_kernel(axes, seqs, parts, plan, x_ref, qkv_in, ctx_ref, gctx_ref, probs_ref, gres_ref, w_ref, *refs):
+    )(lengths, in_slot, out_slot, tokens, context, cots, w_out, w_up, w_down, vectors)
+
+
+def backward_kernel(axes, seqs, parts, plan, dealt, x_ref, qkv_in, ctx_ref, gctx_ref, probs_ref, gres_ref, w_ref, *refs):
     if axes is None:
         gin_ref, dw_ref, dvec_ref = refs[:3]
         mixed, acc_w, stage, copy_sems = refs[3:]
     else:
-        grad_ref, result_ref, gin_ref, dw_ref, dvec_ref, sum_ref, arrived_ref = refs[:7]
-        mixed, acc_w, stage, copy_sems = refs[7:11]
+        grads, result_ref, gin_ref, dw_ref, dvec_ref = refs[:3], refs[3], refs[4], refs[5], refs[6]
+        summed, arrived_ref = refs[7:10], refs[10]
+        mixed, acc_w, stage, copy_sems = refs[11:15]
         place = Place(axes)
-        bufs = {parts[0][2]: refs[11:16]}
-        scatter = Scatter(place, parts, [grad_ref], [sum_ref], bufs, *refs[16:19])
-        exchange = Exchange(place, result_ref, arrived_ref, PIECES, *refs[19:22])
+        bufs = {parts[0][2]: refs[15:20]}
+        scatter = Scatter(place, parts, grads, summed, bufs, *refs[20:23])
+        exchange = Exchange(place, result_ref, arrived_ref, PIECES, *refs[23:26])
     seq, pair = pl.program_id(0), pl.program_id(1)
     time = seq * PAIRS + pair
     steps = seqs * PAIRS
@@ -696,7 +772,7 @@
         def _():
             meet(place, place.friends(result_ref.shape[0]))
 
-        run_steps(scatter, exchange, plan, time, steps)
+        run_steps(scatter, exchange, plan, dealt, time, steps)
 
     @pl.when(time == 0)
     def _():
@@ -761,7 +837,7 @@
             run_rest(scatter, exchange, plan, steps)
 
 
-def attention_backward(axes, tokens, qkv, context, g_context, probs, g_res1, w_qkv, dw_rest, results):
+def attention_backward(axes, tokens, qkv, context, g_context, probs, g_res1, w_qkv, grads, results):
     seqs, rows, width = tokens.shape
     pair_cols = pl.BlockSpec((1, rows, PAIR), lambda s, p: (s, 0, p))
     seq_rows = pl.BlockSpec((1, rows, width), lambda s, p: (s, 0, 0))
@@ -786,26 +862,29 @@
         pltpu.VMEM((2, width, width), bf16),
         sems(2),
     ]
-    extra, parts, plan, talk = [], [], [], {}
+    extra, parts, plan, dealt, talk = [], [], {}, [], {}
     if axes is not None:
         sizes = tuple(size for _, _, size in axes)
         order = (1, 0, 2)
-        grads = dw_rest.reshape(sizes + (-1, dw_rest.shape[1]))
-        block = grads.shape[4:]
-        parts = [(0, pl.ds(start, width), order, start // width) for start in range(0, block[1], width)]
-        plan = [
-            [max(0, place - 2)] + [2 * stage - 1 + max(0, place - 2) for stage in range(1, 5)] for place in range(len(parts))
-        ]
-        extra = [grads, results]
-        in_specs += [ANY, ANY]
-        out_shape += [jax.ShapeDtypeStruct(block, f32), jax.ShapeDtypeStruct(results.shape, bf16)]
-        out_specs += [whole(block), ANY]
+        grads = [grad.reshape(sizes + (-1, grad.shape[1])) for grad in grads]
+        block = (grads[0].shape[4], width)
+        for array, grad in enumerate(grads):
+            parts += [(array, cut, order, len(parts) + i) for i, cut in enumerate(tiles(grad.shape[4:], block))]
+        for place in range(len(parts)):
+            at = max(0, place - 2)
+            plan[place] = [at] + [2 * stage - 1 + at for stage in range(1, 5)]
+        dealt = [piece for piece in range(PIECES)]
+        extra = grads + [results]
+        in_specs += [ANY] * len(extra)
+        out_shape += [jax.ShapeDtypeStruct(grad.shape[4:], f32) for grad in grads]
+        out_shape += [jax.ShapeDtypeStruct(results.shape, bf16)]
+        out_specs += [whole(grad.shape[4:]) for grad in grads] + [ANY]
         friends = results.shape[0] - 1
-        scratch += scatter_buffers(axes, order, len(parts), len(parts), (block[0], width), bf16)
+        scratch += scatter_buffers(axes, order, len(parts), len(parts), block, bf16)
         scratch += scatter_sems(axes, len(parts)) + exchange_sems(friends)
         talk = {"collective_id": 4, "has_side_effects": True}
     return pl.pallas_call(
-        functools.partial(backward_kernel, axes, seqs, parts, plan),
+        functools.partial(backward_kernel, axes, seqs, parts, plan, dealt),
         out_shape=tuple(out_shape),
         grid_spec=pltpu.PrefetchScalarGridSpec(
             num_scalar_prefetch=0,
@@ -818,33 +897,6 @@
         cost_estimate=pl.CostEstimate(flops=120_000_000_000, transcendentals=1, bytes_accessed=100_000_000),
         name="attention_backward",
     )(tokens, qkv.reshape(seqs, 3, PAIRS, rows, PAIR), context, g_context, probs, g_res1, w_qkv, *extra)
-
-
-def gather_kernel(axes, parts, count, *refs):
-    place = Place(axes)
-    gather = Gather(place, parts, refs[:count], refs[count : 2 * count], *refs[2 * count :])
-    meet(place)
-    gather.start()
-    for stage in range(place.core + 1):
-        if stage == 1:
-            gather.local()
-        for part in range(len(parts)):
-            gather.advance(part, stage)
-    for part in range(len(parts)):
-        gather.finish(part)
-
-
-def gather_blocks(axes, parts, shards):
-    sizes = tuple(size for _, _, size in axes)
-    return pl.pallas_call(
-        functools.partial(gather_kernel, axes, parts, len(shards)),
-        out_shape=tuple(jax.ShapeDtypeStruct(sizes + shard.shape, shard.dtype) for shard in shards),
-        in_specs=[ANY] * len(shards),
-        out_specs=tuple([ANY] * len(shards)),
-        scratch_shapes=gather_sems(axes, parts, len(shards)),
-        compiler_params=pltpu.CompilerParams(collective_id=1, has_side_effects=True),
-        name="gather_blocks",
-    )(*shards)
 
 
 def scatter_kernel(axes, parts, orders, *refs):
@@ -879,7 +931,7 @@
     block = grad.shape[4:]
     orders = ((2, 1, 0), (1, 2, 0))
     cut = block[1] // 6
-    parts = [(0, pl.ds(place * cut, cut), orders[place % 2], place // 2) for place in range(6)]
+    parts = [(0, (ALL, pl.ds(place * cut, cut)), orders[place % 2], place // 2) for place in range(6)]
     parts.insert(0, (1, None, orders[0], 0))
     bufs = [buf for order in orders for buf in scatter_buffers(axes, order, 3, 3, (block[0], cut), bf16)]
     bufs += scatter_buffers(axes, orders[0], 1, 1, small.shape[4:], f32)
@@ -921,57 +973,47 @@
     source = jnp.sum(jnp.where(matches, jnp.arange(column, dtype=jnp.int32)[None, :], 0), axis=1)
     peers = jnp.arange(shards, dtype=jnp.int32)
 
-    up_mixed = up_weight.reshape(per, width, chunks).transpose(0, 2, 1).reshape(per, hidden)
-    rest = jnp.concatenate([out_weight, up_mixed, down_weight.reshape(per, hidden)], axis=1)
-    outgoing = cotangent[0][None]
-    for place in range(1, seqs):
-        outgoing = jnp.where((source[place] // seqs == peers)[:, None, None], cotangent[place][None], outgoing)
-    small = jnp.concatenate(
-        [query_bias, value_bias, out_bias, attn_gain, attn_shift, down_bias, ffn_gain, ffn_shift, up_bias]
+    choice = jnp.sum(jnp.where(source[:, None] // seqs == peers[None, :], jnp.arange(seqs, dtype=jnp.int32)[:, None], 0), axis=0)
+
+    rank = lax.axis_index("dp") * shards + member
+    vectors = [query_bias, value_bias, out_bias, attn_gain, attn_shift, down_bias, ffn_gain, ffn_shift]
+    small = lax.dynamic_update_slice(jnp.zeros((16, width), bf16), jnp.stack(vectors), (0, rank * per))
+    start = rank * (chunks * per)
+    small = lax.dynamic_update_slice(small, up_bias[None], (8 + start // width, lax.rem(start, width)))
+    if axes is None:
+        gather = lambda shard: lax.all_gather(shard, BOTH, axis=0, tiled=True)
+        vectors = jnp.sum(lax.all_gather(small, BOTH, axis=0, tiled=False).astype(f32), axis=0)
+        w_qkv, w_out, w_up, w_down = gather(qkv_weight), gather(out_weight), gather(up_weight), gather(down_weight)
+        outgoing = jnp.stack([lax.dynamic_index_in_dim(cotangent, choice[j], 0, keepdims=False) for j in range(shards)])
+        cots = lax.all_to_all(outgoing, "fsdp", split_axis=0, concat_axis=0, tiled=True)
+        qkv, context, probs = attention_forward(axes, own_lengths, choice, tokens, [w_qkv, vectors], None, shards)
+    else:
+        qkv, context, probs, w_qkv, _, w_out, w_up, w_down, cots, vectors = attention_forward(
+            axes, own_lengths, choice, tokens, [qkv_weight, small, out_weight, up_weight, down_weight], cotangent, shards
+        )
+        w_qkv, w_out, w_up, w_down = (array.reshape(-1, array.shape[-1]) for array in (w_qkv, w_out, w_up, w_down))
+    results, g_res1, g_context, dw_out, dw_up, dw_down, dvec, rms = middle(
+        own_lengths, target, target, tokens, context, cots, w_out, w_up, w_down, vectors
     )
-    small = jnp.pad(small, (0, 8 * 128 - small.shape[0])).reshape(8, 128)
-    if axes is None:
-        w_qkv = lax.all_gather(qkv_weight, BOTH, axis=0, tiled=True)
-        small = lax.all_gather(small, BOTH, axis=0, tiled=False)
-    else:
-        cut = qkv_weight.shape[1] // 6
-        orders = ((0, 2, 1), (0, 2, 1), (1, 0, 2))
-        parts = [(1, slice(None), orders[0])] + [(0, pl.ds(i * cut, cut), orders[i % 3]) for i in range(6)]
-        w_qkv, small = gather_blocks(axes, parts, [qkv_weight, small])
-        w_qkv = w_qkv.reshape(width, -1)
-    small = small.reshape(devices, -1)
-    vectors = small[:, : 8 * per].reshape(devices, 8, per).transpose(1, 0, 2).reshape(8, width)
-    bias_up = small[:, 8 * per : 8 * per + chunks * per].reshape(width, chunks).T.reshape(1, hidden)
-
-    if axes is None:
-        weights = lax.all_gather(rest, BOTH, axis=0, tiled=True)
-        cots = lax.all_to_all(outgoing, "fsdp", split_axis=0, concat_axis=0, tiled=True)
-        qkv, context, probs = attention_forward(axes, own_lengths, tokens, w_qkv, vectors, rest, outgoing)
-    else:
-        qkv, context, probs, weights, cots = attention_forward(
-            axes, own_lengths, tokens, w_qkv, vectors, rest, outgoing
-        )
-        weights = weights.reshape(width, -1)
-    results, g_res1, g_context, dw_rest, dvec, dbu, rms = middle(
-        own_lengths, target, target, tokens, context, cots, weights, vectors, bias_up
-    )
-    outs = attention_backward(axes, tokens, qkv, context, g_context, probs, g_res1, w_qkv, dw_rest, results)
+    grads = [dw_out, dw_up, dw_down]
+    outs = attention_backward(axes, tokens, qkv, context, g_context, probs, g_res1, w_qkv, grads, results)
     input_grad, dw_qkv, dqv = outs[:3]
     if axes is None:
         arrived = lax.all_to_all(results, "fsdp", split_axis=0, concat_axis=0, tiled=True)
     else:
-        rest_grad, arrived = outs[3:]
+        outw_grad, upw_grad, downw_grad, arrived = outs[3:]
     layer_out = jnp.stack(
         [lax.dynamic_index_in_dim(arrived, source[t] // seqs, 0, keepdims=False) for t in range(seqs)]
     )
 
-    dvec = (dvec + dqv).reshape(8, devices, per).transpose(1, 0, 2).reshape(devices, 8 * per)
-    dbu = dbu.reshape(chunks, devices, per).transpose(1, 2, 0).reshape(devices, chunks * per)
-    packed = jnp.pad(jnp.concatenate([dvec, dbu], axis=1), ((0, 0), (0, 8 * 128 - (8 + chunks) * per)))
+    packed = (dvec[:8] + dqv).reshape(8, devices, per).transpose(1, 0, 2).reshape(devices, 8 * per)
+    packed = jnp.concatenate([packed, dvec[8 : 8 + chunks].reshape(devices, chunks * per)], axis=1)
+    packed = jnp.pad(packed, ((0, 0), (0, 8 * 128 - packed.shape[1])))
     rms = rms.reshape(seqs * 8, 128)
     if axes is None:
-        scatter = lambda whole: lax.psum_scatter(whole, BOTH, scatter_dimension=0, tiled=True)
-        qkvw_grad, rest_grad = scatter(dw_qkv).astype(f32), scatter(dw_rest).astype(f32)
+        scatter = lambda array: lax.psum_scatter(array, BOTH, scatter_dimension=0, tiled=True)
+        qkvw_grad = scatter(dw_qkv).astype(f32)
+        outw_grad, upw_grad, downw_grad = (scatter(grad).astype(f32) for grad in grads)
         packed = scatter(packed)
         rms = lax.all_gather(rms, "fsdp", axis=0, tiled=False)
     else:
@@ -980,12 +1022,9 @@
     vector = [packed[place * per : (place + 1) * per] for place in range(8)]
     rms = rms.reshape(column, 8, 128)[:, :3, 0]
     branch_rms = jnp.sum(jnp.where((source[:, None] == jnp.arange(column))[:, :, None], rms[None], 0.0), axis=1)
-    outw_grad = rest_grad[:, :width]
-    upw_grad = rest_grad[:, width : width + hidden].reshape(per, chunks, width).transpose(0, 2, 1).reshape(per, hidden)
-    downw_grad = rest_grad[:, width + hidden :].reshape(per * chunks, width)
     return (
         layer_out, input_grad, qkvw_grad, vector[0], vector[1], outw_grad, vector[2], vector[3], vector[4], upw_grad,
-        packed[8 * per : 8 * per + chunks * per], downw_grad, vector[5], vector[6], vector[7], branch_rms,
+        packed[8 * per : (8 + chunks) * per], downw_grad, vector[5], vector[6], vector[7], branch_rms,
     )
 
 

time: 442 us -> 403 us (0.912); the launches traced: 435 us -> 402 us
  Pallas kernels: 395 us -> 374 us
  local copies, waits for them, and re-layouts: 24.4 us -> 16.8 us
    pallas_call x1, Pallas kernels: 120 us -> 103 us  [attention_backward(): pl.pallas_call(functools.partial(backward_kernel, axes, seqs, parts, plan...]
    pallas_call x2 -> x1, Pallas kernels: 135 us -> 132 us  [attention_forward(): pl.pallas_call(functools.partial(forward_kernel, axes, seqs, parts, early...]
    unnamed x48 -> x26, local copies, waits for them, and re-layouts: 9.59 us -> 6.98 us
where the time goes in v4:
time: 403 us; the launch traced here: 402 us
  Pallas kernels  374 us (93%)
  local copies, waits for them, and re-layouts  16.8 us (4%)
  between operations  6.06 us (2%)
  other arithmetic  5.03 us (1%)
    pallas_call x1, Pallas kernels, attention_forward(): pl.pallas_call(functools.partial(forward_kernel, axes, seqs, parts, early...  132 us
    pallas_call x1, Pallas kernels, middle(): pl.pallas_call(middle_kernel, out_shape=(jax.ShapeDtypeStruct((slots, row...  107 us
    pallas_call x1, Pallas kernels, attention_backward(): pl.pallas_call(functools.partial(backward_kernel, axes, seqs, parts, plan...  103 us
    pallas_call x1, Pallas kernels, scatter_sums(): pl.pallas_call(functools.partial(scatter_kernel, axes, parts, orders), ou...  31.9 us

profile of v4, /device:TPU:0, one launch (start us, length us, event | category | flops | bytes accessed | tf_op | source)
XLA Modules:
  0.0 402.2 jit_solution(4283529859283174778)
XLA Ops:
  0.7 0.8 stack.40
  1.5 0.3 dynamic_update_slice.6
  1.8 0.8 dynamic_update_slice.7.refs_1_
  2.6 0.0 copy-start.6
  2.6 0.7 dynamic-slice_subtract_fusion
  3.4 0.2 fusion.1
  3.6 0.6 and_select_fusion
  4.2 0.6 fusion.2.choice_ref
  4.8 1.2 dynamic_slice.16.len_ref
  6.0 0.0 copy-done.6
  6.0 131.8 %attention_forward.1 = (bf16[2,18,1024,128]{3,2,1,0:T(8,128)(2,1)}, bf16[2,1024,768]{2,1,0:T(8,128)(2,1)}, bf16[2,6,2,1024,1024]{4,3,2,1,0:T(8,128)(2,1)}, bf16[...) custom-call(s32[2]{0:T(128)} %dynamic_slice.16.len_ref, ...), custom_call_target="tpu_custom_call" | custom-call | flops 60000002048 | bytes 80000000 | tf_op jit(solution)/shard_map/attention_forward/pallas_call | solution.py:550
  137.8 0.0 copy-done.7
  137.8 107.3 %middle.1 = (bf16[4,1024,768]{2,1,0:T(8,128)(2,1)}, f32[2,1024,768]{2,1,0:T(8,128)}, bf16[2,1024,768]{2,1,0:T(8,128)(2,1)}, bf16[768,768]{1,0:T(8,128)(2,1)}, bf...) custom-call(s32[2]{0:T(128)} %dynamic_slice.16.len_ref, ...), custom_call_target="tpu_custom_call" | custom-call | flops 65229815808 | bytes 60000000 | tf_op jit(solution)/shard_map/middle/pallas_call | solution.py:700
  245.1 0.0 copy-start.5
  245.1 103.3 %attention_backward.1 = (bf16[2,1024,768]{2,1,0:T(8,128)(2,1)}, bf16[768,2304]{1,0:T(8,128)(2,1)}, f32[8,768]{1,0:T(8,128)}, f32[24,768]{1,0:T(8,128)}, f32[24,3...) custom-call(bf16[2,1024,768]{2,1,0:T(8,128)(2,1)} %x_ref.5, bf16[2,3,6,1024,128]{4,3,2,1,0:T(8,128)(2,1)} %bitcast.46, ...), custom_call_target="tpu_custom_call" | custom-call | flops 120000004096 | bytes 100000000 | tf_op jit(solution)/shard_map/attention_backward/pallas_call | solution.py:886
  348.4 0.0 copy-start.8
  348.4 0.0 copy-done.5
  348.4 0.7 slice_add_fusion
  349.2 0.1 reshape.148
  349.3 0.1 copy.39
  349.4 0.1 reshape.149
  349.5 0.1 reshape.150
  349.6 0.1 fusion
  349.6 0.7 copy.43
  350.3 31.9 %scatter_sums.1 = (f32[24,2304]{1,0:T(8,128)}, f32[8,128]{1,0:T(8,128)}, f32[4,16,128]{2,1,0:T(8,128)}) custom-call(bf16[4,2,2,2,24,2304]{5,4,3,2,1,0:T(8,128)(2,1)} %bitcast.29, f32[4,2,2,2,8,128]{5,4,3,2,1,0:T(8,128)} %bitcast.30, f32[16,128]{1,0:T(8,128)} %bitcast.32), custom_call_target="tpu_custom_call" | custom-call | tf_op jit(solution)/shard_map/scatter_sums/pallas_call | solution.py:938
  382.3 0.8 slice.56
  383.0 0.1 copy.42
  383.1 0.0 copy-done.8
  383.1 0.1 iota_compare_fusion.1
  383.2 0.1 select_reduce_fusion
  383.3 0.7 copy.41
  384.0 1.6 fusion.3
  385.5 1.3 slice.51
  386.8 0.6 fusion.4
  392.6 2.1 constant_dynamic-slice_fusion
  394.7 0.0 copy-start
  394.7 1.9 pad_maximum_fusion
  396.6 1.1 copy-done
  397.7 0.0 copy-start.3
  397.7 1.7 copy.51
  399.4 0.0 copy-done.3
  399.4 0.7 copy.52
  400.1 0.0 copy-done.4
  400.1 0.6 copy.53
  400.7 0.0 copy-done.2
  400.7 0.7 copy.54
  401.4 0.0 copy-done.1
  401.4 0.7 copy.55
  (7 shorter events, 0.0 us)
Async XLA Ops:
  2.6 3.4 copy-start.6
  3.6 134.2 %copy-start.7 = (s32[2]{0:T(128)}, s32[2]{0:T(128)S(1)}, u32[]{:S(2)}) copy-start(s32[2]{0:T(128)S(1)} %fusion.1) | copy-start | bytes 28
  245.1 103.3 %copy-start.5 = (f32[16,768]{1,0:T(8,128)S(1)}, f32[16,768]{1,0:T(8,128)}, u32[]{:S(2)}) copy-start(f32[16,768]{1,0:T(8,128)} %get-tuple-element.61) | copy-start | bytes 147460
  348.4 34.7 %copy-start.8 = (s32[2]{0:T(128)S(1)}, s32[2]{0:T(128)}, u32[]{:S(2)}) copy-start(s32[2]{0:T(128)} %copy-done.7) | copy-start | bytes 28
  394.7 3.0 copy-start
  397.7 1.7 copy-start.3
  397.7 2.4 copy-start.4
  397.7 3.0 copy-start.2
  397.7 3.7 copy-start.1

commit v5 on v4

--- a/solution.py
+++ b/solution.py
@@ -900,7 +900,12 @@
 
 
 def scatter_kernel(axes, parts, orders, *refs):
-    grad_ref, small_ref, note_ref, out_ref, out_small, notes_ref = refs[:6]
+    grad_ref, small_ref, note_ref, arrived_ref, pick_ref, out_ref, out_small, notes_ref, layer_ref = refs[:9]
+    came, kept, layer_sems = refs[-3:]
+    refs = refs[3:-3]
+    fetch = pltpu.make_async_copy(arrived_ref, came, layer_sems.at[0])
+    store = pltpu.make_async_copy(kept, layer_ref, layer_sems.at[1])
+    fetch.start()
     place = Place(axes)
     member = place.at["fsdp"]
     friends = place.friends(notes_ref.shape[0])
@@ -918,13 +923,19 @@
     for stage in range(place.core + 2):
         for part in range(len(parts)):
             scatter.advance(part, stage)
+        if stage == 1:
+            fetch.wait()
+            for slot in range(kept.shape[0]):
+                kept[slot] = came[pick_ref[slot]]
+            store.start()
+    store.wait()
     for copy in told:
         copy.wait()
     for part in range(len(parts)):
         scatter.finish(part)
 
 
-def scatter_sums(axes, grad, small, note, shards):
+def scatter_sums(axes, grad, small, note, shards, arrived, pick):
     sizes = tuple(size for _, _, size in axes)
     grad = grad.reshape(sizes + (-1, grad.shape[1]))
     small = small.reshape(sizes + (-1, small.shape[1]))
@@ -941,13 +952,17 @@
             jax.ShapeDtypeStruct(block, f32),
             jax.ShapeDtypeStruct(small.shape[4:], f32),
             jax.ShapeDtypeStruct((shards,) + note.shape, f32),
+            jax.ShapeDtypeStruct(pick.shape + arrived.shape[1:], bf16),
         ),
-        in_specs=[ANY, ANY, VMEM],
-        out_specs=(VMEM, VMEM, VMEM),
-        scratch_shapes=bufs + scatter_sems(axes, len(parts)) + [sems(shards - 1), sems(shards - 1)],
+        in_specs=[ANY, ANY, VMEM, ANY, pl.BlockSpec(memory_space=pltpu.SMEM)],
+        out_specs=(VMEM, VMEM, VMEM, ANY),
+        scratch_shapes=bufs
+        + scatter_sems(axes, len(parts))
+        + [sems(shards - 1), sems(shards - 1)]
+        + [pltpu.VMEM(arrived.shape, bf16), pltpu.VMEM(pick.shape + arrived.shape[1:], bf16), sems(2)],
         compiler_params=pltpu.CompilerParams(collective_id=2, has_side_effects=True, vmem_limit_bytes=56 << 20),
         name="scatter_sums",
-    )(grad, small, note)
+    )(grad, small, note, arrived, pick)
 
 
 def body(
@@ -1002,10 +1017,6 @@
         arrived = lax.all_to_all(results, "fsdp", split_axis=0, concat_axis=0, tiled=True)
     else:
         outw_grad, upw_grad, downw_grad, arrived = outs[3:]
-    layer_out = jnp.stack(
-        [lax.dynamic_index_in_dim(arrived, source[t] // seqs, 0, keepdims=False) for t in range(seqs)]
-    )
-
     packed = (dvec[:8] + dqv).reshape(8, devices, per).transpose(1, 0, 2).reshape(devices, 8 * per)
     packed = jnp.concatenate([packed, dvec[8 : 8 + chunks].reshape(devices, chunks * per)], axis=1)
     packed = jnp.pad(packed, ((0, 0), (0, 8 * 128 - packed.shape[1])))
@@ -1016,8 +1027,12 @@
         outw_grad, upw_grad, downw_grad = (scatter(grad).astype(f32) for grad in grads)
         packed = scatter(packed)
         rms = lax.all_gather(rms, "fsdp", axis=0, tiled=False)
+        picked = [lax.dynamic_index_in_dim(arrived, source[t] // seqs, 0, keepdims=False) for t in range(seqs)]
+        layer_out = jnp.stack(picked)
     else:
-        qkvw_grad, packed, rms = scatter_sums(axes, dw_qkv, packed.reshape(devices * 8, 128), rms, shards)
+        qkvw_grad, packed, rms, layer_out = scatter_sums(
+            axes, dw_qkv, packed.reshape(devices * 8, 128), rms, shards, arrived, source // seqs
+        )
     packed = packed.reshape(-1)
     vector = [packed[place * per : (place + 1) * per] for place in range(8)]
     rms = rms.reshape(column, 8, 128)[:, :3, 0]

time: 403 us -> 397 us (0.985)
  between operations: 6.06 us -> 0.84 us
    pallas_call x1, Pallas kernels: 103 us -> 157 us  [attention_backward(): pl.pallas_call(functools.partial(backward_kernel, axes, seqs, parts, plan...]
    pallas_call x1, Pallas kernels: 107 us -> 53.4 us  [middle(): pl.pallas_call(middle_kernel, out_shape=(jax.ShapeDtypeStruct((slots, row...]
    unnamed x26 -> x27, local copies, waits for them, and re-layouts: 6.98 us -> 10.3 us
where the time goes in v5:
time: 397 us
  Pallas kernels  376 us (95%)
  local copies, waits for them, and re-layouts  17.5 us (4%)
    pallas_call x1, Pallas kernels, attention_backward(): pl.pallas_call(functools.partial(backward_kernel, axes, seqs, parts, plan...  157 us
    pallas_call x1, Pallas kernels, attention_forward(): pl.pallas_call(functools.partial(forward_kernel, axes, seqs, parts, early...  132 us
    pallas_call x1, Pallas kernels, middle(): pl.pallas_call(middle_kernel, out_shape=(jax.ShapeDtypeStruct((slots, row...  53.4 us
    pallas_call x1, Pallas kernels, scatter_sums(): pl.pallas_call(functools.partial(scatter_kernel, axes, parts, orders), ou...  33 us
    unnamed x27, local copies, waits for them, and re-layouts  10.3 us

profile of v5, /device:TPU:0, one launch (start us, length us, event | category | flops | bytes accessed | tf_op | source)
XLA Modules:
  0.0 397.5 jit_solution(1738893022110382378)
XLA Ops:
  0.7 0.7 dynamic-slice_subtract_fusion
  1.4 0.2 fusion.1
  1.6 0.6 and_select_fusion.in_slot.out_slot
  2.2 1.2 dynamic_slice.9.len_ref
  3.5 0.0 copy-start.7
  3.5 0.6 iota_compare_fusion.1
  4.1 0.0 copy-done.7
  4.1 0.6 fusion.2.choice_ref
  4.6 0.8 stack.35
  5.4 0.3 dynamic_update_slice.6
  5.8 0.8 dynamic_update_slice.7.refs_1_
  6.6 0.0 copy-start.6
  6.6 0.6 copy-done.6
  7.2 131.8 %attention_forward.1 = (bf16[2,18,1024,128]{3,2,1,0:T(8,128)(2,1)}, bf16[2,1024,768]{2,1,0:T(8,128)(2,1)}, bf16[2,6,2,1024,1024]{4,3,2,1,0:T(8,128)(2,1)}, bf16[...) custom-call(s32[2]{0:T(128)} %dynamic_slice.9.len_ref, ...), custom_call_target="tpu_custom_call" | custom-call | flops 60000002048 | bytes 80000000 | tf_op jit(solution)/shard_map/attention_forward/pallas_call | solution.py:550
  139.0 53.4 %middle.1 = (bf16[4,1024,768]{2,1,0:T(8,128)(2,1)}, f32[2,1024,768]{2,1,0:T(8,128)}, bf16[2,1024,768]{2,1,0:T(8,128)(2,1)}, bf16[768,768]{1,0:T(8,128)(2,1)}, bf...) custom-call(s32[2]{0:T(128)} %dynamic_slice.9.len_ref, ...), custom_call_target="tpu_custom_call" | custom-call | flops 65229815808 | bytes 60000000 | tf_op jit(solution)/shard_map/middle/pallas_call | solution.py:700
  192.4 0.0 copy-start.5
  192.4 157.3 %attention_backward.1 = (bf16[2,1024,768]{2,1,0:T(8,128)(2,1)}, bf16[768,2304]{1,0:T(8,128)(2,1)}, f32[8,768]{1,0:T(8,128)}, f32[24,768]{1,0:T(8,128)}, f32[24,3...) custom-call(bf16[2,1024,768]{2,1,0:T(8,128)(2,1)} %x_ref.5, bf16[2,3,6,1024,128]{4,3,2,1,0:T(8,128)(2,1)} %bitcast.44, ...), custom_call_target="tpu_custom_call" | custom-call | flops 120000004096 | bytes 100000000 | tf_op jit(solution)/shard_map/attention_backward/pallas_call | solution.py:886
  349.7 0.0 copy-done.5
  349.8 0.7 slice_add_fusion
  350.5 0.1 reshape.150
  350.6 0.1 reshape.148
  350.7 0.1 copy.39
  350.8 0.1 reshape.149
  350.9 0.1 fusion
  351.0 0.7 copy.43
  351.7 0.0 copy-start.8
  351.7 33.0 %scatter_sums.1 = (f32[24,2304]{1,0:T(8,128)}, f32[8,128]{1,0:T(8,128)}, f32[4,16,128]{2,1,0:T(8,128)}, bf16[2,1024,768]{2,1,0:T(8,128)(2,1)}) custom-call(bf16[4,2,2,2,24,2304]{5,4,3,2,1,0:T(8,128)(2,1)} %bitcast.27, f32[4,2,2,2,8,128]{5,4,3,2,1,0:T(8,128)} %bitcast.28, f32[16,128]{1,0:T(8,128)} %bitcast.32, ...), custom_call_target="tpu_custom_call" | custom-call | tf_op jit(solution)/shard_map/scatter_sums/pallas_call | solution.py:949
  384.7 0.0 copy-start
  384.7 1.4 slice.43
  386.1 1.6 fusion.3
  387.7 0.8 slice.48
  388.4 0.1 copy.42
  388.5 0.0 copy-done.8
  388.6 0.1 select_reduce_fusion
  388.6 0.7 copy.41
  389.3 3.8 copy.52
  393.0 0.0 copy-done
  393.1 0.0 copy-start.3
  393.1 0.0 copy-start.1
  393.1 1.7 copy.53
  394.7 0.0 copy-done.3
  394.7 0.7 copy.54
  395.4 0.0 copy-done.4
  395.4 0.6 copy.55
  396.1 0.0 copy-done.2
  396.1 0.7 copy.56
  396.8 0.0 copy-done.1
  396.8 0.7 copy.57
  (6 shorter events, 0.0 us)
Async XLA Ops:
  3.5 0.6 copy-start.7
  6.6 0.6 copy-start.6
  192.4 157.4 %copy-start.5 = (f32[16,768]{1,0:T(8,128)S(1)}, f32[16,768]{1,0:T(8,128)}, u32[]{:S(2)}) copy-start(f32[16,768]{1,0:T(8,128)} %get-tuple-element.60) | copy-start | bytes 147460
  351.7 36.9 %copy-start.8 = (pred[2,8]{1,0:T(4,128)(4,1)S(1)}, pred[2,8]{1,0:T(4,128)(4,1)}, u32[]{:S(2)}) copy-start(pred[2,8]{1,0:T(4,128)(4,1)} %iota_compare_fusion.1) | copy-start | bytes 52
  384.7 8.4 %copy-start = (bf16[2,1024,768]{2,1,0:T(8,128)(2,1)S(1)}, bf16[2,1024,768]{2,1,0:T(8,128)(2,1)}, u32[]{:S(2)}) copy-start(bf16[2,1024,768]{2,1,0:T(8,128)(2,1)} %get-tuple-element.113) | copy-start | bytes 9437188
  393.1 1.7 copy-start.3
  393.1 2.4 copy-start.4
  393.1 3.0 copy-start.2
  393.1 3.7 copy-start.1

commit v6 on v5

--- a/solution.py
+++ b/solution.py
@@ -873,7 +873,7 @@
         for place in range(len(parts)):
             at = max(0, place - 2)
             plan[place] = [at] + [2 * stage - 1 + at for stage in range(1, 5)]
-        dealt = [piece for piece in range(PIECES)]
+        dealt = [piece + 2 for piece in range(PIECES)]
         extra = grads + [results]
         in_specs += [ANY] * len(extra)
         out_shape += [jax.ShapeDtypeStruct(grad.shape[4:], f32) for grad in grads]

time: 397 us -> 401 us (1.010)
    pallas_call x1, Pallas kernels: 53.4 us -> 97.6 us  [middle(): pl.pallas_call(middle_kernel, out_shape=(jax.ShapeDtypeStruct((slots, row...]
    pallas_call x1, Pallas kernels: 157 us -> 119 us  [attention_backward(): pl.pallas_call(functools.partial(backward_kernel, axes, seqs, parts, plan...]
where the time goes in v6:
time: 401 us
  Pallas kernels  379 us (95%)
  local copies, waits for them, and re-layouts  17.5 us (4%)
    pallas_call x1, Pallas kernels, attention_forward(): pl.pallas_call(functools.partial(forward_kernel, axes, seqs, parts, early...  132 us
    pallas_call x1, Pallas kernels, attention_backward(): pl.pallas_call(functools.partial(backward_kernel, axes, seqs, parts, plan...  119 us
    pallas_call x1, Pallas kernels, middle(): pl.pallas_call(middle_kernel, out_shape=(jax.ShapeDtypeStruct((slots, row...  97.6 us
    pallas_call x1, Pallas kernels, scatter_sums(): pl.pallas_call(functools.partial(scatter_kernel, axes, parts, orders), ou...  30.2 us
    unnamed x27, local copies, waits for them, and re-layouts  10.2 us

profile of v6, /device:TPU:0, one launch (start us, length us, event | category | flops | bytes accessed | tf_op | source)
XLA Modules:
  0.0 401.1 jit_solution(1078590484856707627)
XLA Ops:
  0.7 0.7 dynamic-slice_subtract_fusion
  1.4 0.2 fusion.1
  1.6 0.6 and_select_fusion.in_slot.out_slot
  2.2 1.2 dynamic_slice.9.len_ref
  3.5 0.0 copy-start.7
  3.5 0.6 iota_compare_fusion.1
  4.1 0.0 copy-done.7
  4.1 0.6 fusion.2.choice_ref
  4.6 0.8 stack.35
  5.4 0.3 dynamic_update_slice.6
  5.8 0.8 dynamic_update_slice.7.refs_1_
  6.6 0.0 copy-start.6
  6.6 0.6 copy-done.6
  7.2 131.8 %attention_forward.1 = (bf16[2,18,1024,128]{3,2,1,0:T(8,128)(2,1)}, bf16[2,1024,768]{2,1,0:T(8,128)(2,1)}, bf16[2,6,2,1024,1024]{4,3,2,1,0:T(8,128)(2,1)}, bf16[...) custom-call(s32[2]{0:T(128)} %dynamic_slice.9.len_ref, ...), custom_call_target="tpu_custom_call" | custom-call | flops 60000002048 | bytes 80000000 | tf_op jit(solution)/shard_map/attention_forward/pallas_call | solution.py:550
  139.0 97.6 %middle.1 = (bf16[4,1024,768]{2,1,0:T(8,128)(2,1)}, f32[2,1024,768]{2,1,0:T(8,128)}, bf16[2,1024,768]{2,1,0:T(8,128)(2,1)}, bf16[768,768]{1,0:T(8,128)(2,1)}, bf...) custom-call(s32[2]{0:T(128)} %dynamic_slice.9.len_ref, ...), custom_call_target="tpu_custom_call" | custom-call | flops 65229815808 | bytes 60000000 | tf_op jit(solution)/shard_map/middle/pallas_call | solution.py:700
  236.6 0.0 copy-start.5
  236.6 119.5 %attention_backward.1 = (bf16[2,1024,768]{2,1,0:T(8,128)(2,1)}, bf16[768,2304]{1,0:T(8,128)(2,1)}, f32[8,768]{1,0:T(8,128)}, f32[24,768]{1,0:T(8,128)}, f32[24,3...) custom-call(bf16[2,1024,768]{2,1,0:T(8,128)(2,1)} %x_ref.5, bf16[2,3,6,1024,128]{4,3,2,1,0:T(8,128)(2,1)} %bitcast.44, ...), custom_call_target="tpu_custom_call" | custom-call | flops 120000004096 | bytes 100000000 | tf_op jit(solution)/shard_map/attention_backward/pallas_call | solution.py:886
  356.1 0.0 copy-done.5
  356.1 0.7 slice_add_fusion
  356.9 0.1 reshape.150
  356.9 0.1 reshape.148
  357.0 0.1 copy.39
  357.1 0.1 reshape.149
  357.2 0.1 fusion
  357.3 0.7 copy.43
  358.0 0.0 copy-start.8
  358.0 30.2 %scatter_sums.1 = (f32[24,2304]{1,0:T(8,128)}, f32[8,128]{1,0:T(8,128)}, f32[4,16,128]{2,1,0:T(8,128)}, bf16[2,1024,768]{2,1,0:T(8,128)(2,1)}) custom-call(bf16[4,2,2,2,24,2304]{5,4,3,2,1,0:T(8,128)(2,1)} %bitcast.27, f32[4,2,2,2,8,128]{5,4,3,2,1,0:T(8,128)} %bitcast.28, f32[16,128]{1,0:T(8,128)} %bitcast.32, ...), custom_call_target="tpu_custom_call" | custom-call | tf_op jit(solution)/shard_map/scatter_sums/pallas_call | solution.py:949
  388.3 0.0 copy-start
  388.3 1.4 slice.43
  389.7 1.6 fusion.3
  391.2 0.8 slice.48
  392.0 0.1 copy.42
  392.1 0.0 copy-done.8
  392.1 0.1 select_reduce_fusion
  392.2 0.7 copy.41
  392.9 3.8 copy.52
  396.6 0.0 copy-done
  396.6 0.0 copy-start.3
  396.6 0.0 copy-start.1
  396.6 1.7 copy.53
  398.3 0.0 copy-done.3
  398.3 0.7 copy.54
  399.0 0.0 copy-done.4
  399.0 0.6 copy.55
  399.6 0.0 copy-done.2
  399.6 0.7 copy.56
  400.3 0.0 copy-done.1
  400.3 0.7 copy.57
  (6 shorter events, 0.0 us)
Async XLA Ops:
  3.5 0.6 copy-start.7
  6.6 0.6 copy-start.6
  236.6 119.5 %copy-start.5 = (f32[16,768]{1,0:T(8,128)S(1)}, f32[16,768]{1,0:T(8,128)}, u32[]{:S(2)}) copy-start(f32[16,768]{1,0:T(8,128)} %get-tuple-element.60) | copy-start | bytes 147460
  358.0 34.1 %copy-start.8 = (pred[2,8]{1,0:T(4,128)(4,1)S(1)}, pred[2,8]{1,0:T(4,128)(4,1)}, u32[]{:S(2)}) copy-start(pred[2,8]{1,0:T(4,128)(4,1)} %iota_compare_fusion.1) | copy-start | bytes 52
  388.3 8.4 %copy-start = (bf16[2,1024,768]{2,1,0:T(8,128)(2,1)S(1)}, bf16[2,1024,768]{2,1,0:T(8,128)(2,1)}, u32[]{:S(2)}) copy-start(bf16[2,1024,768]{2,1,0:T(8,128)(2,1)} %get-tuple-element.113) | copy-start | bytes 9437188
  396.6 1.7 copy-start.3
  396.6 2.4 copy-start.4
  396.6 3.0 copy-start.2
  396.6 3.7 copy-start.1
